TPU v7x, 256 devices: a whole 4x4x8 slice. The times are simulated.
256 devices in a mesh: ep: 64 (over z, x, core), tp: 4 (over y).
Axes of the slice: x: 4, y: 4, z: 8, core: 2. Of those that a mesh axis runs over, the one named last changes fastest.
Arguments:
- tokens: bfloat16 [2, 1024, 4096], P(None, 'ep'), may hold values from -6 to 6
- route_ids: int32 [2, 1024, 8], P(None, 'ep'), may hold values from 0 to 15, all different within a row; in each aligned block of 16 rows (0 to 15, 16 to 31, ..., all dimensions but the last counted through in order) at most 10 rows name the same one
- route_weights: float32 [2, 1024, 8], P(None, 'ep'), may hold values from 0.1 to 0.4
- train_map: int32 [64], replicated, may hold values from 0 to 63, each once
- serve_place: int32 [64], replicated, may hold values from 0 to 15, as said below
- train_gate: bfloat16 [64, 1024, 1536], P('ep', None, 'tp'), may hold values from -0.09375 to 0.09375
- train_up: bfloat16 [64, 1024, 1536], P('ep', None, 'tp'), may hold values from -0.09375 to 0.09375
- train_down: bfloat16 [64, 1024, 1536], P('ep', None, 'tp'), may hold values from -0.15625 to 0.15625
Outputs:
- serve_gate: bfloat16 [64, 4096, 1536], P('ep', None, 'tp')
- serve_up: bfloat16 [64, 4096, 1536], P('ep', None, 'tp')
- serve_down: bfloat16 [64, 4096, 1536], P('ep', None, 'tp')
- moe_out: bfloat16 [2, 1024, 4096], P(None, 'ep', 'tp')
Inputs may be any that keep to these rules, and one draw needn't show every extreme that they name: `route_ids`: each row names 8 different experts; in each aligned block of 16 rows (one index of ep in one step) no expert is named by more than 10 rows. `train_map`: each trainer slot holds a different piece; piece q is part q % 4 of expert q // 4. `serve_place`: every expert occupies two or more serving slots, and some expert exactly two.
All inputs are finite; a program needn't handle non-finite values.
Results may differ from a plain program's by a relative error of at most 0.012.
Values may be sent and summed in bfloat16 or wider, within the bound.
No kernel may reach another device: no remote copies, remote signals or barrier semaphores. Data moves between devices by JAX's collectives and lax.ppermute only.
A program may use at most 128 MiB of HBM per device.

v0:
```python
import jax
import jax.numpy as jnp
from jax import lax
from jax.experimental import pallas as pl
from jax.experimental.pallas import tpu as pltpu
from jax.sharding import Mesh, PartitionSpec as P

EXPERTS = 16
MOST = 10
Z, X, C, Y = 8, 4, 2, 4
PLANE = X * C
EP = ("z", "x", "c")
XC = ("x", "c")


def exchange(value, axes):
    return lax.all_to_all(value, axes, split_axis=0, concat_axis=0, tiled=True)


def shift(value, step):
    return lax.ppermute(value, "z", [(i, (i + step) % Z) for i in range(Z)])


class Ring:
    def __init__(self, block):
        self.ahead = [block]
        self.behind = [block]
        self.far = []

    def hop(self):
        if len(self.ahead) < Z // 2:
            self.behind.append(shift(self.behind[-1], 1))
            self.ahead.append(shift(self.ahead[-1], -1))
        else:
            half = self.ahead[0].shape[0] // 2
            self.far = [shift(self.behind[-1][:half], 1), shift(self.ahead[-1][half:], -1)]
        return self

    def hold(self, value):
        last = self.far or [self.behind[-1], self.ahead[-1]]
        value, held = lax.optimization_barrier((value, last))
        if self.far:
            self.far = held
        else:
            self.behind[-1], self.ahead[-1] = held
        return value

    def pick(self, index):
        blocks = self.ahead + self.far + self.behind[:0:-1]
        return pick_pieces(index.reshape(-1), blocks)


def pick_kernel(index_ref, *refs):
    blocks, out_ref, held_ref, read_sems, write_sems = refs[:-4], *refs[-4:]
    count = out_ref.shape[0]
    half = blocks[Z // 2].shape[0]

    def read(i, carry):
        distance = index_ref[i] >> 4
        place = index_ref[i] & 15

        def copy(block, piece):
            pltpu.make_async_copy(block.at[piece], held_ref.at[i], read_sems.at[i]).start()

        for k in range(Z):
            if k == Z // 2:
                pl.when((distance == k) & (place < half))(lambda: copy(blocks[Z // 2], place))
                pl.when((distance == k) & (place >= half))(
                    lambda: copy(blocks[Z // 2 + 1], place - half)
                )
            else:
                block = blocks[k if k < Z // 2 else k + 1]
                pl.when(distance == k)(lambda block=block: copy(block, place))
        return carry

    def write(i, carry):
        pltpu.make_async_copy(blocks[0].at[0], held_ref.at[i], read_sems.at[i]).wait()
        pltpu.make_async_copy(held_ref.at[i], out_ref.at[i], write_sems.at[i]).start()
        return carry

    def finish(i, carry):
        pltpu.make_async_copy(held_ref.at[i], out_ref.at[i], write_sems.at[i]).wait()
        return carry

    lax.fori_loop(0, count, read, 0)
    lax.fori_loop(0, count, write, 0)
    lax.fori_loop(0, count, finish, 0)


def pick_pieces(index, blocks):
    count = index.shape[0]
    shape = (count,) + blocks[0].shape[1:]
    return pl.pallas_call(
        pick_kernel,
        out_shape=jax.ShapeDtypeStruct(shape, blocks[0].dtype),
        in_specs=[pl.BlockSpec(memory_space=pltpu.SMEM)]
        + [pl.BlockSpec(memory_space=pl.ANY)] * len(blocks),
        out_specs=pl.BlockSpec(memory_space=pl.ANY),
        scratch_shapes=[
            pltpu.VMEM(shape, blocks[0].dtype),
            pltpu.SemaphoreType.DMA((count,)),
            pltpu.SemaphoreType.DMA((count,)),
        ],
        name="pick_pieces",
    )(index, *blocks)


def take_rows(value, index):
    return value.at[index].get(mode="promise_in_bounds")


def body(
    tokens, route_ids, route_weights, train_map, serve_place, train_gate, train_up, train_down
):
    plane = lax.axis_index("z")
    line = lax.axis_index(XC)
    quarter = lax.axis_index("y")
    slot_count = serve_place.shape[0]
    part_count = slot_count // EXPERTS
    piece_rows = train_gate.shape[1]
    width = train_gate.shape[2]
    block_rows = piece_rows // PLANE
    steps, tok_count, model_width = tokens.shape
    out_width = model_width // Y
    own_tokens = steps * tok_count
    line_tokens = own_tokens * Z
    capacity = Z * steps * MOST // 2

    slot_iota = jnp.arange(slot_count, dtype=jnp.int32)
    inverse = jnp.sum(
        jnp.where(train_map[:, None] == slot_iota[None, :], slot_iota[:, None], 0), axis=0
    )
    relative = (inverse - plane * PLANE + slot_count) % slot_count
    place_rank = jnp.sum(
        (serve_place[:, None] == serve_place[None, :])
        & (slot_iota[None, :] < slot_iota[:, None]),
        axis=1,
    )
    near_experts = lax.dynamic_slice(serve_place, (plane * PLANE,), (PLANE,))
    near_rank = lax.dynamic_slice(place_rank, (plane * PLANE,), (PLANE,))
    near_count = jnp.sum(near_experts[:, None] == serve_place[None, :], axis=1)
    wanted = near_experts[:, None] * part_count + jnp.arange(part_count, dtype=jnp.int32)[None, :]
    chosen = take_rows(relative // PLANE * 16 + relative % PLANE, wanted)
    chosen_slot = take_rows(inverse, wanted)

    def spread(piece):
        return exchange(piece.reshape(PLANE, block_rows, width), XC)

    def gather_planes(block):
        rows = lax.all_gather(block.reshape(-1, width), "z", axis=0, tiled=True)
        return rows.reshape(slot_count, block_rows, width)

    def assemble(arrived):
        return jnp.swapaxes(arrived, 0, 1).reshape(1, part_count * piece_rows, width)

    experts = jnp.arange(EXPERTS, dtype=jnp.int32)
    hot = route_ids.reshape(own_tokens, -1)[:, :, None] == experts
    named = jnp.any(hot, axis=1).astype(jnp.bfloat16)
    weight = jnp.sum(
        jnp.where(hot, route_weights.reshape(own_tokens, -1)[:, :, None], 0.0), axis=1
    )
    high = weight.astype(jnp.bfloat16)
    rest = weight - high.astype(jnp.float32)
    middle = rest.astype(jnp.bfloat16)
    low = (rest - middle.astype(jnp.float32)).astype(jnp.bfloat16)
    own_rows = lax.dynamic_slice(
        tokens.reshape(own_tokens, model_width),
        (0, quarter * out_width),
        (own_tokens, out_width),
    )
    own_block = jnp.concatenate([own_rows, named, high, middle, low], axis=1)
    block_gate = spread(train_gate)
    block_gate, train_up, own_block = lax.optimization_barrier((block_gate, train_up, own_block))
    gate_all = gather_planes(block_gate)
    block_up = spread(train_up)
    block_up, train_down = lax.optimization_barrier((block_up, train_down))
    up_all = gather_planes(block_up)
    line_block = exchange(jnp.broadcast_to(own_block, (Z,) + own_block.shape), "z")
    line_block, train_down = lax.optimization_barrier((line_block, train_down))
    block_down = spread(train_down)
    line_block = line_block.reshape(line_tokens, -1)
    line_rows = line_block[:, :out_width]
    line_routes = line_block[:, out_width : out_width + 4 * EXPERTS]
    token_iota = jnp.arange(line_tokens, dtype=jnp.int32)
    earlier = (token_iota[None, :] < token_iota[:, None]).astype(jnp.bfloat16)
    near_hot = near_experts[:, None] == experts[None, :]

    def place(routes, line_index):
        names = routes[..., :EXPERTS]
        seen = jnp.einsum("ut,lte->lue", earlier, names, preferred_element_type=jnp.float32)

        def of_near(table):
            return jnp.sum(
                jnp.where(near_hot[None, :, None, :], table.astype(jnp.float32)[:, None], 0.0), axis=3
            )

        near_seen = of_near(seen).astype(jnp.int32)
        turn = (near_seen + line_index[:, None, None]) % near_count[None, :, None]
        position = near_seen // near_count[None, :, None]
        sent = (of_near(names) > 0.5) & (turn == near_rank[None, :, None])
        rows = jnp.arange(capacity, dtype=jnp.int32)[None, None, :, None]
        return sent[:, :, None, :] & (position[:, :, None, :] == rows)

    own_placing = place(line_routes[None], line[None])[0].astype(jnp.bfloat16)
    send_rows = jnp.einsum(
        "spt,td->spd", own_placing, line_rows, preferred_element_type=jnp.float32
    ).astype(jnp.bfloat16)
    route_rows = line_routes.reshape(-1, out_width)
    send_rows = jnp.concatenate(
        [send_rows, jnp.broadcast_to(route_rows, (PLANE,) + route_rows.shape)], axis=1
    )
    received = exchange(send_rows, XC)
    quarters = received[:, :capacity].reshape(PLANE * capacity, out_width)
    half = quarters.shape[0] // 2
    to_next = [(i, (i + 1) % Y) for i in range(Y)]
    to_last = [(i, (i - 1) % Y) for i in range(Y)]
    from_last = lax.ppermute(quarters, "y", to_next)
    from_next = lax.ppermute(quarters, "y", to_last)
    gate_all, from_last, from_next = lax.optimization_barrier((gate_all, from_last, from_next))
    far = [
        lax.ppermute(from_last[:half], "y", to_next),
        lax.ppermute(from_next[half:], "y", to_last),
    ]
    up_all, far, block_down = lax.optimization_barrier((up_all, far, block_down))
    inputs = take_rows(
        jnp.stack([quarters, from_next, jnp.concatenate(far, axis=0), from_last]),
        (jnp.arange(Y, dtype=jnp.int32) - quarter + Y) % Y,
    )
    routes = received[:, capacity:].reshape(PLANE, line_tokens, -1)
    placing = place(routes, jnp.arange(PLANE, dtype=jnp.int32))
    weights = sum(
        routes[..., k * EXPERTS : (k + 1) * EXPERTS].astype(jnp.float32) for k in (1, 2, 3)
    )
    own_expert = lax.dynamic_slice(near_experts, (line,), (1,))
    own_weight = jnp.sum(jnp.where(experts == own_expert, weights, 0.0), axis=2)
    own_sent = lax.dynamic_slice(
        placing, (0, line, 0, 0), (PLANE, 1, capacity, line_tokens)
    )[:, 0]
    row_weight = jnp.sum(jnp.where(own_sent, own_weight[:, None, :], 0.0), axis=2)
    placing = placing.astype(jnp.bfloat16)

    serve_gate = assemble(exchange(take_rows(gate_all, chosen_slot), XC))
    arrived_up = exchange(take_rows(up_all, chosen_slot), XC)
    down_ring = Ring(block_down).hop().hop()
    arrived_up = down_ring.hold(arrived_up)
    down_ring.hop()
    serve_up = assemble(arrived_up)
    by_part = (part_count, piece_rows, width)
    gate_act = jnp.einsum(
        "ymd,ydf->mf", inputs, serve_gate.reshape(by_part), preferred_element_type=jnp.float32
    )
    up_act = jnp.einsum(
        "ymd,ydf->mf", inputs, serve_up.reshape(by_part), preferred_element_type=jnp.float32
    )
    hidden = (jax.nn.silu(gate_act) * up_act * row_weight.reshape(-1, 1)).astype(jnp.bfloat16)

    hidden = down_ring.hold(hidden)
    down_ring.hop()

    plane_hidden = lax.all_gather(hidden, XC, axis=0, tiled=False).reshape(
        PLANE, PLANE, capacity, width
    )
    down_rows = down_ring.pick(chosen).reshape(PLANE, part_count, block_rows, width)
    serve_down = assemble(exchange(down_rows, XC))
    partial_value = jnp.einsum(
        "slpf,syrf->slpyr", plane_hidden, down_rows, preferred_element_type=jnp.float32
    ).astype(jnp.bfloat16)
    plane_out = jnp.einsum(
        "lspt,slpyr->yltr", placing, partial_value, preferred_element_type=jnp.float32
    ).astype(jnp.bfloat16)
    line_out = lax.psum_scatter(
        plane_out.reshape(-1, block_rows), "y", scatter_dimension=0, tiled=True
    )
    home = exchange(
        jnp.swapaxes(line_out.reshape(PLANE, Z, own_tokens, block_rows), 0, 1).reshape(
            Z * PLANE, own_tokens, block_rows
        ),
        EP,
    )
    total = jnp.sum(
        home.reshape(Z, PLANE, own_tokens, block_rows).astype(jnp.float32), axis=0
    ).astype(jnp.bfloat16)
    moe_out = jnp.swapaxes(total, 0, 1).reshape(steps, tok_count, out_width)
    return (serve_gate, serve_up, serve_down, moe_out)


def solution(mesh):
    fine = Mesh(mesh.devices.reshape(Z, X, C, Y), ("z", "x", "c", "y"))
    in_specs = (
        P(None, EP, None),
        P(None, EP, None),
        P(None, EP, None),
        P(),
        P(),
        P(EP, None, "y"),
        P(EP, None, "y"),
        P(EP, None, "y"),
    )
    out_specs = (P(EP, None, "y"), P(EP, None, "y"), P(EP, None, "y"), P(None, EP, "y"))
    return jax.shard_map(body, mesh=fine, in_specs=in_specs, out_specs=out_specs, check_vma=False)
```

profile of v0, /device:TPU:1, one launch (start us, length us, event | category | flops | bytes accessed | tf_op | source)
XLA Modules:
  0.0 385.6 jit_solution(12689534197168429504)
XLA Ops:
  7.2 6.8 %all-to-all-start = ((bf16[8,128,384]{2,1,0:T(8,128)(2,1)}), bf16[8,128,384]{2,1,0:T(8,128)(2,1)S(1)}, u32[]{:S(2)}, u32[]{:S(2)}) async-start(bf16[8,128,384]{2,1,0:T(8,128)(2,1)} %bitcast.132), calls=%async_computation | async-start | bytes 1572864 | tf_op jit(solution)/shard_map/all_to_all | solution.py:17
  14.0 0.7 copy.81
  14.9 0.7 copy.82
  16.1 10.2 %all-to-all-done = bf16[8,128,384]{2,1,0:T(8,128)(2,1)S(1)} async-done(((bf16[8,128,384]{2,1,0:T(8,128)(2,1)}), bf16[8,128,384]{2,1,0:T(8,128)(2,1)S(1)}, u32[]{:S(2)}, u32[]{:S(2)}) %all-to-all-start) | async-done | bytes 786464 | tf_op jit(solution)/shard_map/all_to_all | solution.py:17
  26.3 0.9 copy-done.11
  27.3 16.2 %all_to_all.45 = bf16[8,128,384]{2,1,0:T(8,128)(2,1)} all-to-all(bf16[8,128,384]{2,1,0:T(8,128)(2,1)S(1)} %bitcast.133), channel_id=1, replica_groups=mesh['z'=8,'x'=4,'c'=2,'y'=4] {'x','c'}, dimensions={0} | all-to-all | bytes 1572864 | tf_op jit(solution)/shard_map/all_to_all | solution.py:17
  43.5 0.9 broadcast_in_dim.164
  44.4 7.3 %all-to-all-start.1 = ((bf16[8,32,1088]{2,1,0:T(8,128)(2,1)}), bf16[8,32,1088]{2,1,0:T(8,128)(2,1)S(1)}, u32[]{:S(2)}, u32[]{:S(2)}) async-start(bf16[8,32,1088]{2,1,0:T(8,128)(2,1)} %broadcast_in_dim.164), calls=%async_computation.1 | async-start | bytes 1179648 | tf_op jit(solution)/shard_map/all_to_all | solution.py:17
  52.3 24.3 %all-to-all-done.1 = bf16[8,32,1088]{2,1,0:T(8,128)(2,1)S(1)} async-done(((bf16[8,32,1088]{2,1,0:T(8,128)(2,1)}), bf16[8,32,1088]{2,1,0:T(8,128)(2,1)S(1)}, u32[]{:S(2)}, u32[]{:S(2)}) %all-to-all-start.1) | async-done | bytes 557088 | tf_op jit(solution)/shard_map/all_to_all | solution.py:17
  78.2 25.2 %all_to_all.46 = bf16[8,96,1024]{2,1,0:T(8,128)(2,1)S(1)} all-to-all(bf16[8,96,1024]{2,1,0:T(8,128)(2,1)S(1)} %pad_maximum_fusion.1), channel_id=1, replica_groups=mesh['z'=8,'x'=4,'c'=2,'y'=4] {'x','c'}, dimensions={0} | all-to-all | bytes 3145728 | tf_op jit(solution)/shard_map/all_to_all | solution.py:17
  103.4 1.1 copy-done.4
  104.7 1.4 collective-permute-start
  106.1 1.5 collective-permute-start.1
  107.6 4.9 %all-to-all-start.5 = ((bf16[8,128,384]{2,1,0:T(8,128)(2,1)}), bf16[8,128,384]{2,1,0:T(8,128)(2,1)S(1)}, u32[]{:S(2)}, u32[]{:S(2)}) async-start(bf16[8,128,384]{2,1,0:T(8,128)(2,1)} %bitcast.18), calls=%async_computation.5 | async-start | bytes 1572864 | tf_op jit(solution)/shard_map/all_to_all | solution.py:17
  113.6 21.9 %collective-permute-done = bf16[640,1024]{1,0:T(8,128)(2,1)} collective-permute-done((bf16[640,1024]{1,0:T(8,128)(2,1)S(1)}, bf16[640,1024]{1,0:T(8,128)(2,1)}, u32[]{:S(2)}, u32[]{:S(2)}) %collective-permute-start) | collective-permute-done | bytes 1310752 | tf_op jit(solution)/shard_map/ppermute | solution.py:217
  135.5 5.5 %gather_fusion.1 = bf16[32,128,384]{2,1,0:T(8,128)(2,1)} fusion(bf16[64,128,384]{2,1,0:T(8,128)(2,1)} %bitcast.131, s32[1024]{0:T(1024)S(1)} %pad_clamp_fusion.1), kind=kCustom, calls=%fused_computation.1 | custom fusion | bytes 6291584 | tf_op jit(solution)/shard_map/gather | solution.py:109
  141.0 0.9 copy-done.8
  141.9 5.4 %all-to-all-start.4 = ((bf16[8,4,128,384]{3,2,1,0:T(8,128)(2,1)}), bf16[8,4,128,384]{3,2,1,0:T(8,128)(2,1)S(1)}, u32[]{:S(2)}, u32[]{:S(2)}) async-start(bf16[8,4,128,384]{3,2,1,0:T(8,128)(2,1)} %bitcast.115), calls=%async_computation.4 | async-start | bytes 6291456 | tf_op jit(solution)/shard_map/all_to_all | solution.py:17
  147.4 1.1 slice.43
  148.5 1.4 collective-permute-start.2
  149.9 1.1 slice.44
  151.0 1.5 collective-permute-start.3
  152.5 13.8 %collective-permute-done.2 = bf16[320,1024]{1,0:T(8,128)(2,1)} collective-permute-done((bf16[320,1024]{1,0:T(8,128)(2,1)S(1)}, bf16[320,1024]{1,0:T(8,128)(2,1)}, u32[]{:S(2)}, u32[]{:S(2)}) %collective-permute-start.2) | collective-permute-done | bytes 655392 | tf_op jit(solution)/shard_map/ppermute | solution.py:221
  166.3 0.9 collective-permute-done.3
  167.2 22.6 %all-gather.7.cloned.1.call-done = bf16[8192,384]{1,0:T(8,128)(2,1)} async-done(((bf16[1024,384]{1,0:T(8,128)(2,1)}), bf16[8192,384]{1,0:T(8,128)(2,1)}) %all-gather.7.cloned.1.call-update) | async-done | bytes 6291472 | tf_op jit(solution)/shard_map/all_gather | solution.py:150
  189.8 5.4 %gather_fusion.2 = bf16[32,128,384]{2,1,0:T(8,128)(2,1)} fusion(bf16[64,128,384]{2,1,0:T(8,128)(2,1)} %bitcast.130, s32[1024]{0:T(1024)S(1)} %pad_clamp_fusion.1), kind=kCustom, calls=%fused_computation.2 | custom fusion | bytes 6291584 | tf_op jit(solution)/shard_map/gather | solution.py:109
  195.3 1.7 copy-done.2
  196.9 5.0 %all-to-all-start.6 = ((bf16[8,4,128,384]{3,2,1,0:T(8,128)(2,1)}), bf16[8,4,128,384]{3,2,1,0:T(8,128)(2,1)}, u32[]{:S(2)}, u32[]{:S(2)}) async-start(bf16[8,4,128,384]{3,2,1,0:T(8,128)(2,1)} %bitcast.112), calls=%async_computation.6 | async-start | bytes 6291456 | tf_op jit(solution)/shard_map/all_to_all | solution.py:17
  203.2 1.0 slice.66
  205.6 2.7 collective-permute-start.6
  208.3 0.8 add_select_fusion
  209.1 0.8 fusion.29
  209.8 1.3 fusion.2
  211.2 14.7 %collective-permute-done.4.refs_8_ = bf16[8,128,384]{2,1,0:T(8,128)(2,1)} collective-permute-done((bf16[8,128,384]{2,1,0:T(8,128)(2,1)S(1)}, bf16[8,128,384]{2,1,0:T(8,128)(2,1)}, u32[]{:S(2)}, u32[]{:S(2)}) %collective-permute-start.4) | collective-permute-done | bytes 786464 | tf_op jit(solution)/shard_map/ppermute | solution.py:21
  225.9 2.7 collective-permute-start.7
  228.6 0.8 select_reduce_fusion
  229.7 1.4 maximum_bitcast_fusion
  231.1 4.6 %pad_maximum_fusion = bf16[4,640,1024]{2,1,0:T(8,128)(2,1)} fusion(bf16[1,640,1024]{2,1,0:T(8,128)(2,1)} %bitcast.25, bf16[1,640,1024]{2,1,0:T(8,128)(2,1)S(1)} %maximum_bitcast_fusion, bf16[1,640,1024]{2,1,0:T(8,128)(2,1)} %bitcast.23, bf16[1,640,1024]{2,1,0:T(8,128)(2,1)S(1)} %bitcast.119), kind=kLoop, calls=%fused_computation.5 | loop fusion | flops 7864320 | bytes 10485760 | tf_op jit(solution)/shard_map/stack | solution.py:226
  235.7 5.9 %gather_fusion.4 = bf16[4,640,1024]{2,1,0:T(8,128)(2,1)} fusion(bf16[4,640,1024]{2,1,0:T(8,128)(2,1)} %pad_maximum_fusion, s32[1024]{0:T(1024)S(1)} %pad_clamp_fusion), kind=kCustom, calls=%fused_computation.4 | custom fusion | bytes 10485776 | tf_op jit(solution)/shard_map/gather | solution.py:109
  241.6 2.0 copy.88
  243.6 1.9 collective-permute-done.5.refs_7_
  245.5 2.7 collective-permute-start.9
  248.1 6.3 %convolution_bitcast_fusion.1 = f32[640,384]{1,0:T(8,128)S(1)} fusion(bf16[4,640,1024]{2,1,0:T(8,128)(2,1)} %gather_fusion.4, bf16[4,1024,384]{2,1,0:T(8,128)(2,1)} %bitcast.120), kind=kOutput, calls=%fused_computation.22 | convolution fusion | flops 2013265920 | bytes 9371648 | tf_op jit(solution)/shard_map/ymd,ydf->mf/dot_general | solution.py:249
  254.5 2.5 copy.89
  257.0 1.7 copy-done.10
  258.7 3.7 fusion.19
  262.4 1.6 collective-permute-done.8.refs_6_
  264.6 2.4 collective-permute-start.11
  267.0 1.2 gather_fusion.3
  268.2 4.9 %collective-permute-done.10.refs_4_ = bf16[4,128,384]{2,1,0:T(8,128)(2,1)S(1)} collective-permute-done((bf16[4,128,384]{2,1,0:T(8,128)(2,1)S(1)}, bf16[4,128,384]{2,1,0:T(8,128)(2,1)S(1)}, u32[]{:S(2)}, u32[]{:S(2)}) %collective-permute-start.10) | collective-permute-done | bytes 393248 | tf_op jit(solution)/shard_map/ppermute | solution.py:21
  273.2 0.7 copy-done.15
  273.9 0.8 copy-done.16
  274.7 4.6 %pick_pieces.1 = bf16[32,128,384]{2,1,0:T(8,128)(2,1)} custom-call(s32[32]{0:T(128)} %gather_fusion.3, bf16[8,128,384]{2,1,0:T(8,128)(2,1)} %copy-done.8, bf16[8,128,384]{2,1,0:T(8,128)(2,1)} %collective-permute-done.6.refs_1_, bf16[8,128,384]{2,1,0:T(8,128)(2,1)} %collective-permute-done.7.refs_2_, bf16[8,128,384]{2,1,0:T(8,128)(2,1)} %copy-done.13, ...), custom_call_target="tpu_custom_call" | custom-call | tf_op jit(solution)/shard_map/pick_pieces/pallas_call | solution.py:93
  279.3 19.7 %all-gather.9.cloned.1.call-done = bf16[5120,384]{1,0:T(8,128)(2,1)} async-done(((bf16[640,384]{1,0:T(8,128)(2,1)}), bf16[5120,384]{1,0:T(8,128)(2,1)}) %all-gather.9.cloned.1.call-update) | async-done | bytes 3932176 | tf_op jit(solution)/shard_map/all_gather | solution.py:260
  299.0 7.5 %fusion.12 = bf16[4,8,256,128]{2,3,0,1:T(8,128)(2,1)S(1)} fusion(s32[8,8,256]{2,1,0:T(8,128)S(1)} %add_select_fusion, pred[8,8,256]{2,1,0:T(8,128)(4,1)S(1)} %fusion.29, bf16[8,8,80,384,1]{3,2,1,0,4:T(8,128)(2,1)} %bitcast.136, bf16[8,4,128,384]{3,2,1,0:T(8,128)(2,1)} %bitcast.113), kind=kOutput, calls=%fused_computation.16 | convolution fusion | flops 3361734656 | bytes 9256960 | tf_op jit(solution)/shard_map/lspt,slpyr->yltr/dot_general | solution.py:268
  306.5 2.4 copy.96
  308.9 3.8 all-to-all-start.7
  312.7 28.2 %reduce-scatter.2.cloned.1.call-done = bf16[2048,128]{1,0:T(8,128)(2,1)} async-done(((bf16[8192,128]{1,0:T(8,128)(2,1)}), bf16[2048,128]{1,0:T(8,128)(2,1)}) %reduce-scatter.2.cloned.1.call-update) | async-done | bytes 524304 | tf_op jit(solution)/shard_map/reduce_scatter | solution.py:271
  340.9 1.9 copy.97
  342.8 7.5 %all-to-all-done.7 = bf16[8,4,128,384]{3,2,1,0:T(8,128)(2,1)S(1)} async-done(((bf16[8,4,128,384]{3,2,1,0:T(8,128)(2,1)}), bf16[8,4,128,384]{3,2,1,0:T(8,128)(2,1)S(1)}, u32[]{:S(2)}, u32[]{:S(2)}) %all-to-all-start.7) | async-done | bytes 3145760 | tf_op jit(solution)/shard_map/all_to_all | solution.py:17
  350.3 9.2 %all-to-all-start.8 = ((bf16[64,32,128]{2,1,0:T(8,128)(2,1)}), bf16[64,32,128]{2,1,0:T(8,128)(2,1)}, u32[]{:S(2)}, u32[]{:S(2)}) async-start(bf16[64,32,128]{2,1,0:T(8,128)(2,1)} %bitcast.129), calls=%async_computation.9 | async-start | bytes 1048576 | tf_op jit(solution)/shard_map/all_to_all | solution.py:17
  359.6 2.0 copy.93
  361.6 15.6 %all-to-all-done.8 = bf16[64,32,128]{2,1,0:T(8,128)(2,1)} async-done(((bf16[64,32,128]{2,1,0:T(8,128)(2,1)}), bf16[64,32,128]{2,1,0:T(8,128)(2,1)}, u32[]{:S(2)}, u32[]{:S(2)}) %all-to-all-start.8) | async-done | bytes 524320 | tf_op jit(solution)/shard_map/all_to_all | solution.py:17
  377.2 1.1 reduce_sum.112
  (108 shorter events, 8.6 us)
Async XLA Ops:
  7.2 8.9 %copy-start = (bf16[2,16,4096]{2,1,0:T(8,128)(2,1)S(1)}, bf16[2,16,4096]{2,1,0:T(8,128)(2,1)}, u32[]{:S(2)}) copy-start(bf16[2,16,4096]{2,1,0:T(8,128)(2,1)} %param.8) | copy-start | bytes 786436
  7.2 20.1 %copy-start.14 = (bf16[1,1024,384]{2,1,0:T(8,128)(2,1)S(1)}, bf16[1,1024,384]{2,1,0:T(8,128)(2,1)}, u32[]{:S(2)}) copy-start(bf16[1,1024,384]{2,1,0:T(8,128)(2,1)} %param.14) | copy-start | bytes 2359300
  7.2 19.1 %all-to-all-start = ((bf16[8,128,384]{2,1,0:T(8,128)(2,1)}), bf16[8,128,384]{2,1,0:T(8,128)(2,1)S(1)}, u32[]{:S(2)}, u32[]{:S(2)}) async-start(bf16[8,128,384]{2,1,0:T(8,128)(2,1)} %bitcast.132), calls=%async_computation | async-start | bytes 1572864 | tf_op jit(solution)/shard_map/all_to_all | solution.py:17
  14.0 37.6 %copy-start.17 = (s32[64]{0:T(128)S(1)}, s32[64]{0:T(128)}, u32[]{:S(2)}) copy-start(s32[64]{0:T(128)} %param.12) | copy-start | bytes 772
  14.0 121.5 %all-gather.5.cloned.1.call-start = ((), (), s32[]{:S(2)}) async-start(), calls=%async_computation.10 | async-start | bytes 7077888 | tf_op jit(solution)/shard_map/all_gather | solution.py:150
  26.3 0.9 copy-start.11
  27.2 162.6 %all-gather.7.cloned.1.call-start = ((), (), s32[]{:S(2)}) async-start(), calls=%async_computation.11 | async-start | bytes 7077888 | tf_op jit(solution)/shard_map/all_gather | solution.py:150
  44.4 32.2 %all-to-all-start.1 = ((bf16[8,32,1088]{2,1,0:T(8,128)(2,1)}), bf16[8,32,1088]{2,1,0:T(8,128)(2,1)S(1)}, u32[]{:S(2)}, u32[]{:S(2)}) async-start(bf16[8,32,1088]{2,1,0:T(8,128)(2,1)} %broadcast_in_dim.164), calls=%async_computation.1 | async-start | bytes 1179648 | tf_op jit(solution)/shard_map/all_to_all | solution.py:17
  78.2 34.4 %copy-start.18 = (s32[64]{0:T(128)S(1)}, s32[64]{0:T(128)}, u32[]{:S(2)}) copy-start(s32[64]{0:T(128)} %param.11) | copy-start | bytes 772
  103.4 1.1 copy-start.4
  104.7 36.3 %copy-start.5 = (bf16[8,80,1024]{2,1,0:T(8,128)(2,1)}, bf16[8,80,1024]{2,1,0:T(8,128)(2,1)S(1)}, u32[]{:S(2)}) copy-start(bf16[8,80,1024]{2,1,0:T(8,128)(2,1)S(1)} %slice.65) | copy-start | bytes 3932164
  104.7 30.8 %collective-permute-start = (bf16[640,1024]{1,0:T(8,128)(2,1)S(1)}, bf16[640,1024]{1,0:T(8,128)(2,1)}, u32[]{:S(2)}, u32[]{:S(2)}) collective-permute-start(bf16[640,1024]{1,0:T(8,128)(2,1)S(1)} %bitcast.117), channel_id=1, source_target_pairs={{0,1},{1,2},{2,3},{3,0},{4,5},{5,6},{6,7},{7,4},{8,9},{9,10},{10,1... | collective-permute-start | bytes 3932168 | tf_op jit(solution)/shard_map/ppermute | solution.py:217
  106.1 29.4 %collective-permute-start.1 = (bf16[640,1024]{1,0:T(8,128)(2,1)S(1)}, bf16[640,1024]{1,0:T(8,128)(2,1)}, u32[]{:S(2)}, u32[]{:S(2)}) collective-permute-start(bf16[640,1024]{1,0:T(8,128)(2,1)S(1)} %bitcast.118), channel_id=1, source_target_pairs={{0,3},{1,0},{2,1},{3,2},{4,7},{5,4},{6,5},{7,6},{8,11},{9,8},{10,9... | collective-permute-start | bytes 3932168 | tf_op jit(solution)/shard_map/ppermute | solution.py:218
  107.6 33.4 %all-to-all-start.5 = ((bf16[8,128,384]{2,1,0:T(8,128)(2,1)}), bf16[8,128,384]{2,1,0:T(8,128)(2,1)S(1)}, u32[]{:S(2)}, u32[]{:S(2)}) async-start(bf16[8,128,384]{2,1,0:T(8,128)(2,1)} %bitcast.18), calls=%async_computation.5 | async-start | bytes 1572864 | tf_op jit(solution)/shard_map/all_to_all | solution.py:17
  141.0 0.9 copy-start.8
  141.9 53.3 %all-to-all-start.4 = ((bf16[8,4,128,384]{3,2,1,0:T(8,128)(2,1)}), bf16[8,4,128,384]{3,2,1,0:T(8,128)(2,1)S(1)}, u32[]{:S(2)}, u32[]{:S(2)}) async-start(bf16[8,4,128,384]{3,2,1,0:T(8,128)(2,1)} %bitcast.115), calls=%async_computation.4 | async-start | bytes 6291456 | tf_op jit(solution)/shard_map/all_to_all | solution.py:17
  148.5 17.8 %collective-permute-start.2 = (bf16[320,1024]{1,0:T(8,128)(2,1)S(1)}, bf16[320,1024]{1,0:T(8,128)(2,1)}, u32[]{:S(2)}, u32[]{:S(2)}) collective-permute-start(bf16[320,1024]{1,0:T(8,128)(2,1)S(1)} %slice.43), channel_id=1, source_target_pairs={{0,1},{1,2},{2,3},{3,0},{4,5},{5,6},{6,7},{7,4},{8,9},{9,10},{10,1... | collective-permute-start | bytes 1966088 | tf_op jit(solution)/shard_map/ppermute | solution.py:221
  151.0 16.2 %collective-permute-start.3 = (bf16[320,1024]{1,0:T(8,128)(2,1)S(1)}, bf16[320,1024]{1,0:T(8,128)(2,1)}, u32[]{:S(2)}, u32[]{:S(2)}) collective-permute-start(bf16[320,1024]{1,0:T(8,128)(2,1)S(1)} %slice.44), channel_id=1, source_target_pairs={{0,3},{1,0},{2,1},{3,2},{4,7},{5,4},{6,5},{7,6},{8,11},{9,8},{10,9... | collective-permute-start | bytes 1966088 | tf_op jit(solution)/shard_map/ppermute | solution.py:222
  195.3 1.7 copy-start.2
  196.9 48.5 %all-to-all-start.6 = ((bf16[8,4,128,384]{3,2,1,0:T(8,128)(2,1)}), bf16[8,4,128,384]{3,2,1,0:T(8,128)(2,1)}, u32[]{:S(2)}, u32[]{:S(2)}) async-start(bf16[8,4,128,384]{3,2,1,0:T(8,128)(2,1)} %bitcast.112), calls=%async_computation.6 | async-start | bytes 6291456 | tf_op jit(solution)/shard_map/all_to_all | solution.py:17
  201.9 3.6 copy-start.9
  201.9 97.1 %all-gather.9.cloned.1.call-start = ((), (), s32[]{:S(2)}) async-start(), calls=%async_computation.13 | async-start | bytes 4423680 | tf_op jit(solution)/shard_map/all_gather | solution.py:260
  205.0 26.1 %copy-start.6 = (bf16[8,80,1024]{2,1,0:T(8,128)(2,1)S(1)}, bf16[8,80,1024]{2,1,0:T(8,128)(2,1)}, u32[]{:S(2)}) copy-start(bf16[8,80,1024]{2,1,0:T(8,128)(2,1)} %copy-done.5) | copy-start | bytes 3932164
  205.6 20.3 %collective-permute-start.4 = (bf16[8,128,384]{2,1,0:T(8,128)(2,1)S(1)}, bf16[8,128,384]{2,1,0:T(8,128)(2,1)}, u32[]{:S(2)}, u32[]{:S(2)}) collective-permute-start(bf16[8,128,384]{2,1,0:T(8,128)(2,1)S(1)} %copy-done.9), channel_id=1, source_target_pairs={{0,32},{32,64},{64,96},{96,128},{128,160},{160,192},{192,224},{224... | collective-permute-start | bytes 2359304 | tf_op jit(solution)/shard_map/ppermute | solution.py:21
  205.6 20.3 %collective-permute-start.6 = (bf16[8,128,384]{2,1,0:T(8,128)(2,1)S(1)}, bf16[8,128,384]{2,1,0:T(8,128)(2,1)}, u32[]{:S(2)}, u32[]{:S(2)}) collective-permute-start(bf16[8,128,384]{2,1,0:T(8,128)(2,1)S(1)} %copy-done.9), channel_id=1, source_target_pairs={{0,224},{32,0},{64,32},{96,64},{128,96},{160,128},{192,160},{224,1... | collective-permute-start | bytes 2359304 | tf_op jit(solution)/shard_map/ppermute | solution.py:21
  225.9 19.6 %collective-permute-start.5 = (bf16[8,128,384]{2,1,0:T(8,128)(2,1)}, bf16[8,128,384]{2,1,0:T(8,128)(2,1)}, u32[]{:S(2)}, u32[]{:S(2)}) collective-permute-start(bf16[8,128,384]{2,1,0:T(8,128)(2,1)} %collective-permute-done.4.refs_8_), channel_id=1, source_target_pairs={{0,32},{32,64},{64,96},{96,128},{128,160},{160,192},{192,224},{224... | collective-permute-start | bytes 2359304 | tf_op jit(solution)/shard_map/ppermute | solution.py:21
  225.9 19.5 %collective-permute-start.7 = (bf16[8,128,384]{2,1,0:T(8,128)(2,1)}, bf16[8,128,384]{2,1,0:T(8,128)(2,1)}, u32[]{:S(2)}, u32[]{:S(2)}) collective-permute-start(bf16[8,128,384]{2,1,0:T(8,128)(2,1)} %collective-permute-done.6.refs_1_), channel_id=1, source_target_pairs={{0,224},{32,0},{64,32},{96,64},{128,96},{160,128},{192,160},{224,1... | collective-permute-start | bytes 2359304 | tf_op jit(solution)/shard_map/ppermute | solution.py:21
  235.7 5.9 %copy-start.3 = (bf16[8,4,128,384]{3,2,1,0:T(8,128)(2,1)S(1)}, bf16[8,4,128,384]{3,2,1,0:T(8,128)(2,1)}, u32[]{:S(2)}) copy-start(bf16[8,4,128,384]{3,2,1,0:T(8,128)(2,1)} %copy-done.2) | copy-start | bytes 9437188
  245.5 18.5 %collective-permute-start.8 = (bf16[8,128,384]{2,1,0:T(8,128)(2,1)}, bf16[8,128,384]{2,1,0:T(8,128)(2,1)S(1)}, u32[]{:S(2)}, u32[]{:S(2)}) collective-permute-start(bf16[8,128,384]{2,1,0:T(8,128)(2,1)} %collective-permute-done.5.refs_7_), channel_id=1, source_target_pairs={{0,32},{32,64},{64,96},{96,128},{128,160},{160,192},{192,224},{224... | collective-permute-start | bytes 2359304 | tf_op jit(solution)/shard_map/ppermute | solution.py:21
  245.5 18.5 %collective-permute-start.9 = (bf16[8,128,384]{2,1,0:T(8,128)(2,1)}, bf16[8,128,384]{2,1,0:T(8,128)(2,1)S(1)}, u32[]{:S(2)}, u32[]{:S(2)}) collective-permute-start(bf16[8,128,384]{2,1,0:T(8,128)(2,1)} %collective-permute-done.7.refs_2_), channel_id=1, source_target_pairs={{0,224},{32,0},{64,32},{96,64},{128,96},{160,128},{192,160},{224,1... | collective-permute-start | bytes 2359304 | tf_op jit(solution)/shard_map/ppermute | solution.py:21
  254.5 4.2 %copy-start.7 = (bf16[4,640,1024]{2,1,0:T(8,128)(2,1)S(1)}, bf16[4,640,1024]{2,1,0:T(8,128)(2,1)}, u32[]{:S(2)}) copy-start(bf16[4,640,1024]{2,1,0:T(8,128)(2,1)} %gather_fusion.4) | copy-start | bytes 15728644
  257.0 1.7 copy-start.10
  264.0 9.2 %copy-start.12 = (bf16[8,128,384]{2,1,0:T(8,128)(2,1)}, bf16[8,128,384]{2,1,0:T(8,128)(2,1)S(1)}, u32[]{:S(2)}) copy-start(bf16[8,128,384]{2,1,0:T(8,128)(2,1)S(1)} %collective-permute-done.8.refs_6_) | copy-start | bytes 2359300
  264.0 9.2 %copy-start.13 = (bf16[8,128,384]{2,1,0:T(8,128)(2,1)}, bf16[8,128,384]{2,1,0:T(8,128)(2,1)S(1)}, u32[]{:S(2)}) copy-start(bf16[8,128,384]{2,1,0:T(8,128)(2,1)S(1)} %collective-permute-done.9.refs_3_) | copy-start | bytes 2359300
  264.0 76.9 %reduce-scatter.2.cloned.1.call-start = ((), (), s32[]{:S(2)}) async-start(), calls=%async_computation.12 | async-start | bytes 2621440 | tf_op jit(solution)/shard_map/reduce_scatter | solution.py:271
  264.1 9.0 %collective-permute-start.10 = (bf16[4,128,384]{2,1,0:T(8,128)(2,1)S(1)}, bf16[4,128,384]{2,1,0:T(8,128)(2,1)S(1)}, u32[]{:S(2)}, u32[]{:S(2)}) collective-permute-start(bf16[4,128,384]{2,1,0:T(8,128)(2,1)S(1)} %slice.50), channel_id=1, source_target_pairs={{0,32},{32,64},{64,96},{96,128},{128,160},{160,192},{192,224},{224... | collective-permute-start | bytes 1179656 | tf_op jit(solution)/shard_map/ppermute | solution.py:21
  264.6 8.5 %collective-permute-start.11 = (bf16[4,128,384]{2,1,0:T(8,128)(2,1)S(1)}, bf16[4,128,384]{2,1,0:T(8,128)(2,1)S(1)}, u32[]{:S(2)}, u32[]{:S(2)}) collective-permute-start(bf16[4,128,384]{2,1,0:T(8,128)(2,1)S(1)} %slice.51), channel_id=1, source_target_pairs={{0,224},{32,0},{64,32},{96,64},{128,96},{160,128},{192,160},{224,1... | collective-permute-start | bytes 1179656 | tf_op jit(solution)/shard_map/ppermute | solution.py:21
  273.2 0.7 copy-start.15
  273.9 0.8 copy-start.16
  308.9 41.4 %all-to-all-start.7 = ((bf16[8,4,128,384]{3,2,1,0:T(8,128)(2,1)}), bf16[8,4,128,384]{3,2,1,0:T(8,128)(2,1)S(1)}, u32[]{:S(2)}, u32[]{:S(2)}) async-start(bf16[8,4,128,384]{3,2,1,0:T(8,128)(2,1)} %bitcast.114), calls=%async_computation.7 | async-start | bytes 6291456 | tf_op jit(solution)/shard_map/all_to_all | solution.py:17
  350.3 26.9 %all-to-all-start.8 = ((bf16[64,32,128]{2,1,0:T(8,128)(2,1)}), bf16[64,32,128]{2,1,0:T(8,128)(2,1)}, u32[]{:S(2)}, u32[]{:S(2)}) async-start(bf16[64,32,128]{2,1,0:T(8,128)(2,1)} %bitcast.129), calls=%async_computation.9 | async-start | bytes 1048576 | tf_op jit(solution)/shard_map/all_to_all | solution.py:17
  359.6 19.5 %copy-start.1 = (bf16[2,16,4096]{2,1,0:T(8,128)(2,1)S(1)}, bf16[2,16,4096]{2,1,0:T(8,128)(2,1)}, u32[]{:S(2)}) copy-start(bf16[2,16,4096]{2,1,0:T(8,128)(2,1)} %param.8) | copy-start | bytes 786436
Sparse Core Ops, SparseCore 0:
  27.4 87.5 all-gather.4
  116.7 73.0 all-gather.6
  264.1 34.8 all-gather.8
  309.0 31.8 reduce-scatter.1
where the time goes:
time: 387 us; the launch traced here: 386 us
  waiting for transfers between devices  188 us (49%)
  starting transfers between devices  59.3 us (15%)
  local copies, waits for them, and re-layouts  46.1 us (12%)
  blocking collectives  41.4 us (11%)
  matrix products  18.5 us (5%)
  between operations  14.1 us (4%)
  other arithmetic  13.6 us (4%)
  Pallas kernels  4.63 us (1%)
    all_to_all x7, waiting for transfers between devices, exchange(): return lax.all_to_all(value, axes, split_axis=0, concat_axis=0, tiled=True)  57.6 us
    all_to_all x7, starting transfers between devices, exchange(): return lax.all_to_all(value, axes, split_axis=0, concat_axis=0, tiled=True)  42.4 us
    all_to_all x2, blocking collectives, exchange(): return lax.all_to_all(value, axes, split_axis=0, concat_axis=0, tiled=True)  41.4 us
    reduce_scatter x1, waiting for transfers between devices, body(): lax.psum_scatter(plane_out.reshape(-1, block_rows), 'y', scatter_dimensio...  28.2 us
    ppermute x8, waiting for transfers between devices, shift(): return lax.ppermute(value, 'z', [(i, (i + step) % Z) for i in range(Z)])  23.1 us
    all_gather x2, waiting for transfers between devices, gather_planes(): rows = lax.all_gather(block.reshape(-1, width), 'z', axis=0, tiled=True)  22.6 us
    ppermute x1, waiting for transfers between devices, body(): from_last = lax.ppermute(quarters, 'y', to_next)  21.9 us
    all_gather x1, waiting for transfers between devices, body(): lax.all_gather(hidden, XC, axis=0, tiled=False)  19.7 us
  transfers between devices with their start and end apart: 23, of which 14 were waited for; matrix products, arithmetic and copies ran while one was open for 15% of the time, Pallas kernels for 1%

commit v1 on v0

--- a/solution.py
+++ b/solution.py
@@ -175,9 +175,12 @@
     block_up = spread(train_up)
     block_up, train_down = lax.optimization_barrier((block_up, train_down))
     up_all = gather_planes(block_up)
-    line_block = exchange(jnp.broadcast_to(own_block, (Z,) + own_block.shape), "z")
-    line_block, train_down = lax.optimization_barrier((line_block, train_down))
+    own_block = jnp.pad(own_block, ((0, 0), (0, -own_block.shape[1] % 128)))
+    token_ring = Ring(own_block.reshape(2, own_tokens // 2, -1)).hop().hop().hop().hop()
+    train_down = token_ring.hold(train_down)
     block_down = spread(train_down)
+    planes = jnp.arange(Z, dtype=jnp.int32)
+    line_block = token_ring.pick(((planes - plane + Z) % Z * 16)[:, None] + jnp.arange(2)[None, :])
     line_block = line_block.reshape(line_tokens, -1)
     line_rows = line_block[:, :out_width]
     line_routes = line_block[:, out_width : out_width + 4 * EXPERTS]
@@ -221,11 +224,11 @@
         lax.ppermute(from_last[:half], "y", to_next),
         lax.ppermute(from_next[half:], "y", to_last),
     ]
-    up_all, far, block_down = lax.optimization_barrier((up_all, far, block_down))
     inputs = take_rows(
         jnp.stack([quarters, from_next, jnp.concatenate(far, axis=0), from_last]),
         (jnp.arange(Y, dtype=jnp.int32) - quarter + Y) % Y,
     )
+    up_all, inputs, block_down = lax.optimization_barrier((up_all, inputs, block_down))
     routes = received[:, capacity:].reshape(PLANE, line_tokens, -1)
     placing = place(routes, jnp.arange(PLANE, dtype=jnp.int32))
     weights = sum(
@@ -239,23 +242,24 @@
     row_weight = jnp.sum(jnp.where(own_sent, own_weight[:, None, :], 0.0), axis=2)
     placing = placing.astype(jnp.bfloat16)
 
+    by_part = (part_count, piece_rows, width)
     serve_gate = assemble(exchange(take_rows(gate_all, chosen_slot), XC))
     arrived_up = exchange(take_rows(up_all, chosen_slot), XC)
-    down_ring = Ring(block_down).hop().hop()
+    gate_act = jnp.einsum(
+        "ymd,ydf->mf", inputs, serve_gate.reshape(by_part), preferred_element_type=jnp.float32
+    )
+    arrived_up, gate_act = lax.optimization_barrier((arrived_up, gate_act))
+    down_ring = Ring(block_down).hop()
     arrived_up = down_ring.hold(arrived_up)
     down_ring.hop()
     serve_up = assemble(arrived_up)
-    by_part = (part_count, piece_rows, width)
-    gate_act = jnp.einsum(
-        "ymd,ydf->mf", inputs, serve_gate.reshape(by_part), preferred_element_type=jnp.float32
-    )
     up_act = jnp.einsum(
         "ymd,ydf->mf", inputs, serve_up.reshape(by_part), preferred_element_type=jnp.float32
     )
     hidden = (jax.nn.silu(gate_act) * up_act * row_weight.reshape(-1, 1)).astype(jnp.bfloat16)
 
     hidden = down_ring.hold(hidden)
-    down_ring.hop()
+    down_ring.hop().hop()
 
     plane_hidden = lax.all_gather(hidden, XC, axis=0, tiled=False).reshape(
         PLANE, PLANE, capacity, width

time: 387 us -> 380 us (0.982)
  waiting for transfers between devices: 188 us -> 167 us
  starting transfers between devices: 59.3 us -> 65.2 us
    all_gather x2, waiting for transfers between devices: 22.6 us -> 0.33 us  [gather_planes(): rows = lax.all_gather(block.reshape(-1, width), 'z', axis=0, tiled=True)]
    ppermute x8 -> x16, waiting for transfers between devices: 23.1 us -> 45.2 us  [shift(): return lax.ppermute(value, 'z', [(i, (i + step) % Z) for i in range(Z)])]
    ppermute x1, waiting for transfers between devices: 0.01 us -> 21.2 us  [body(): from_next = lax.ppermute(quarters, 'y', to_last)]
    all_gather x1, waiting for transfers between devices: 19.7 us -> 0.02 us  [body(): lax.all_gather(hidden, XC, axis=0, tiled=False)]
    ppermute x1, waiting for transfers between devices: 21.9 us -> 3.23 us  [body(): from_last = lax.ppermute(quarters, 'y', to_next)]
    ppermute x8 -> x16, starting transfers between devices: 10.9 us -> 22 us  [shift(): return lax.ppermute(value, 'z', [(i, (i + step) % Z) for i in range(Z)])]
    all_to_all x7 -> x6, starting transfers between devices: 42.4 us -> 37.3 us  [exchange(): return lax.all_to_all(value, axes, split_axis=0, concat_axis=0, tiled=True)]
    unnamed x41 -> x63, local copies, waits for them, and re-layouts: 9.4 us -> 11.5 us
  transfers between devices with their start and end apart: 23 -> 30, of which waited for: 14 -> 19; matrix products, arithmetic and copies ran while one was open for 15% -> 16% of each run, Pallas kernels for 1% -> 2%
where the time goes in v1:
time: 380 us; the launch traced here: 379 us
  waiting for transfers between devices  167 us (44%)
  starting transfers between devices  65.2 us (17%)
  local copies, waits for them, and re-layouts  47.2 us (12%)
  blocking collectives  43.1 us (11%)
  matrix products  22 us (6%)
  between operations  14.3 us (4%)
  other arithmetic  12.5 us (3%)
  Pallas kernels  7.24 us (2%)
    all_to_all x6, waiting for transfers between devices, exchange(): return lax.all_to_all(value, axes, split_axis=0, concat_axis=0, tiled=True)  57.5 us
    ppermute x16, waiting for transfers between devices, shift(): return lax.ppermute(value, 'z', [(i, (i + step) % Z) for i in range(Z)])  45.2 us
    all_to_all x2, blocking collectives, exchange(): return lax.all_to_all(value, axes, split_axis=0, concat_axis=0, tiled=True)  43.1 us
    all_to_all x6, starting transfers between devices, exchange(): return lax.all_to_all(value, axes, split_axis=0, concat_axis=0, tiled=True)  37.3 us
    reduce_scatter x1, waiting for transfers between devices, body(): lax.psum_scatter(plane_out.reshape(-1, block_rows), 'y', scatter_dimensio...  24.6 us
    ppermute x16, starting transfers between devices, shift(): return lax.ppermute(value, 'z', [(i, (i + step) % Z) for i in range(Z)])  22 us
    ppermute x1, waiting for transfers between devices, body(): from_next = lax.ppermute(quarters, 'y', to_last)  21.2 us
    gather x6, local copies, waits for them, and re-layouts, take_rows(): return value.at[index].get(mode='promise_in_bounds')  18.6 us
  transfers between devices with their start and end apart: 30, of which 19 were waited for; matrix products, arithmetic and copies ran while one was open for 16% of the time, Pallas kernels for 2%

profile of v1, /device:TPU:1, one launch (start us, length us, event | category | flops | bytes accessed | tf_op | source)
XLA Modules:
  0.0 378.6 jit_solution(13942787293361784708)
XLA Ops:
  7.2 6.8 %all-to-all-start = ((bf16[8,128,384]{2,1,0:T(8,128)(2,1)}), bf16[8,128,384]{2,1,0:T(8,128)(2,1)S(1)}, u32[]{:S(2)}, u32[]{:S(2)}) async-start(bf16[8,128,384]{2,1,0:T(8,128)(2,1)} %bitcast.133), calls=%async_computation | async-start | bytes 1572864 | tf_op jit(solution)/shard_map/all_to_all | solution.py:17
  16.1 10.2 %all-to-all-done = bf16[8,128,384]{2,1,0:T(8,128)(2,1)S(1)} async-done(((bf16[8,128,384]{2,1,0:T(8,128)(2,1)}), bf16[8,128,384]{2,1,0:T(8,128)(2,1)S(1)}, u32[]{:S(2)}, u32[]{:S(2)}) %all-to-all-start) | async-done | bytes 786464 | tf_op jit(solution)/shard_map/all_to_all | solution.py:17
  26.3 0.9 copy-done.11
  27.3 16.2 %all_to_all.40 = bf16[8,128,384]{2,1,0:T(8,128)(2,1)} all-to-all(bf16[8,128,384]{2,1,0:T(8,128)(2,1)S(1)} %bitcast.134), channel_id=1, replica_groups=mesh['z'=8,'x'=4,'c'=2,'y'=4] {'x','c'}, dimensions={0} | all-to-all | bytes 1572864 | tf_op jit(solution)/shard_map/all_to_all | solution.py:17
  43.8 0.8 collective-permute-start.3
  44.6 4.0 %collective-permute-start = (bf16[2,16,1152]{2,1,0:T(8,128)(2,1)S(1)}, bf16[2,16,1152]{2,1,0:T(8,128)(2,1)S(1)}, u32[]{:S(2)}, u32[]{:S(2)}) collective-permute-start(bf16[2,16,1152]{2,1,0:T(8,128)(2,1)S(1)} %bitcast.137), channel_id=1, source_target_pairs={{0,224},{32,0},{64,32},{96,64},{128,96},{160,128},{192,160},{224,1... | collective-permute-start | bytes 221192 | tf_op jit(solution)/shard_map/ppermute | solution.py:21
  48.7 3.9 %collective-permute-done.3.refs_8_ = bf16[2,16,1152]{2,1,0:T(8,128)(2,1)S(1)} collective-permute-done((bf16[2,16,1152]{2,1,0:T(8,128)(2,1)S(1)}, bf16[2,16,1152]{2,1,0:T(8,128)(2,1)S(1)}, u32[]{:S(2)}, u32[]{:S(2)}) %collective-permute-start.3) | collective-permute-done | bytes 73760 | tf_op jit(solution)/shard_map/ppermute | solution.py:21
  52.7 2.7 collective-permute-start.1
  55.4 3.7 collective-permute-done.4.refs_7_
  59.2 2.7 collective-permute-start.2
  61.9 3.7 collective-permute-done.5.refs_6_
  65.6 2.7 collective-permute-start.7
  69.2 1.5 collective-permute-done.6.refs_4_
  71.9 2.7 pick_pieces.2
  74.6 0.9 slice_bitcast_fusion.4
  76.4 1.6 convolution_convert_fusion
  78.2 27.0 %all_to_all.41 = bf16[8,96,1024]{2,1,0:T(8,128)(2,1)S(1)} all-to-all(bf16[8,96,1024]{2,1,0:T(8,128)(2,1)S(1)} %pad_maximum_fusion.1), channel_id=1, replica_groups=mesh['z'=8,'x'=4,'c'=2,'y'=4] {'x','c'}, dimensions={0} | all-to-all | bytes 3145728 | tf_op jit(solution)/shard_map/all_to_all | solution.py:17
  105.1 1.1 copy-done.4
  106.4 2.8 collective-permute-start.9
  109.2 4.7 %all-to-all-start.4 = ((bf16[8,128,384]{2,1,0:T(8,128)(2,1)}), bf16[8,128,384]{2,1,0:T(8,128)(2,1)S(1)}, u32[]{:S(2)}, u32[]{:S(2)}) async-start(bf16[8,128,384]{2,1,0:T(8,128)(2,1)} %bitcast.24), calls=%async_computation.4 | async-start | bytes 1572864 | tf_op jit(solution)/shard_map/all_to_all | solution.py:17
  115.1 21.2 %collective-permute-done.9 = bf16[640,1024]{1,0:T(8,128)(2,1)} collective-permute-done((bf16[640,1024]{1,0:T(8,128)(2,1)S(1)}, bf16[640,1024]{1,0:T(8,128)(2,1)}, u32[]{:S(2)}, u32[]{:S(2)}) %collective-permute-start.9) | collective-permute-done | bytes 1310752 | tf_op jit(solution)/shard_map/ppermute | solution.py:221
  136.3 3.2 collective-permute-done.8
  139.5 5.5 %gather_fusion.1 = bf16[32,128,384]{2,1,0:T(8,128)(2,1)} fusion(bf16[64,128,384]{2,1,0:T(8,128)(2,1)} %bitcast.132, s32[1024]{0:T(1024)S(1)} %pad_clamp_fusion.1), kind=kCustom, calls=%fused_computation.1 | custom fusion | bytes 6291584 | tf_op jit(solution)/shard_map/gather | solution.py:109
  145.1 0.9 copy-done.7
  145.9 5.7 %all-to-all-start.3 = ((bf16[8,4,128,384]{3,2,1,0:T(8,128)(2,1)}), bf16[8,4,128,384]{3,2,1,0:T(8,128)(2,1)S(1)}, u32[]{:S(2)}, u32[]{:S(2)}) async-start(bf16[8,4,128,384]{3,2,1,0:T(8,128)(2,1)} %bitcast.114), calls=%async_computation.3 | async-start | bytes 6291456 | tf_op jit(solution)/shard_map/all_to_all | solution.py:17
  151.7 1.2 slice.52
  152.9 1.1 slice.51
  154.3 2.7 collective-permute-start.11
  157.1 14.9 %collective-permute-done.10 = bf16[320,1024]{1,0:T(8,128)(2,1)S(1)} collective-permute-done((bf16[320,1024]{1,0:T(8,128)(2,1)S(1)}, bf16[320,1024]{1,0:T(8,128)(2,1)S(1)}, u32[]{:S(2)}, u32[]{:S(2)}) %collective-permute-start.10) | collective-permute-done | bytes 655392 | tf_op jit(solution)/shard_map/ppermute | solution.py:224
  172.1 4.6 %pad_maximum_fusion = bf16[4,640,1024]{2,1,0:T(8,128)(2,1)} fusion(bf16[1,640,1024]{2,1,0:T(8,128)(2,1)} %bitcast.22, bf16[1,640,1024]{2,1,0:T(8,128)(2,1)S(1)} %maximum_bitcast_fusion, bf16[1,640,1024]{2,1,0:T(8,128)(2,1)} %bitcast.20, bf16[1,640,1024]{2,1,0:T(8,128)(2,1)S(1)} %bitcast.120), kind=kLoop, calls=%fused_computation.5 | loop fusion | flops 7864320 | bytes 10485760 | tf_op jit(solution)/shard_map/stack | solution.py:228
  176.7 5.7 %gather_fusion.2 = bf16[4,640,1024]{2,1,0:T(8,128)(2,1)} fusion(bf16[4,640,1024]{2,1,0:T(8,128)(2,1)} %pad_maximum_fusion, s32[1024]{0:T(1024)S(1)} %pad_clamp_fusion), kind=kCustom, calls=%fused_computation.2 | custom fusion | bytes 10485776 | tf_op jit(solution)/shard_map/gather | solution.py:109
  182.7 5.4 %gather_fusion.3 = bf16[32,128,384]{2,1,0:T(8,128)(2,1)} fusion(bf16[64,128,384]{2,1,0:T(8,128)(2,1)} %bitcast.131, s32[1024]{0:T(1024)S(1)} %pad_clamp_fusion.1), kind=kCustom, calls=%fused_computation.3 | custom fusion | bytes 6291584 | tf_op jit(solution)/shard_map/gather | solution.py:109
  188.2 1.1 all-to-all-done.3
  189.3 1.7 copy-done.2
  190.9 5.2 %all-to-all-start.5 = ((bf16[8,4,128,384]{3,2,1,0:T(8,128)(2,1)}), bf16[8,4,128,384]{3,2,1,0:T(8,128)(2,1)}, u32[]{:S(2)}, u32[]{:S(2)}) async-start(bf16[8,4,128,384]{3,2,1,0:T(8,128)(2,1)} %bitcast.113), calls=%async_computation.5 | async-start | bytes 6291456 | tf_op jit(solution)/shard_map/all_to_all | solution.py:17
  197.4 1.0 slice.76
  201.2 1.3 fusion.2
  202.6 2.5 collective-permute-start.13
  206.5 1.7 copy-done.9
  208.1 6.3 %convolution_bitcast_fusion.1 = f32[640,384]{1,0:T(8,128)} fusion(bf16[4,640,1024]{2,1,0:T(8,128)(2,1)} %gather_fusion.2, bf16[4,1024,384]{2,1,0:T(8,128)(2,1)S(1)} %bitcast.121), kind=kOutput, calls=%fused_computation.22 | convolution fusion | flops 2013265920 | bytes 9371648 | tf_op jit(solution)/shard_map/ymd,ydf->mf/dot_general | solution.py:248
  214.4 19.4 %all-to-all-done.5 = bf16[8,4,128,384]{3,2,1,0:T(8,128)(2,1)} async-done(((bf16[8,4,128,384]{3,2,1,0:T(8,128)(2,1)}), bf16[8,4,128,384]{3,2,1,0:T(8,128)(2,1)}, u32[]{:S(2)}, u32[]{:S(2)}) %all-to-all-start.5) | async-done | bytes 3145760 | tf_op jit(solution)/shard_map/all_to_all | solution.py:17
  233.8 2.5 collective-permute-start.15
  236.6 2.5 copy.90
  239.1 1.7 copy-done.10
  240.8 6.2 %fusion.19 = bf16[640,384]{1,0:T(8,128)(2,1)} fusion(bf16[4,640,1024]{2,1,0:T(8,128)(2,1)} %gather_fusion.2, bf16[4,1024,384]{2,1,0:T(8,128)(2,1)S(1)} %bitcast.123, f32[640,384]{1,0:T(8,128)S(1)} %copy-done.29, f32[640]{0:T(1024)S(1)} %mul.54), kind=kOutput, calls=%fused_computation.24 | convolution fusion | flops 2014986240 | bytes 9865728 | tf_op jit(solution)/shard_map/ymd,ydf->mf/dot_general | solution.py:256
  247.0 5.6 %collective-permute-done.15.refs_2_ = bf16[8,128,384]{2,1,0:T(8,128)(2,1)S(1)} collective-permute-done((bf16[8,128,384]{2,1,0:T(8,128)(2,1)}, bf16[8,128,384]{2,1,0:T(8,128)(2,1)S(1)}, u32[]{:S(2)}, u32[]{:S(2)}) %collective-permute-start.15) | collective-permute-done | bytes 786464 | tf_op jit(solution)/shard_map/ppermute | solution.py:21
  252.6 3.1 collective-permute-done.14.refs_7_
  255.8 1.0 collective-permute-start.16
  257.3 15.8 %collective-permute-done.16.refs_3_ = bf16[8,128,384]{2,1,0:T(8,128)(2,1)S(1)} collective-permute-done((bf16[8,128,384]{2,1,0:T(8,128)(2,1)}, bf16[8,128,384]{2,1,0:T(8,128)(2,1)S(1)}, u32[]{:S(2)}, u32[]{:S(2)}) %collective-permute-start.16) | collective-permute-done | bytes 786464 | tf_op jit(solution)/shard_map/ppermute | solution.py:21
  273.2 2.5 collective-permute-start.19
  275.9 1.2 gather_fusion.4
  277.1 4.4 %collective-permute-done.19.refs_5_ = bf16[4,128,384]{2,1,0:T(8,128)(2,1)S(1)} collective-permute-done((bf16[4,128,384]{2,1,0:T(8,128)(2,1)S(1)}, bf16[4,128,384]{2,1,0:T(8,128)(2,1)S(1)}, u32[]{:S(2)}, u32[]{:S(2)}) %collective-permute-start.19) | collective-permute-done | bytes 393248 | tf_op jit(solution)/shard_map/ppermute | solution.py:21
  281.5 3.4 collective-permute-done.18.refs_4_
  285.7 4.6 %pick_pieces.3 = bf16[32,128,384]{2,1,0:T(8,128)(2,1)} custom-call(s32[32]{0:T(128)} %gather_fusion.4, bf16[8,128,384]{2,1,0:T(8,128)(2,1)} %copy-done.7, bf16[8,128,384]{2,1,0:T(8,128)(2,1)} %collective-permute-done.13.refs_1_, bf16[8,128,384]{2,1,0:T(8,128)(2,1)} %copy-done.14, bf16[8,128,384]{2,1,0:T(8,128)(2,1)} %copy-done.12, ...), custom_call_target="tpu_custom_call" | custom-call | tf_op jit(solution)/shard_map/pick_pieces/pallas_call | solution.py:93
  290.3 7.5 %fusion.12 = bf16[4,8,256,128]{2,3,0,1:T(8,128)(2,1)S(1)} fusion(s32[8,8,256]{2,1,0:T(8,128)S(1)} %add_select_fusion, pred[8,8,256]{2,1,0:T(8,128)(4,1)S(1)} %fusion.29, bf16[8,8,80,384,1]{3,2,1,0,4:T(8,128)(2,1)} %bitcast.140, bf16[8,4,128,384]{3,2,1,0:T(8,128)(2,1)} %bitcast.115), kind=kOutput, calls=%fused_computation.16 | convolution fusion | flops 3361734656 | bytes 9256960 | tf_op jit(solution)/shard_map/lspt,slpyr->yltr/dot_general | solution.py:272
  297.8 2.4 copy.96
  300.2 7.2 %all-to-all-start.6 = ((bf16[8,4,128,384]{3,2,1,0:T(8,128)(2,1)}), bf16[8,4,128,384]{3,2,1,0:T(8,128)(2,1)S(1)}, u32[]{:S(2)}, u32[]{:S(2)}) async-start(bf16[8,4,128,384]{3,2,1,0:T(8,128)(2,1)} %bitcast.116), calls=%async_computation.6 | async-start | bytes 6291456 | tf_op jit(solution)/shard_map/all_to_all | solution.py:17
  307.4 24.6 %reduce-scatter.2.cloned.1.call-done = bf16[2048,128]{1,0:T(8,128)(2,1)} async-done(((bf16[8192,128]{1,0:T(8,128)(2,1)}), bf16[2048,128]{1,0:T(8,128)(2,1)}) %reduce-scatter.2.cloned.1.call-update) | async-done | bytes 524304 | tf_op jit(solution)/shard_map/reduce_scatter | solution.py:275
  332.0 1.9 copy.97
  333.9 11.1 %all-to-all-done.6 = bf16[8,4,128,384]{3,2,1,0:T(8,128)(2,1)S(1)} async-done(((bf16[8,4,128,384]{3,2,1,0:T(8,128)(2,1)}), bf16[8,4,128,384]{3,2,1,0:T(8,128)(2,1)S(1)}, u32[]{:S(2)}, u32[]{:S(2)}) %all-to-all-start.6) | async-done | bytes 3145760 | tf_op jit(solution)/shard_map/all_to_all | solution.py:17
  345.0 7.6 %all-to-all-start.7 = ((bf16[64,32,128]{2,1,0:T(8,128)(2,1)}), bf16[64,32,128]{2,1,0:T(8,128)(2,1)}, u32[]{:S(2)}, u32[]{:S(2)}) async-start(bf16[64,32,128]{2,1,0:T(8,128)(2,1)} %bitcast.130), calls=%async_computation.8 | async-start | bytes 1048576 | tf_op jit(solution)/shard_map/all_to_all | solution.py:17
  352.6 2.0 copy.93
  354.7 15.6 %all-to-all-done.7 = bf16[64,32,128]{2,1,0:T(8,128)(2,1)} async-done(((bf16[64,32,128]{2,1,0:T(8,128)(2,1)}), bf16[64,32,128]{2,1,0:T(8,128)(2,1)}, u32[]{:S(2)}, u32[]{:S(2)}) %all-to-all-start.7) | async-done | bytes 524320 | tf_op jit(solution)/shard_map/all_to_all | solution.py:17
  370.3 1.1 reduce_sum.112
  (149 shorter events, 15.8 us)
Async XLA Ops:
  7.2 8.9 %copy-start = (bf16[2,16,4096]{2,1,0:T(8,128)(2,1)S(1)}, bf16[2,16,4096]{2,1,0:T(8,128)(2,1)}, u32[]{:S(2)}) copy-start(bf16[2,16,4096]{2,1,0:T(8,128)(2,1)} %param.8) | copy-start | bytes 786436
  7.2 20.1 %copy-start.15 = (bf16[1,1024,384]{2,1,0:T(8,128)(2,1)S(1)}, bf16[1,1024,384]{2,1,0:T(8,128)(2,1)}, u32[]{:S(2)}) copy-start(bf16[1,1024,384]{2,1,0:T(8,128)(2,1)} %param.14) | copy-start | bytes 2359300
  7.2 36.3 %copy-start.27 = (s32[64]{0:T(128)S(1)}, s32[64]{0:T(128)}, u32[]{:S(2)}) copy-start(s32[64]{0:T(128)} %param.12) | copy-start | bytes 772
  7.2 19.1 %all-to-all-start = ((bf16[8,128,384]{2,1,0:T(8,128)(2,1)}), bf16[8,128,384]{2,1,0:T(8,128)(2,1)S(1)}, u32[]{:S(2)}, u32[]{:S(2)}) async-start(bf16[8,128,384]{2,1,0:T(8,128)(2,1)} %bitcast.133), calls=%async_computation | async-start | bytes 1572864 | tf_op jit(solution)/shard_map/all_to_all | solution.py:17
  14.0 125.5 %all-gather.5.cloned.1.call-start = ((), (), s32[]{:S(2)}) async-start(), calls=%async_computation.9 | async-start | bytes 7077888 | tf_op jit(solution)/shard_map/all_gather | solution.py:150
  26.3 0.9 copy-start.11
  27.2 155.5 %all-gather.7.cloned.1.call-start = ((), (), s32[]{:S(2)}) async-start(), calls=%async_computation.10 | async-start | bytes 7077888 | tf_op jit(solution)/shard_map/all_gather | solution.py:150
  43.8 26.9 %copy-start.18 = (bf16[32,1152]{1,0:T(8,128)(2,1)}, bf16[32,1152]{1,0:T(8,128)(2,1)S(1)}, u32[]{:S(2)}) copy-start(bf16[32,1152]{1,0:T(8,128)(2,1)S(1)} %pad.4) | copy-start | bytes 221188
  43.8 8.8 %collective-permute-start.3 = (bf16[2,16,1152]{2,1,0:T(8,128)(2,1)S(1)}, bf16[2,16,1152]{2,1,0:T(8,128)(2,1)S(1)}, u32[]{:S(2)}, u32[]{:S(2)}) collective-permute-start(bf16[2,16,1152]{2,1,0:T(8,128)(2,1)S(1)} %bitcast.136), channel_id=1, source_target_pairs={{0,32},{32,64},{64,96},{96,128},{128,160},{160,192},{192,224},{224... | collective-permute-start | bytes 221192 | tf_op jit(solution)/shard_map/ppermute | solution.py:21
  44.6 8.0 %collective-permute-start = (bf16[2,16,1152]{2,1,0:T(8,128)(2,1)S(1)}, bf16[2,16,1152]{2,1,0:T(8,128)(2,1)S(1)}, u32[]{:S(2)}, u32[]{:S(2)}) collective-permute-start(bf16[2,16,1152]{2,1,0:T(8,128)(2,1)S(1)} %bitcast.137), channel_id=1, source_target_pairs={{0,224},{32,0},{64,32},{96,64},{128,96},{160,128},{192,160},{224,1... | collective-permute-start | bytes 221192 | tf_op jit(solution)/shard_map/ppermute | solution.py:21
  52.7 18.1 %copy-start.21 = (bf16[2,16,1152]{2,1,0:T(8,128)(2,1)}, bf16[2,16,1152]{2,1,0:T(8,128)(2,1)S(1)}, u32[]{:S(2)}) copy-start(bf16[2,16,1152]{2,1,0:T(8,128)(2,1)S(1)} %collective-permute-done.3.refs_8_) | copy-start | bytes 221188
  52.7 6.5 %collective-permute-start.4 = (bf16[2,16,1152]{2,1,0:T(8,128)(2,1)S(1)}, bf16[2,16,1152]{2,1,0:T(8,128)(2,1)S(1)}, u32[]{:S(2)}, u32[]{:S(2)}) collective-permute-start(bf16[2,16,1152]{2,1,0:T(8,128)(2,1)S(1)} %collective-permute-done.3.refs_8_), channel_id=1, source_target_pairs={{0,32},{32,64},{64,96},{96,128},{128,160},{160,192},{192,224},{224... | collective-permute-start | bytes 221192 | tf_op jit(solution)/shard_map/ppermute | solution.py:21
  52.7 18.1 %copy-start.22 = (bf16[2,16,1152]{2,1,0:T(8,128)(2,1)}, bf16[2,16,1152]{2,1,0:T(8,128)(2,1)S(1)}, u32[]{:S(2)}) copy-start(bf16[2,16,1152]{2,1,0:T(8,128)(2,1)S(1)} %collective-permute-done.refs_1_) | copy-start | bytes 221188
  52.7 6.5 %collective-permute-start.1 = (bf16[2,16,1152]{2,1,0:T(8,128)(2,1)S(1)}, bf16[2,16,1152]{2,1,0:T(8,128)(2,1)S(1)}, u32[]{:S(2)}, u32[]{:S(2)}) collective-permute-start(bf16[2,16,1152]{2,1,0:T(8,128)(2,1)S(1)} %collective-permute-done.refs_1_), channel_id=1, source_target_pairs={{0,224},{32,0},{64,32},{96,64},{128,96},{160,128},{192,160},{224,1... | collective-permute-start | bytes 221192 | tf_op jit(solution)/shard_map/ppermute | solution.py:21
  59.2 11.6 %copy-start.23 = (bf16[2,16,1152]{2,1,0:T(8,128)(2,1)}, bf16[2,16,1152]{2,1,0:T(8,128)(2,1)S(1)}, u32[]{:S(2)}) copy-start(bf16[2,16,1152]{2,1,0:T(8,128)(2,1)S(1)} %collective-permute-done.4.refs_7_) | copy-start | bytes 221188
  59.2 6.4 %collective-permute-start.5 = (bf16[2,16,1152]{2,1,0:T(8,128)(2,1)S(1)}, bf16[2,16,1152]{2,1,0:T(8,128)(2,1)S(1)}, u32[]{:S(2)}, u32[]{:S(2)}) collective-permute-start(bf16[2,16,1152]{2,1,0:T(8,128)(2,1)S(1)} %collective-permute-done.4.refs_7_), channel_id=1, source_target_pairs={{0,32},{32,64},{64,96},{96,128},{128,160},{160,192},{192,224},{224... | collective-permute-start | bytes 221192 | tf_op jit(solution)/shard_map/ppermute | solution.py:21
  59.2 11.6 %copy-start.24 = (bf16[2,16,1152]{2,1,0:T(8,128)(2,1)}, bf16[2,16,1152]{2,1,0:T(8,128)(2,1)S(1)}, u32[]{:S(2)}) copy-start(bf16[2,16,1152]{2,1,0:T(8,128)(2,1)S(1)} %collective-permute-done.1.refs_2_) | copy-start | bytes 221188
  59.2 6.4 %collective-permute-start.2 = (bf16[2,16,1152]{2,1,0:T(8,128)(2,1)S(1)}, bf16[2,16,1152]{2,1,0:T(8,128)(2,1)S(1)}, u32[]{:S(2)}, u32[]{:S(2)}) collective-permute-start(bf16[2,16,1152]{2,1,0:T(8,128)(2,1)S(1)} %collective-permute-done.1.refs_2_), channel_id=1, source_target_pairs={{0,224},{32,0},{64,32},{96,64},{128,96},{160,128},{192,160},{224,1... | collective-permute-start | bytes 221192 | tf_op jit(solution)/shard_map/ppermute | solution.py:21
  65.5 5.2 %copy-start.19 = (bf16[2,16,1152]{2,1,0:T(8,128)(2,1)}, bf16[2,16,1152]{2,1,0:T(8,128)(2,1)S(1)}, u32[]{:S(2)}) copy-start(bf16[2,16,1152]{2,1,0:T(8,128)(2,1)S(1)} %collective-permute-done.5.refs_6_) | copy-start | bytes 221188
  65.5 5.2 %collective-permute-start.6 = (bf16[1,16,1152]{2,1,0:T(8,128)(2,1)S(1)}, bf16[1,16,1152]{2,1,0:T(8,128)(2,1)S(1)}, u32[]{:S(2)}, u32[]{:S(2)}) collective-permute-start(bf16[1,16,1152]{2,1,0:T(8,128)(2,1)S(1)} %slice.70), channel_id=1, source_target_pairs={{0,32},{32,64},{64,96},{96,128},{128,160},{160,192},{192,224},{224... | collective-permute-start | bytes 110600 | tf_op jit(solution)/shard_map/ppermute | solution.py:21
  65.6 5.2 %copy-start.20 = (bf16[2,16,1152]{2,1,0:T(8,128)(2,1)}, bf16[2,16,1152]{2,1,0:T(8,128)(2,1)S(1)}, u32[]{:S(2)}) copy-start(bf16[2,16,1152]{2,1,0:T(8,128)(2,1)S(1)} %collective-permute-done.2.refs_3_) | copy-start | bytes 221188
  65.6 5.1 %collective-permute-start.7 = (bf16[1,16,1152]{2,1,0:T(8,128)(2,1)S(1)}, bf16[1,16,1152]{2,1,0:T(8,128)(2,1)S(1)}, u32[]{:S(2)}, u32[]{:S(2)}) collective-permute-start(bf16[1,16,1152]{2,1,0:T(8,128)(2,1)S(1)} %slice.71), channel_id=1, source_target_pairs={{0,224},{32,0},{64,32},{96,64},{128,96},{160,128},{192,160},{224,1... | collective-permute-start | bytes 110600 | tf_op jit(solution)/shard_map/ppermute | solution.py:21
  70.7 0.6 copy-start.25
  71.3 0.6 copy-start.26
  78.1 36.0 %copy-start.28 = (s32[64]{0:T(128)S(1)}, s32[64]{0:T(128)}, u32[]{:S(2)}) copy-start(s32[64]{0:T(128)} %param.11) | copy-start | bytes 772
  105.1 1.1 copy-start.4
  106.4 38.6 %copy-start.5 = (bf16[8,80,1024]{2,1,0:T(8,128)(2,1)}, bf16[8,80,1024]{2,1,0:T(8,128)(2,1)S(1)}, u32[]{:S(2)}) copy-start(bf16[8,80,1024]{2,1,0:T(8,128)(2,1)S(1)} %slice.75) | copy-start | bytes 3932164
  106.4 29.9 %collective-permute-start.9 = (bf16[640,1024]{1,0:T(8,128)(2,1)S(1)}, bf16[640,1024]{1,0:T(8,128)(2,1)}, u32[]{:S(2)}, u32[]{:S(2)}) collective-permute-start(bf16[640,1024]{1,0:T(8,128)(2,1)S(1)} %bitcast.118), channel_id=1, source_target_pairs={{0,3},{1,0},{2,1},{3,2},{4,7},{5,4},{6,5},{7,6},{8,11},{9,8},{10,9... | collective-permute-start | bytes 3932168 | tf_op jit(solution)/shard_map/ppermute | solution.py:221
  109.2 30.3 %collective-permute-start.8 = (bf16[640,1024]{1,0:T(8,128)(2,1)S(1)}, bf16[640,1024]{1,0:T(8,128)(2,1)}, u32[]{:S(2)}, u32[]{:S(2)}) collective-permute-start(bf16[640,1024]{1,0:T(8,128)(2,1)S(1)} %bitcast.119), channel_id=1, source_target_pairs={{0,1},{1,2},{2,3},{3,0},{4,5},{5,6},{6,7},{7,4},{8,9},{9,10},{10,1... | collective-permute-start | bytes 3932168 | tf_op jit(solution)/shard_map/ppermute | solution.py:220
  109.2 35.8 %all-to-all-start.4 = ((bf16[8,128,384]{2,1,0:T(8,128)(2,1)}), bf16[8,128,384]{2,1,0:T(8,128)(2,1)S(1)}, u32[]{:S(2)}, u32[]{:S(2)}) async-start(bf16[8,128,384]{2,1,0:T(8,128)(2,1)} %bitcast.24), calls=%async_computation.4 | async-start | bytes 1572864 | tf_op jit(solution)/shard_map/all_to_all | solution.py:17
  145.0 0.9 copy-start.7
  145.9 43.3 %all-to-all-start.3 = ((bf16[8,4,128,384]{3,2,1,0:T(8,128)(2,1)}), bf16[8,4,128,384]{3,2,1,0:T(8,128)(2,1)S(1)}, u32[]{:S(2)}, u32[]{:S(2)}) async-start(bf16[8,4,128,384]{3,2,1,0:T(8,128)(2,1)} %bitcast.114), calls=%async_computation.3 | async-start | bytes 6291456 | tf_op jit(solution)/shard_map/all_to_all | solution.py:17
  151.7 20.4 %copy-start.6 = (bf16[8,80,1024]{2,1,0:T(8,128)(2,1)S(1)}, bf16[8,80,1024]{2,1,0:T(8,128)(2,1)}, u32[]{:S(2)}) copy-start(bf16[8,80,1024]{2,1,0:T(8,128)(2,1)} %copy-done.5) | copy-start | bytes 3932164
  154.1 17.9 %collective-permute-start.10 = (bf16[320,1024]{1,0:T(8,128)(2,1)S(1)}, bf16[320,1024]{1,0:T(8,128)(2,1)S(1)}, u32[]{:S(2)}, u32[]{:S(2)}) collective-permute-start(bf16[320,1024]{1,0:T(8,128)(2,1)S(1)} %slice.51), channel_id=1, source_target_pairs={{0,1},{1,2},{2,3},{3,0},{4,5},{5,6},{6,7},{7,4},{8,9},{9,10},{10,1... | collective-permute-start | bytes 1966088 | tf_op jit(solution)/shard_map/ppermute | solution.py:224
  154.3 17.6 %collective-permute-start.11 = (bf16[320,1024]{1,0:T(8,128)(2,1)S(1)}, bf16[320,1024]{1,0:T(8,128)(2,1)S(1)}, u32[]{:S(2)}, u32[]{:S(2)}) collective-permute-start(bf16[320,1024]{1,0:T(8,128)(2,1)S(1)} %slice.52), channel_id=1, source_target_pairs={{0,3},{1,0},{2,1},{3,2},{4,7},{5,4},{6,5},{7,6},{8,11},{9,8},{10,9... | collective-permute-start | bytes 1966088 | tf_op jit(solution)/shard_map/ppermute | solution.py:225
  189.3 1.7 copy-start.2
  190.9 42.9 %all-to-all-start.5 = ((bf16[8,4,128,384]{3,2,1,0:T(8,128)(2,1)}), bf16[8,4,128,384]{3,2,1,0:T(8,128)(2,1)}, u32[]{:S(2)}, u32[]{:S(2)}) async-start(bf16[8,4,128,384]{3,2,1,0:T(8,128)(2,1)} %bitcast.113), calls=%async_computation.5 | async-start | bytes 6291456 | tf_op jit(solution)/shard_map/all_to_all | solution.py:17
  196.1 6.4 %copy-start.8 = (bf16[8,128,384]{2,1,0:T(8,128)(2,1)S(1)}, bf16[8,128,384]{2,1,0:T(8,128)(2,1)}, u32[]{:S(2)}) copy-start(bf16[8,128,384]{2,1,0:T(8,128)(2,1)} %copy-done.7) | copy-start | bytes 2359300
  196.1 94.1 %all-gather.9.cloned.1.call-start = ((), (), s32[]{:S(2)}) async-start(), calls=%async_computation.12 | async-start | bytes 4423680 | tf_op jit(solution)/shard_map/all_gather | solution.py:264
  198.9 7.0 %copy-start.3 = (bf16[8,4,128,384]{3,2,1,0:T(8,128)(2,1)S(1)}, bf16[8,4,128,384]{3,2,1,0:T(8,128)(2,1)}, u32[]{:S(2)}) copy-start(bf16[8,4,128,384]{3,2,1,0:T(8,128)(2,1)} %copy-done.2) | copy-start | bytes 9437188
  202.6 31.2 %collective-permute-start.13 = (bf16[8,128,384]{2,1,0:T(8,128)(2,1)S(1)}, bf16[8,128,384]{2,1,0:T(8,128)(2,1)}, u32[]{:S(2)}, u32[]{:S(2)}) collective-permute-start(bf16[8,128,384]{2,1,0:T(8,128)(2,1)S(1)} %copy-done.8), channel_id=1, source_target_pairs={{0,224},{32,0},{64,32},{96,64},{128,96},{160,128},{192,160},{224,1... | collective-permute-start | bytes 2359304 | tf_op jit(solution)/shard_map/ppermute | solution.py:21
  205.1 28.7 %collective-permute-start.12 = (bf16[8,128,384]{2,1,0:T(8,128)(2,1)S(1)}, bf16[8,128,384]{2,1,0:T(8,128)(2,1)}, u32[]{:S(2)}, u32[]{:S(2)}) collective-permute-start(bf16[8,128,384]{2,1,0:T(8,128)(2,1)S(1)} %copy-done.8), channel_id=1, source_target_pairs={{0,32},{32,64},{64,96},{96,128},{128,160},{160,192},{192,224},{224... | collective-permute-start | bytes 2359304 | tf_op jit(solution)/shard_map/ppermute | solution.py:21
  206.4 1.7 copy-start.9
  233.8 18.8 %collective-permute-start.15 = (bf16[8,128,384]{2,1,0:T(8,128)(2,1)}, bf16[8,128,384]{2,1,0:T(8,128)(2,1)S(1)}, u32[]{:S(2)}, u32[]{:S(2)}) collective-permute-start(bf16[8,128,384]{2,1,0:T(8,128)(2,1)} %collective-permute-done.13.refs_1_), channel_id=1, source_target_pairs={{0,224},{32,0},{64,32},{96,64},{128,96},{160,128},{192,160},{224,1... | collective-permute-start | bytes 2359304 | tf_op jit(solution)/shard_map/ppermute | solution.py:21
  236.3 19.4 %collective-permute-start.14 = (bf16[8,128,384]{2,1,0:T(8,128)(2,1)}, bf16[8,128,384]{2,1,0:T(8,128)(2,1)}, u32[]{:S(2)}, u32[]{:S(2)}) collective-permute-start(bf16[8,128,384]{2,1,0:T(8,128)(2,1)} %collective-permute-done.12.refs_8_), channel_id=1, source_target_pairs={{0,32},{32,64},{64,96},{96,128},{128,160},{160,192},{192,224},{224... | collective-permute-start | bytes 2359304 | tf_op jit(solution)/shard_map/ppermute | solution.py:21
  236.6 4.2 %copy-start.29 = (f32[640,384]{1,0:T(8,128)S(1)}, f32[640,384]{1,0:T(8,128)}, u32[]{:S(2)}) copy-start(f32[640,384]{1,0:T(8,128)} %convolution_bitcast_fusion.1) | copy-start | bytes 2949124
  239.1 1.7 copy-start.10
  252.6 3.1 copy-start.14
  255.7 76.3 %reduce-scatter.2.cloned.1.call-start = ((), (), s32[]{:S(2)}) async-start(), calls=%async_computation.11 | async-start | bytes 2621440 | tf_op jit(solution)/shard_map/reduce_scatter | solution.py:275
  255.8 17.4 %collective-permute-start.16 = (bf16[8,128,384]{2,1,0:T(8,128)(2,1)}, bf16[8,128,384]{2,1,0:T(8,128)(2,1)S(1)}, u32[]{:S(2)}, u32[]{:S(2)}) collective-permute-start(bf16[8,128,384]{2,1,0:T(8,128)(2,1)} %copy-done.14), channel_id=1, source_target_pairs={{0,224},{32,0},{64,32},{96,64},{128,96},{160,128},{192,160},{224,1... | collective-permute-start | bytes 2359304 | tf_op jit(solution)/shard_map/ppermute | solution.py:21
  256.8 18.9 %collective-permute-start.17 = (bf16[8,128,384]{2,1,0:T(8,128)(2,1)}, bf16[8,128,384]{2,1,0:T(8,128)(2,1)S(1)}, u32[]{:S(2)}, u32[]{:S(2)}) collective-permute-start(bf16[8,128,384]{2,1,0:T(8,128)(2,1)} %collective-permute-done.14.refs_7_), channel_id=1, source_target_pairs={{0,32},{32,64},{64,96},{96,128},{128,160},{160,192},{192,224},{224... | collective-permute-start | bytes 2359304 | tf_op jit(solution)/shard_map/ppermute | solution.py:21
  273.1 11.7 %copy-start.12 = (bf16[8,128,384]{2,1,0:T(8,128)(2,1)}, bf16[8,128,384]{2,1,0:T(8,128)(2,1)S(1)}, u32[]{:S(2)}) copy-start(bf16[8,128,384]{2,1,0:T(8,128)(2,1)S(1)} %collective-permute-done.16.refs_3_) | copy-start | bytes 2359300
  273.2 8.3 %collective-permute-start.19 = (bf16[4,128,384]{2,1,0:T(8,128)(2,1)S(1)}, bf16[4,128,384]{2,1,0:T(8,128)(2,1)S(1)}, u32[]{:S(2)}, u32[]{:S(2)}) collective-permute-start(bf16[4,128,384]{2,1,0:T(8,128)(2,1)S(1)} %slice.82), channel_id=1, source_target_pairs={{0,224},{32,0},{64,32},{96,64},{128,96},{160,128},{192,160},{224,1... | collective-permute-start | bytes 1179656 | tf_op jit(solution)/shard_map/ppermute | solution.py:21
  275.7 9.2 %copy-start.13 = (bf16[8,128,384]{2,1,0:T(8,128)(2,1)}, bf16[8,128,384]{2,1,0:T(8,128)(2,1)S(1)}, u32[]{:S(2)}) copy-start(bf16[8,128,384]{2,1,0:T(8,128)(2,1)S(1)} %collective-permute-done.17.refs_6_) | copy-start | bytes 2359300
  275.7 9.1 %collective-permute-start.18 = (bf16[4,128,384]{2,1,0:T(8,128)(2,1)S(1)}, bf16[4,128,384]{2,1,0:T(8,128)(2,1)S(1)}, u32[]{:S(2)}, u32[]{:S(2)}) collective-permute-start(bf16[4,128,384]{2,1,0:T(8,128)(2,1)S(1)} %slice.81), channel_id=1, source_target_pairs={{0,32},{32,64},{64,96},{96,128},{128,160},{160,192},{192,224},{224... | collective-permute-start | bytes 1179656 | tf_op jit(solution)/shard_map/ppermute | solution.py:21
  281.5 3.4 copy-start.16
  284.9 0.8 copy-start.17
  300.2 44.8 %all-to-all-start.6 = ((bf16[8,4,128,384]{3,2,1,0:T(8,128)(2,1)}), bf16[8,4,128,384]{3,2,1,0:T(8,128)(2,1)S(1)}, u32[]{:S(2)}, u32[]{:S(2)}) async-start(bf16[8,4,128,384]{3,2,1,0:T(8,128)(2,1)} %bitcast.116), calls=%async_computation.6 | async-start | bytes 6291456 | tf_op jit(solution)/shard_map/all_to_all | solution.py:17
  345.0 25.2 %all-to-all-start.7 = ((bf16[64,32,128]{2,1,0:T(8,128)(2,1)}), bf16[64,32,128]{2,1,0:T(8,128)(2,1)}, u32[]{:S(2)}, u32[]{:S(2)}) async-start(bf16[64,32,128]{2,1,0:T(8,128)(2,1)} %bitcast.130), calls=%async_computation.8 | async-start | bytes 1048576 | tf_op jit(solution)/shard_map/all_to_all | solution.py:17
  352.6 19.5 %copy-start.1 = (bf16[2,16,4096]{2,1,0:T(8,128)(2,1)S(1)}, bf16[2,16,4096]{2,1,0:T(8,128)(2,1)}, u32[]{:S(2)}) copy-start(bf16[2,16,4096]{2,1,0:T(8,128)(2,1)} %param.8) | copy-start | bytes 786436
Sparse Core Ops, SparseCore 0:
  27.4 80.4 all-gather.4
  109.6 73.0 all-gather.6
  255.8 31.9 all-gather.8
  300.3 31.6 reduce-scatter.1

commit v2 on v1

--- a/solution.py
+++ b/solution.py
@@ -224,11 +224,12 @@
         lax.ppermute(from_last[:half], "y", to_next),
         lax.ppermute(from_next[half:], "y", to_last),
     ]
+    far, block_down = lax.optimization_barrier((far, block_down))
     inputs = take_rows(
         jnp.stack([quarters, from_next, jnp.concatenate(far, axis=0), from_last]),
         (jnp.arange(Y, dtype=jnp.int32) - quarter + Y) % Y,
     )
-    up_all, inputs, block_down = lax.optimization_barrier((up_all, inputs, block_down))
+    up_all, inputs = lax.optimization_barrier((up_all, inputs))
     routes = received[:, capacity:].reshape(PLANE, line_tokens, -1)
     placing = place(routes, jnp.arange(PLANE, dtype=jnp.int32))
     weights = sum(
@@ -245,11 +246,13 @@
     by_part = (part_count, piece_rows, width)
     serve_gate = assemble(exchange(take_rows(gate_all, chosen_slot), XC))
     arrived_up = exchange(take_rows(up_all, chosen_slot), XC)
+    down_ring = Ring(block_down).hop()
+    inputs = down_ring.hold(inputs)
     gate_act = jnp.einsum(
         "ymd,ydf->mf", inputs, serve_gate.reshape(by_part), preferred_element_type=jnp.float32
     )
     arrived_up, gate_act = lax.optimization_barrier((arrived_up, gate_act))
-    down_ring = Ring(block_down).hop()
+    down_ring.hop()
     arrived_up = down_ring.hold(arrived_up)
     down_ring.hop()
     serve_up = assemble(arrived_up)
@@ -258,8 +261,7 @@
     )
     hidden = (jax.nn.silu(gate_act) * up_act * row_weight.reshape(-1, 1)).astype(jnp.bfloat16)
 
-    hidden = down_ring.hold(hidden)
-    down_ring.hop().hop()
+    down_ring.hop()
 
     plane_hidden = lax.all_gather(hidden, XC, axis=0, tiled=False).reshape(
         PLANE, PLANE, capacity, width

time: 380 us -> 377 us (level)
  waiting for transfers between devices: 167 us -> 159 us
    all_to_all x6, waiting for transfers between devices: 57.5 us -> 36.6 us  [exchange(): return lax.all_to_all(value, axes, split_axis=0, concat_axis=0, tiled=True)]
    ppermute x16, waiting for transfers between devices: 45.2 us -> 56.9 us  [shift(): return lax.ppermute(value, 'z', [(i, (i + step) % Z) for i in range(Z)])]
    unnamed x63 -> x67, local copies, waits for them, and re-layouts: 11.5 us -> 11.5 us
  transfers between devices with their start and end apart: 30 -> 30, of which waited for: 19 -> 19; matrix products, arithmetic and copies ran while one was open for 16% -> 14% of each run, Pallas kernels for 2% -> 2%
where the time goes in v2:
time: 377 us; the launch traced here: 376 us
  waiting for transfers between devices  159 us (42%)
  starting transfers between devices  67.9 us (18%)
  local copies, waits for them, and re-layouts  49.3 us (13%)
  blocking collectives  43.1 us (11%)
  matrix products  22.1 us (6%)
  between operations  14.3 us (4%)
  other arithmetic  12.5 us (3%)
  Pallas kernels  7.03 us (2%)
    ppermute x16, waiting for transfers between devices, shift(): return lax.ppermute(value, 'z', [(i, (i + step) % Z) for i in range(Z)])  56.9 us
    all_to_all x2, blocking collectives, exchange(): return lax.all_to_all(value, axes, split_axis=0, concat_axis=0, tiled=True)  43.1 us
    all_to_all x6, starting transfers between devices, exchange(): return lax.all_to_all(value, axes, split_axis=0, concat_axis=0, tiled=True)  38.3 us
    all_to_all x6, waiting for transfers between devices, exchange(): return lax.all_to_all(value, axes, split_axis=0, concat_axis=0, tiled=True)  36.6 us
    reduce_scatter x1, waiting for transfers between devices, body(): lax.psum_scatter(plane_out.reshape(-1, block_rows), 'y', scatter_dimensio...  26 us
    ppermute x16, starting transfers between devices, shift(): return lax.ppermute(value, 'z', [(i, (i + step) % Z) for i in range(Z)])  23.8 us
    ppermute x1, waiting for transfers between devices, body(): from_next = lax.ppermute(quarters, 'y', to_last)  21.2 us
    gather x6, local copies, waits for them, and re-layouts, take_rows(): return value.at[index].get(mode='promise_in_bounds')  18.6 us
  transfers between devices with their start and end apart: 30, of which 19 were waited for; matrix products, arithmetic and copies ran while one was open for 14% of the time, Pallas kernels for 2%

profile of v2, /device:TPU:1, one launch (start us, length us, event | category | flops | bytes accessed | tf_op | source)
XLA Modules:
  0.0 375.6 jit_solution(12692688477248219461)
XLA Ops:
  7.2 6.8 %all-to-all-start = ((bf16[8,128,384]{2,1,0:T(8,128)(2,1)}), bf16[8,128,384]{2,1,0:T(8,128)(2,1)S(1)}, u32[]{:S(2)}, u32[]{:S(2)}) async-start(bf16[8,128,384]{2,1,0:T(8,128)(2,1)} %bitcast.133), calls=%async_computation | async-start | bytes 1572864 | tf_op jit(solution)/shard_map/all_to_all | solution.py:17
  16.1 10.2 %all-to-all-done = bf16[8,128,384]{2,1,0:T(8,128)(2,1)S(1)} async-done(((bf16[8,128,384]{2,1,0:T(8,128)(2,1)}), bf16[8,128,384]{2,1,0:T(8,128)(2,1)S(1)}, u32[]{:S(2)}, u32[]{:S(2)}) %all-to-all-start) | async-done | bytes 786464 | tf_op jit(solution)/shard_map/all_to_all | solution.py:17
  26.3 0.9 copy-done.10
  27.3 16.2 %all_to_all.40 = bf16[8,128,384]{2,1,0:T(8,128)(2,1)} all-to-all(bf16[8,128,384]{2,1,0:T(8,128)(2,1)S(1)} %bitcast.134), channel_id=1, replica_groups=mesh['z'=8,'x'=4,'c'=2,'y'=4] {'x','c'}, dimensions={0} | all-to-all | bytes 1572864 | tf_op jit(solution)/shard_map/all_to_all | solution.py:17
  44.6 4.0 %collective-permute-start = (bf16[2,16,1152]{2,1,0:T(8,128)(2,1)S(1)}, bf16[2,16,1152]{2,1,0:T(8,128)(2,1)S(1)}, u32[]{:S(2)}, u32[]{:S(2)}) collective-permute-start(bf16[2,16,1152]{2,1,0:T(8,128)(2,1)S(1)} %bitcast.137), channel_id=1, source_target_pairs={{0,224},{32,0},{64,32},{96,64},{128,96},{160,128},{192,160},{224,1... | collective-permute-start | bytes 221192 | tf_op jit(solution)/shard_map/ppermute | solution.py:21
  48.7 3.9 %collective-permute-done.3.refs_8_ = bf16[2,16,1152]{2,1,0:T(8,128)(2,1)S(1)} collective-permute-done((bf16[2,16,1152]{2,1,0:T(8,128)(2,1)S(1)}, bf16[2,16,1152]{2,1,0:T(8,128)(2,1)S(1)}, u32[]{:S(2)}, u32[]{:S(2)}) %collective-permute-start.3) | collective-permute-done | bytes 73760 | tf_op jit(solution)/shard_map/ppermute | solution.py:21
  52.7 2.7 collective-permute-start.1
  55.4 3.7 collective-permute-done.4.refs_7_
  59.2 2.7 collective-permute-start.2
  61.9 3.7 collective-permute-done.5.refs_6_
  65.6 2.7 collective-permute-start.7
  69.2 1.5 collective-permute-done.6.refs_4_
  71.9 2.7 pick_pieces.2
  74.6 0.9 slice_bitcast_fusion.4
  76.4 1.6 convolution_convert_fusion
  78.1 27.0 %all_to_all.41 = bf16[8,96,1024]{2,1,0:T(8,128)(2,1)S(1)} all-to-all(bf16[8,96,1024]{2,1,0:T(8,128)(2,1)S(1)} %pad_maximum_fusion.1), channel_id=1, replica_groups=mesh['z'=8,'x'=4,'c'=2,'y'=4] {'x','c'}, dimensions={0} | all-to-all | bytes 3145728 | tf_op jit(solution)/shard_map/all_to_all | solution.py:17
  105.1 1.1 copy-done.3
  106.4 2.8 collective-permute-start.9
  109.2 4.7 %all-to-all-start.4 = ((bf16[8,128,384]{2,1,0:T(8,128)(2,1)}), bf16[8,128,384]{2,1,0:T(8,128)(2,1)S(1)}, u32[]{:S(2)}, u32[]{:S(2)}) async-start(bf16[8,128,384]{2,1,0:T(8,128)(2,1)} %bitcast.21), calls=%async_computation.4 | async-start | bytes 1572864 | tf_op jit(solution)/shard_map/all_to_all | solution.py:17
  115.1 21.2 %collective-permute-done.9 = bf16[640,1024]{1,0:T(8,128)(2,1)} collective-permute-done((bf16[640,1024]{1,0:T(8,128)(2,1)S(1)}, bf16[640,1024]{1,0:T(8,128)(2,1)}, u32[]{:S(2)}, u32[]{:S(2)}) %collective-permute-start.9) | collective-permute-done | bytes 1310752 | tf_op jit(solution)/shard_map/ppermute | solution.py:221
  136.3 3.2 collective-permute-done.8
  139.5 5.5 %gather_fusion.1 = bf16[32,128,384]{2,1,0:T(8,128)(2,1)} fusion(bf16[64,128,384]{2,1,0:T(8,128)(2,1)} %bitcast.132, s32[1024]{0:T(1024)S(1)} %pad_clamp_fusion.1), kind=kCustom, calls=%fused_computation.1 | custom fusion | bytes 6291584 | tf_op jit(solution)/shard_map/gather | solution.py:109
  145.0 0.9 copy-done.6
  145.9 5.7 %all-to-all-start.3 = ((bf16[8,4,128,384]{3,2,1,0:T(8,128)(2,1)}), bf16[8,4,128,384]{3,2,1,0:T(8,128)(2,1)S(1)}, u32[]{:S(2)}, u32[]{:S(2)}) async-start(bf16[8,4,128,384]{3,2,1,0:T(8,128)(2,1)} %bitcast.114), calls=%async_computation.3 | async-start | bytes 6291456 | tf_op jit(solution)/shard_map/all_to_all | solution.py:17
  151.7 1.2 slice.52
  152.9 1.1 slice.51
  154.3 2.7 collective-permute-start.11
  157.0 14.9 %collective-permute-done.10 = bf16[320,1024]{1,0:T(8,128)(2,1)S(1)} collective-permute-done((bf16[320,1024]{1,0:T(8,128)(2,1)S(1)}, bf16[320,1024]{1,0:T(8,128)(2,1)S(1)}, u32[]{:S(2)}, u32[]{:S(2)}) %collective-permute-start.10) | collective-permute-done | bytes 655392 | tf_op jit(solution)/shard_map/ppermute | solution.py:224
  172.0 4.6 %pad_maximum_fusion = bf16[4,640,1024]{2,1,0:T(8,128)(2,1)} fusion(bf16[1,640,1024]{2,1,0:T(8,128)(2,1)} %bitcast.23, bf16[1,640,1024]{2,1,0:T(8,128)(2,1)S(1)} %maximum_bitcast_fusion, bf16[1,640,1024]{2,1,0:T(8,128)(2,1)} %bitcast.20, bf16[1,640,1024]{2,1,0:T(8,128)(2,1)S(1)} %bitcast.120), kind=kLoop, calls=%fused_computation.5 | loop fusion | flops 7864320 | bytes 10485760 | tf_op jit(solution)/shard_map/stack | solution.py:229
  176.7 5.7 %gather_fusion.2 = bf16[4,640,1024]{2,1,0:T(8,128)(2,1)} fusion(bf16[4,640,1024]{2,1,0:T(8,128)(2,1)} %pad_maximum_fusion, s32[1024]{0:T(1024)S(1)} %pad_clamp_fusion), kind=kCustom, calls=%fused_computation.2 | custom fusion | bytes 10485776 | tf_op jit(solution)/shard_map/gather | solution.py:109
  182.7 5.4 %gather_fusion.3 = bf16[32,128,384]{2,1,0:T(8,128)(2,1)} fusion(bf16[64,128,384]{2,1,0:T(8,128)(2,1)} %bitcast.131, s32[1024]{0:T(1024)S(1)} %pad_clamp_fusion.1), kind=kCustom, calls=%fused_computation.3 | custom fusion | bytes 6291584 | tf_op jit(solution)/shard_map/gather | solution.py:109
  188.2 1.1 all-to-all-done.3
  189.3 1.7 copy-done.2
  190.9 5.2 %all-to-all-start.5 = ((bf16[8,4,128,384]{3,2,1,0:T(8,128)(2,1)}), bf16[8,4,128,384]{3,2,1,0:T(8,128)(2,1)}, u32[]{:S(2)}, u32[]{:S(2)}) async-start(bf16[8,4,128,384]{3,2,1,0:T(8,128)(2,1)} %bitcast.113), calls=%async_computation.5 | async-start | bytes 6291456 | tf_op jit(solution)/shard_map/all_to_all | solution.py:17
  197.3 1.0 slice.78
  199.7 2.5 collective-permute-start.13
  204.6 1.3 fusion.2
  205.9 13.1 %collective-permute-done.13.refs_1_ = bf16[8,128,384]{2,1,0:T(8,128)(2,1)S(1)} collective-permute-done((bf16[8,128,384]{2,1,0:T(8,128)(2,1)S(1)}, bf16[8,128,384]{2,1,0:T(8,128)(2,1)S(1)}, u32[]{:S(2)}, u32[]{:S(2)}) %collective-permute-start.13) | collective-permute-done | bytes 786464 | tf_op jit(solution)/shard_map/ppermute | solution.py:21
  219.0 3.2 collective-permute-done.12.refs_8_
  222.2 2.7 collective-permute-start.15
  225.2 2.4 copy.88
  227.6 1.7 copy-done.8
  229.2 6.3 %convolution_bitcast_fusion.1 = f32[640,384]{1,0:T(8,128)} fusion(bf16[4,640,1024]{2,1,0:T(8,128)(2,1)} %gather_fusion.2, bf16[4,1024,384]{2,1,0:T(8,128)(2,1)S(1)} %bitcast.121), kind=kOutput, calls=%fused_computation.22 | convolution fusion | flops 2013265920 | bytes 9371648 | tf_op jit(solution)/shard_map/ymd,ydf->mf/dot_general | solution.py:251
  235.5 5.7 %collective-permute-done.14.refs_7_ = bf16[8,128,384]{2,1,0:T(8,128)(2,1)S(1)} collective-permute-done((bf16[8,128,384]{2,1,0:T(8,128)(2,1)S(1)}, bf16[8,128,384]{2,1,0:T(8,128)(2,1)S(1)}, u32[]{:S(2)}, u32[]{:S(2)}) %collective-permute-start.14) | collective-permute-done | bytes 786464 | tf_op jit(solution)/shard_map/ppermute | solution.py:21
  241.2 2.7 copy.90
  244.0 1.7 copy-done.9
  245.6 6.3 %fusion.19 = bf16[640,384]{1,0:T(8,128)(2,1)} fusion(bf16[4,640,1024]{2,1,0:T(8,128)(2,1)} %gather_fusion.2, bf16[4,1024,384]{2,1,0:T(8,128)(2,1)S(1)} %bitcast.123, f32[640,384]{1,0:T(8,128)S(1)} %copy-done.31, f32[640]{0:T(1024)S(1)} %mul.54), kind=kOutput, calls=%fused_computation.24 | convolution fusion | flops 2014986240 | bytes 9865728 | tf_op jit(solution)/shard_map/ymd,ydf->mf/dot_general | solution.py:259
  252.0 2.3 collective-permute-start.16
  254.4 14.9 %collective-permute-done.16.refs_3_ = bf16[8,128,384]{2,1,0:T(8,128)(2,1)S(1)} collective-permute-done((bf16[8,128,384]{2,1,0:T(8,128)(2,1)}, bf16[8,128,384]{2,1,0:T(8,128)(2,1)S(1)}, u32[]{:S(2)}, u32[]{:S(2)}) %collective-permute-start.16) | collective-permute-done | bytes 786464 | tf_op jit(solution)/shard_map/ppermute | solution.py:21
  269.4 3.3 collective-permute-start.19
  272.8 1.2 gather_fusion.4
  274.0 3.8 %collective-permute-done.19.refs_5_ = bf16[4,128,384]{2,1,0:T(8,128)(2,1)S(1)} collective-permute-done((bf16[4,128,384]{2,1,0:T(8,128)(2,1)S(1)}, bf16[4,128,384]{2,1,0:T(8,128)(2,1)S(1)}, u32[]{:S(2)}, u32[]{:S(2)}) %collective-permute-start.19) | collective-permute-done | bytes 393248 | tf_op jit(solution)/shard_map/ppermute | solution.py:21
  277.8 3.4 collective-permute-done.18.refs_4_
  281.9 4.4 %pick_pieces.3 = bf16[32,128,384]{2,1,0:T(8,128)(2,1)} custom-call(s32[32]{0:T(128)} %gather_fusion.4, bf16[8,128,384]{2,1,0:T(8,128)(2,1)} %copy-done.6, bf16[8,128,384]{2,1,0:T(8,128)(2,1)} %copy-done.13, bf16[8,128,384]{2,1,0:T(8,128)(2,1)} %collective-permute-done.15.refs_2_, bf16[8,128,384]{2,1,0:T(8,128)(2,1)} %copy-done.11, ...), custom_call_target="tpu_custom_call" | custom-call | tf_op jit(solution)/shard_map/pick_pieces/pallas_call | solution.py:93
  286.3 7.5 %fusion.12 = bf16[4,8,256,128]{2,3,0,1:T(8,128)(2,1)S(1)} fusion(s32[8,8,256]{2,1,0:T(8,128)S(1)} %add_select_fusion, pred[8,8,256]{2,1,0:T(8,128)(4,1)S(1)} %fusion.29, bf16[8,8,80,384,1]{3,2,1,0,4:T(8,128)(2,1)} %bitcast.140, bf16[8,4,128,384]{3,2,1,0:T(8,128)(2,1)} %bitcast.115), kind=kOutput, calls=%fused_computation.16 | convolution fusion | flops 3361734656 | bytes 9256960 | tf_op jit(solution)/shard_map/lspt,slpyr->yltr/dot_general | solution.py:274
  293.8 2.4 copy.96
  296.2 7.9 %all-to-all-start.6 = ((bf16[8,4,128,384]{3,2,1,0:T(8,128)(2,1)}), bf16[8,4,128,384]{3,2,1,0:T(8,128)(2,1)S(1)}, u32[]{:S(2)}, u32[]{:S(2)}) async-start(bf16[8,4,128,384]{3,2,1,0:T(8,128)(2,1)} %bitcast.116), calls=%async_computation.6 | async-start | bytes 6291456 | tf_op jit(solution)/shard_map/all_to_all | solution.py:17
  304.1 26.0 %reduce-scatter.2.cloned.1.call-done = bf16[2048,128]{1,0:T(8,128)(2,1)} async-done(((bf16[8192,128]{1,0:T(8,128)(2,1)}), bf16[2048,128]{1,0:T(8,128)(2,1)}) %reduce-scatter.2.cloned.1.call-update) | async-done | bytes 524304 | tf_op jit(solution)/shard_map/reduce_scatter | solution.py:277
  330.1 1.9 copy.97
  332.0 9.7 %all-to-all-done.6 = bf16[8,4,128,384]{3,2,1,0:T(8,128)(2,1)S(1)} async-done(((bf16[8,4,128,384]{3,2,1,0:T(8,128)(2,1)}), bf16[8,4,128,384]{3,2,1,0:T(8,128)(2,1)S(1)}, u32[]{:S(2)}, u32[]{:S(2)}) %all-to-all-start.6) | async-done | bytes 3145760 | tf_op jit(solution)/shard_map/all_to_all | solution.py:17
  341.7 7.9 %all-to-all-start.7 = ((bf16[64,32,128]{2,1,0:T(8,128)(2,1)}), bf16[64,32,128]{2,1,0:T(8,128)(2,1)}, u32[]{:S(2)}, u32[]{:S(2)}) async-start(bf16[64,32,128]{2,1,0:T(8,128)(2,1)} %bitcast.130), calls=%async_computation.8 | async-start | bytes 1048576 | tf_op jit(solution)/shard_map/all_to_all | solution.py:17
  349.6 2.0 copy.91
  351.6 15.6 %all-to-all-done.7 = bf16[64,32,128]{2,1,0:T(8,128)(2,1)} async-done(((bf16[64,32,128]{2,1,0:T(8,128)(2,1)}), bf16[64,32,128]{2,1,0:T(8,128)(2,1)}, u32[]{:S(2)}, u32[]{:S(2)}) %all-to-all-start.7) | async-done | bytes 524320 | tf_op jit(solution)/shard_map/all_to_all | solution.py:17
  367.2 1.1 reduce_sum.112
  (153 shorter events, 15.6 us)
Async XLA Ops:
  7.2 8.9 %copy-start = (bf16[2,16,4096]{2,1,0:T(8,128)(2,1)S(1)}, bf16[2,16,4096]{2,1,0:T(8,128)(2,1)}, u32[]{:S(2)}) copy-start(bf16[2,16,4096]{2,1,0:T(8,128)(2,1)} %param.8) | copy-start | bytes 786436
  7.2 20.1 %copy-start.17 = (bf16[1,1024,384]{2,1,0:T(8,128)(2,1)S(1)}, bf16[1,1024,384]{2,1,0:T(8,128)(2,1)}, u32[]{:S(2)}) copy-start(bf16[1,1024,384]{2,1,0:T(8,128)(2,1)} %param.14) | copy-start | bytes 2359300
  7.2 36.3 %copy-start.29 = (s32[64]{0:T(128)S(1)}, s32[64]{0:T(128)}, u32[]{:S(2)}) copy-start(s32[64]{0:T(128)} %param.12) | copy-start | bytes 772
  7.2 19.1 %all-to-all-start = ((bf16[8,128,384]{2,1,0:T(8,128)(2,1)}), bf16[8,128,384]{2,1,0:T(8,128)(2,1)S(1)}, u32[]{:S(2)}, u32[]{:S(2)}) async-start(bf16[8,128,384]{2,1,0:T(8,128)(2,1)} %bitcast.133), calls=%async_computation | async-start | bytes 1572864 | tf_op jit(solution)/shard_map/all_to_all | solution.py:17
  14.0 125.5 %all-gather.5.cloned.1.call-start = ((), (), s32[]{:S(2)}) async-start(), calls=%async_computation.9 | async-start | bytes 7077888 | tf_op jit(solution)/shard_map/all_gather | solution.py:150
  26.3 0.9 copy-start.10
  27.2 155.5 %all-gather.7.cloned.1.call-start = ((), (), s32[]{:S(2)}) async-start(), calls=%async_computation.10 | async-start | bytes 7077888 | tf_op jit(solution)/shard_map/all_gather | solution.py:150
  43.8 26.9 %copy-start.20 = (bf16[32,1152]{1,0:T(8,128)(2,1)}, bf16[32,1152]{1,0:T(8,128)(2,1)S(1)}, u32[]{:S(2)}) copy-start(bf16[32,1152]{1,0:T(8,128)(2,1)S(1)} %pad.4) | copy-start | bytes 221188
  43.8 8.8 %collective-permute-start.3 = (bf16[2,16,1152]{2,1,0:T(8,128)(2,1)S(1)}, bf16[2,16,1152]{2,1,0:T(8,128)(2,1)S(1)}, u32[]{:S(2)}, u32[]{:S(2)}) collective-permute-start(bf16[2,16,1152]{2,1,0:T(8,128)(2,1)S(1)} %bitcast.136), channel_id=1, source_target_pairs={{0,32},{32,64},{64,96},{96,128},{128,160},{160,192},{192,224},{224... | collective-permute-start | bytes 221192 | tf_op jit(solution)/shard_map/ppermute | solution.py:21
  44.6 8.0 %collective-permute-start = (bf16[2,16,1152]{2,1,0:T(8,128)(2,1)S(1)}, bf16[2,16,1152]{2,1,0:T(8,128)(2,1)S(1)}, u32[]{:S(2)}, u32[]{:S(2)}) collective-permute-start(bf16[2,16,1152]{2,1,0:T(8,128)(2,1)S(1)} %bitcast.137), channel_id=1, source_target_pairs={{0,224},{32,0},{64,32},{96,64},{128,96},{160,128},{192,160},{224,1... | collective-permute-start | bytes 221192 | tf_op jit(solution)/shard_map/ppermute | solution.py:21
  52.7 18.1 %copy-start.23 = (bf16[2,16,1152]{2,1,0:T(8,128)(2,1)}, bf16[2,16,1152]{2,1,0:T(8,128)(2,1)S(1)}, u32[]{:S(2)}) copy-start(bf16[2,16,1152]{2,1,0:T(8,128)(2,1)S(1)} %collective-permute-done.3.refs_8_) | copy-start | bytes 221188
  52.7 6.5 %collective-permute-start.4 = (bf16[2,16,1152]{2,1,0:T(8,128)(2,1)S(1)}, bf16[2,16,1152]{2,1,0:T(8,128)(2,1)S(1)}, u32[]{:S(2)}, u32[]{:S(2)}) collective-permute-start(bf16[2,16,1152]{2,1,0:T(8,128)(2,1)S(1)} %collective-permute-done.3.refs_8_), channel_id=1, source_target_pairs={{0,32},{32,64},{64,96},{96,128},{128,160},{160,192},{192,224},{224... | collective-permute-start | bytes 221192 | tf_op jit(solution)/shard_map/ppermute | solution.py:21
  52.7 18.1 %copy-start.24 = (bf16[2,16,1152]{2,1,0:T(8,128)(2,1)}, bf16[2,16,1152]{2,1,0:T(8,128)(2,1)S(1)}, u32[]{:S(2)}) copy-start(bf16[2,16,1152]{2,1,0:T(8,128)(2,1)S(1)} %collective-permute-done.refs_1_) | copy-start | bytes 221188
  52.7 6.5 %collective-permute-start.1 = (bf16[2,16,1152]{2,1,0:T(8,128)(2,1)S(1)}, bf16[2,16,1152]{2,1,0:T(8,128)(2,1)S(1)}, u32[]{:S(2)}, u32[]{:S(2)}) collective-permute-start(bf16[2,16,1152]{2,1,0:T(8,128)(2,1)S(1)} %collective-permute-done.refs_1_), channel_id=1, source_target_pairs={{0,224},{32,0},{64,32},{96,64},{128,96},{160,128},{192,160},{224,1... | collective-permute-start | bytes 221192 | tf_op jit(solution)/shard_map/ppermute | solution.py:21
  59.2 11.6 %copy-start.25 = (bf16[2,16,1152]{2,1,0:T(8,128)(2,1)}, bf16[2,16,1152]{2,1,0:T(8,128)(2,1)S(1)}, u32[]{:S(2)}) copy-start(bf16[2,16,1152]{2,1,0:T(8,128)(2,1)S(1)} %collective-permute-done.4.refs_7_) | copy-start | bytes 221188
  59.2 6.4 %collective-permute-start.5 = (bf16[2,16,1152]{2,1,0:T(8,128)(2,1)S(1)}, bf16[2,16,1152]{2,1,0:T(8,128)(2,1)S(1)}, u32[]{:S(2)}, u32[]{:S(2)}) collective-permute-start(bf16[2,16,1152]{2,1,0:T(8,128)(2,1)S(1)} %collective-permute-done.4.refs_7_), channel_id=1, source_target_pairs={{0,32},{32,64},{64,96},{96,128},{128,160},{160,192},{192,224},{224... | collective-permute-start | bytes 221192 | tf_op jit(solution)/shard_map/ppermute | solution.py:21
  59.2 11.6 %copy-start.26 = (bf16[2,16,1152]{2,1,0:T(8,128)(2,1)}, bf16[2,16,1152]{2,1,0:T(8,128)(2,1)S(1)}, u32[]{:S(2)}) copy-start(bf16[2,16,1152]{2,1,0:T(8,128)(2,1)S(1)} %collective-permute-done.1.refs_2_) | copy-start | bytes 221188
  59.2 6.4 %collective-permute-start.2 = (bf16[2,16,1152]{2,1,0:T(8,128)(2,1)S(1)}, bf16[2,16,1152]{2,1,0:T(8,128)(2,1)S(1)}, u32[]{:S(2)}, u32[]{:S(2)}) collective-permute-start(bf16[2,16,1152]{2,1,0:T(8,128)(2,1)S(1)} %collective-permute-done.1.refs_2_), channel_id=1, source_target_pairs={{0,224},{32,0},{64,32},{96,64},{128,96},{160,128},{192,160},{224,1... | collective-permute-start | bytes 221192 | tf_op jit(solution)/shard_map/ppermute | solution.py:21
  65.5 5.2 %copy-start.21 = (bf16[2,16,1152]{2,1,0:T(8,128)(2,1)}, bf16[2,16,1152]{2,1,0:T(8,128)(2,1)S(1)}, u32[]{:S(2)}) copy-start(bf16[2,16,1152]{2,1,0:T(8,128)(2,1)S(1)} %collective-permute-done.5.refs_6_) | copy-start | bytes 221188
  65.5 5.2 %collective-permute-start.6 = (bf16[1,16,1152]{2,1,0:T(8,128)(2,1)S(1)}, bf16[1,16,1152]{2,1,0:T(8,128)(2,1)S(1)}, u32[]{:S(2)}, u32[]{:S(2)}) collective-permute-start(bf16[1,16,1152]{2,1,0:T(8,128)(2,1)S(1)} %slice.70), channel_id=1, source_target_pairs={{0,32},{32,64},{64,96},{96,128},{128,160},{160,192},{192,224},{224... | collective-permute-start | bytes 110600 | tf_op jit(solution)/shard_map/ppermute | solution.py:21
  65.6 5.2 %copy-start.22 = (bf16[2,16,1152]{2,1,0:T(8,128)(2,1)}, bf16[2,16,1152]{2,1,0:T(8,128)(2,1)S(1)}, u32[]{:S(2)}) copy-start(bf16[2,16,1152]{2,1,0:T(8,128)(2,1)S(1)} %collective-permute-done.2.refs_3_) | copy-start | bytes 221188
  65.6 5.1 %collective-permute-start.7 = (bf16[1,16,1152]{2,1,0:T(8,128)(2,1)S(1)}, bf16[1,16,1152]{2,1,0:T(8,128)(2,1)S(1)}, u32[]{:S(2)}, u32[]{:S(2)}) collective-permute-start(bf16[1,16,1152]{2,1,0:T(8,128)(2,1)S(1)} %slice.71), channel_id=1, source_target_pairs={{0,224},{32,0},{64,32},{96,64},{128,96},{160,128},{192,160},{224,1... | collective-permute-start | bytes 110600 | tf_op jit(solution)/shard_map/ppermute | solution.py:21
  70.7 0.6 copy-start.27
  71.3 0.6 copy-start.28
  78.1 36.0 %copy-start.30 = (s32[64]{0:T(128)S(1)}, s32[64]{0:T(128)}, u32[]{:S(2)}) copy-start(s32[64]{0:T(128)} %param.11) | copy-start | bytes 772
  105.1 1.1 copy-start.3
  106.4 38.6 %copy-start.4 = (bf16[8,80,1024]{2,1,0:T(8,128)(2,1)}, bf16[8,80,1024]{2,1,0:T(8,128)(2,1)S(1)}, u32[]{:S(2)}) copy-start(bf16[8,80,1024]{2,1,0:T(8,128)(2,1)S(1)} %slice.75) | copy-start | bytes 3932164
  106.4 29.9 %collective-permute-start.9 = (bf16[640,1024]{1,0:T(8,128)(2,1)S(1)}, bf16[640,1024]{1,0:T(8,128)(2,1)}, u32[]{:S(2)}, u32[]{:S(2)}) collective-permute-start(bf16[640,1024]{1,0:T(8,128)(2,1)S(1)} %bitcast.118), channel_id=1, source_target_pairs={{0,3},{1,0},{2,1},{3,2},{4,7},{5,4},{6,5},{7,6},{8,11},{9,8},{10,9... | collective-permute-start | bytes 3932168 | tf_op jit(solution)/shard_map/ppermute | solution.py:221
  109.2 30.3 %collective-permute-start.8 = (bf16[640,1024]{1,0:T(8,128)(2,1)S(1)}, bf16[640,1024]{1,0:T(8,128)(2,1)}, u32[]{:S(2)}, u32[]{:S(2)}) collective-permute-start(bf16[640,1024]{1,0:T(8,128)(2,1)S(1)} %bitcast.119), channel_id=1, source_target_pairs={{0,1},{1,2},{2,3},{3,0},{4,5},{5,6},{6,7},{7,4},{8,9},{9,10},{10,1... | collective-permute-start | bytes 3932168 | tf_op jit(solution)/shard_map/ppermute | solution.py:220
  109.2 35.8 %all-to-all-start.4 = ((bf16[8,128,384]{2,1,0:T(8,128)(2,1)}), bf16[8,128,384]{2,1,0:T(8,128)(2,1)S(1)}, u32[]{:S(2)}, u32[]{:S(2)}) async-start(bf16[8,128,384]{2,1,0:T(8,128)(2,1)} %bitcast.21), calls=%async_computation.4 | async-start | bytes 1572864 | tf_op jit(solution)/shard_map/all_to_all | solution.py:17
  145.0 0.9 copy-start.6
  145.9 43.3 %all-to-all-start.3 = ((bf16[8,4,128,384]{3,2,1,0:T(8,128)(2,1)}), bf16[8,4,128,384]{3,2,1,0:T(8,128)(2,1)S(1)}, u32[]{:S(2)}, u32[]{:S(2)}) async-start(bf16[8,4,128,384]{3,2,1,0:T(8,128)(2,1)} %bitcast.114), calls=%async_computation.3 | async-start | bytes 6291456 | tf_op jit(solution)/shard_map/all_to_all | solution.py:17
  151.7 20.4 %copy-start.5 = (bf16[8,80,1024]{2,1,0:T(8,128)(2,1)S(1)}, bf16[8,80,1024]{2,1,0:T(8,128)(2,1)}, u32[]{:S(2)}) copy-start(bf16[8,80,1024]{2,1,0:T(8,128)(2,1)} %copy-done.4) | copy-start | bytes 3932164
  154.1 17.9 %collective-permute-start.10 = (bf16[320,1024]{1,0:T(8,128)(2,1)S(1)}, bf16[320,1024]{1,0:T(8,128)(2,1)S(1)}, u32[]{:S(2)}, u32[]{:S(2)}) collective-permute-start(bf16[320,1024]{1,0:T(8,128)(2,1)S(1)} %slice.51), channel_id=1, source_target_pairs={{0,1},{1,2},{2,3},{3,0},{4,5},{5,6},{6,7},{7,4},{8,9},{9,10},{10,1... | collective-permute-start | bytes 1966088 | tf_op jit(solution)/shard_map/ppermute | solution.py:224
  154.3 17.6 %collective-permute-start.11 = (bf16[320,1024]{1,0:T(8,128)(2,1)S(1)}, bf16[320,1024]{1,0:T(8,128)(2,1)S(1)}, u32[]{:S(2)}, u32[]{:S(2)}) collective-permute-start(bf16[320,1024]{1,0:T(8,128)(2,1)S(1)} %slice.52), channel_id=1, source_target_pairs={{0,3},{1,0},{2,1},{3,2},{4,7},{5,4},{6,5},{7,6},{8,11},{9,8},{10,9... | collective-permute-start | bytes 1966088 | tf_op jit(solution)/shard_map/ppermute | solution.py:225
  189.3 1.7 copy-start.2
  190.9 44.6 %all-to-all-start.5 = ((bf16[8,4,128,384]{3,2,1,0:T(8,128)(2,1)}), bf16[8,4,128,384]{3,2,1,0:T(8,128)(2,1)}, u32[]{:S(2)}, u32[]{:S(2)}) async-start(bf16[8,4,128,384]{3,2,1,0:T(8,128)(2,1)} %bitcast.113), calls=%async_computation.5 | async-start | bytes 6291456 | tf_op jit(solution)/shard_map/all_to_all | solution.py:17
  196.1 3.6 copy-start.7
  196.1 90.2 %all-gather.9.cloned.1.call-start = ((), (), s32[]{:S(2)}) async-start(), calls=%async_computation.12 | async-start | bytes 4423680 | tf_op jit(solution)/shard_map/all_gather | solution.py:266
  199.7 19.3 %collective-permute-start.13 = (bf16[8,128,384]{2,1,0:T(8,128)(2,1)S(1)}, bf16[8,128,384]{2,1,0:T(8,128)(2,1)S(1)}, u32[]{:S(2)}, u32[]{:S(2)}) collective-permute-start(bf16[8,128,384]{2,1,0:T(8,128)(2,1)S(1)} %copy-done.7), channel_id=1, source_target_pairs={{0,224},{32,0},{64,32},{96,64},{128,96},{160,128},{192,160},{224,1... | collective-permute-start | bytes 2359304 | tf_op jit(solution)/shard_map/ppermute | solution.py:21
  202.2 19.9 %collective-permute-start.12 = (bf16[8,128,384]{2,1,0:T(8,128)(2,1)S(1)}, bf16[8,128,384]{2,1,0:T(8,128)(2,1)S(1)}, u32[]{:S(2)}, u32[]{:S(2)}) collective-permute-start(bf16[8,128,384]{2,1,0:T(8,128)(2,1)S(1)} %copy-done.7), channel_id=1, source_target_pairs={{0,32},{32,64},{64,96},{96,128},{128,160},{160,192},{192,224},{224... | collective-permute-start | bytes 2359304 | tf_op jit(solution)/shard_map/ppermute | solution.py:21
  219.0 8.6 %copy-start.13 = (bf16[8,128,384]{2,1,0:T(8,128)(2,1)}, bf16[8,128,384]{2,1,0:T(8,128)(2,1)S(1)}, u32[]{:S(2)}) copy-start(bf16[8,128,384]{2,1,0:T(8,128)(2,1)S(1)} %collective-permute-done.13.refs_1_) | copy-start | bytes 2359300
  222.2 5.4 %copy-start.14 = (bf16[8,128,384]{2,1,0:T(8,128)(2,1)}, bf16[8,128,384]{2,1,0:T(8,128)(2,1)S(1)}, u32[]{:S(2)}) copy-start(bf16[8,128,384]{2,1,0:T(8,128)(2,1)S(1)} %collective-permute-done.12.refs_8_) | copy-start | bytes 2359300
  222.2 19.0 %collective-permute-start.14 = (bf16[8,128,384]{2,1,0:T(8,128)(2,1)S(1)}, bf16[8,128,384]{2,1,0:T(8,128)(2,1)S(1)}, u32[]{:S(2)}, u32[]{:S(2)}) collective-permute-start(bf16[8,128,384]{2,1,0:T(8,128)(2,1)S(1)} %collective-permute-done.12.refs_8_), channel_id=1, source_target_pairs={{0,32},{32,64},{64,96},{96,128},{128,160},{160,192},{192,224},{224... | collective-permute-start | bytes 2359304 | tf_op jit(solution)/shard_map/ppermute | solution.py:21
  222.2 19.0 %collective-permute-start.15 = (bf16[8,128,384]{2,1,0:T(8,128)(2,1)S(1)}, bf16[8,128,384]{2,1,0:T(8,128)(2,1)}, u32[]{:S(2)}, u32[]{:S(2)}) collective-permute-start(bf16[8,128,384]{2,1,0:T(8,128)(2,1)S(1)} %collective-permute-done.13.refs_1_), channel_id=1, source_target_pairs={{0,224},{32,0},{64,32},{96,64},{128,96},{160,128},{192,160},{224,1... | collective-permute-start | bytes 2359304 | tf_op jit(solution)/shard_map/ppermute | solution.py:21
  227.6 1.7 copy-start.8
  241.2 2.7 copy-start.15
  241.2 4.4 %copy-start.31 = (f32[640,384]{1,0:T(8,128)S(1)}, f32[640,384]{1,0:T(8,128)}, u32[]{:S(2)}) copy-start(f32[640,384]{1,0:T(8,128)} %convolution_bitcast_fusion.1) | copy-start | bytes 2949124
  243.9 1.7 copy-start.9
  245.6 8.8 %copy-start.16 = (bf16[8,128,384]{2,1,0:T(8,128)(2,1)S(1)}, bf16[8,128,384]{2,1,0:T(8,128)(2,1)}, u32[]{:S(2)}) copy-start(bf16[8,128,384]{2,1,0:T(8,128)(2,1)} %copy-done.15) | copy-start | bytes 2359300
  252.0 78.1 %reduce-scatter.2.cloned.1.call-start = ((), (), s32[]{:S(2)}) async-start(), calls=%async_computation.11 | async-start | bytes 2621440 | tf_op jit(solution)/shard_map/reduce_scatter | solution.py:277
  252.0 17.3 %collective-permute-start.16 = (bf16[8,128,384]{2,1,0:T(8,128)(2,1)}, bf16[8,128,384]{2,1,0:T(8,128)(2,1)S(1)}, u32[]{:S(2)}, u32[]{:S(2)}) collective-permute-start(bf16[8,128,384]{2,1,0:T(8,128)(2,1)} %collective-permute-done.15.refs_2_), channel_id=1, source_target_pairs={{0,224},{32,0},{64,32},{96,64},{128,96},{160,128},{192,160},{224,1... | collective-permute-start | bytes 2359304 | tf_op jit(solution)/shard_map/ppermute | solution.py:21
  254.4 18.3 %collective-permute-start.17 = (bf16[8,128,384]{2,1,0:T(8,128)(2,1)S(1)}, bf16[8,128,384]{2,1,0:T(8,128)(2,1)S(1)}, u32[]{:S(2)}, u32[]{:S(2)}) collective-permute-start(bf16[8,128,384]{2,1,0:T(8,128)(2,1)S(1)} %copy-done.16), channel_id=1, source_target_pairs={{0,32},{32,64},{64,96},{96,128},{128,160},{160,192},{192,224},{224... | collective-permute-start | bytes 2359304 | tf_op jit(solution)/shard_map/ppermute | solution.py:21
  269.3 11.9 %copy-start.11 = (bf16[8,128,384]{2,1,0:T(8,128)(2,1)}, bf16[8,128,384]{2,1,0:T(8,128)(2,1)S(1)}, u32[]{:S(2)}) copy-start(bf16[8,128,384]{2,1,0:T(8,128)(2,1)S(1)} %collective-permute-done.16.refs_3_) | copy-start | bytes 2359300
  269.4 8.4 %collective-permute-start.19 = (bf16[4,128,384]{2,1,0:T(8,128)(2,1)S(1)}, bf16[4,128,384]{2,1,0:T(8,128)(2,1)S(1)}, u32[]{:S(2)}, u32[]{:S(2)}) collective-permute-start(bf16[4,128,384]{2,1,0:T(8,128)(2,1)S(1)} %slice.77), channel_id=1, source_target_pairs={{0,224},{32,0},{64,32},{96,64},{128,96},{160,128},{192,160},{224,1... | collective-permute-start | bytes 1179656 | tf_op jit(solution)/shard_map/ppermute | solution.py:21
  272.6 8.5 %copy-start.12 = (bf16[8,128,384]{2,1,0:T(8,128)(2,1)}, bf16[8,128,384]{2,1,0:T(8,128)(2,1)S(1)}, u32[]{:S(2)}) copy-start(bf16[8,128,384]{2,1,0:T(8,128)(2,1)S(1)} %collective-permute-done.17.refs_6_) | copy-start | bytes 2359300
  272.7 8.5 %collective-permute-start.18 = (bf16[4,128,384]{2,1,0:T(8,128)(2,1)S(1)}, bf16[4,128,384]{2,1,0:T(8,128)(2,1)S(1)}, u32[]{:S(2)}, u32[]{:S(2)}) collective-permute-start(bf16[4,128,384]{2,1,0:T(8,128)(2,1)S(1)} %slice.76), channel_id=1, source_target_pairs={{0,32},{32,64},{64,96},{96,128},{128,160},{160,192},{192,224},{224... | collective-permute-start | bytes 1179656 | tf_op jit(solution)/shard_map/ppermute | solution.py:21
  277.8 3.4 copy-start.18
  281.2 0.8 copy-start.19
  296.2 45.4 %all-to-all-start.6 = ((bf16[8,4,128,384]{3,2,1,0:T(8,128)(2,1)}), bf16[8,4,128,384]{3,2,1,0:T(8,128)(2,1)S(1)}, u32[]{:S(2)}, u32[]{:S(2)}) async-start(bf16[8,4,128,384]{3,2,1,0:T(8,128)(2,1)} %bitcast.116), calls=%async_computation.6 | async-start | bytes 6291456 | tf_op jit(solution)/shard_map/all_to_all | solution.py:17
  341.7 25.6 %all-to-all-start.7 = ((bf16[64,32,128]{2,1,0:T(8,128)(2,1)}), bf16[64,32,128]{2,1,0:T(8,128)(2,1)}, u32[]{:S(2)}, u32[]{:S(2)}) async-start(bf16[64,32,128]{2,1,0:T(8,128)(2,1)} %bitcast.130), calls=%async_computation.8 | async-start | bytes 1048576 | tf_op jit(solution)/shard_map/all_to_all | solution.py:17
  349.6 19.5 %copy-start.1 = (bf16[2,16,4096]{2,1,0:T(8,128)(2,1)S(1)}, bf16[2,16,4096]{2,1,0:T(8,128)(2,1)}, u32[]{:S(2)}) copy-start(bf16[2,16,4096]{2,1,0:T(8,128)(2,1)} %param.8) | copy-start | bytes 786436
Sparse Core Ops, SparseCore 0:
  27.4 80.4 all-gather.4
  109.6 73.0 all-gather.6
  252.1 33.9 all-gather.8
  296.4 33.6 reduce-scatter.1

commit v3 on v2

--- a/solution.py
+++ b/solution.py
@@ -219,12 +219,14 @@
     to_last = [(i, (i - 1) % Y) for i in range(Y)]
     from_last = lax.ppermute(quarters, "y", to_next)
     from_next = lax.ppermute(quarters, "y", to_last)
-    gate_all, from_last, from_next = lax.optimization_barrier((gate_all, from_last, from_next))
+    gate_all, block_down, from_last, from_next = lax.optimization_barrier(
+        (gate_all, block_down, from_last, from_next)
+    )
     far = [
         lax.ppermute(from_last[:half], "y", to_next),
         lax.ppermute(from_next[half:], "y", to_last),
     ]
-    far, block_down = lax.optimization_barrier((far, block_down))
+    down_all = gather_planes(block_down)
     inputs = take_rows(
         jnp.stack([quarters, from_next, jnp.concatenate(far, axis=0), from_last]),
         (jnp.arange(Y, dtype=jnp.int32) - quarter + Y) % Y,
@@ -246,28 +248,25 @@
     by_part = (part_count, piece_rows, width)
     serve_gate = assemble(exchange(take_rows(gate_all, chosen_slot), XC))
     arrived_up = exchange(take_rows(up_all, chosen_slot), XC)
-    down_ring = Ring(block_down).hop()
-    inputs = down_ring.hold(inputs)
     gate_act = jnp.einsum(
         "ymd,ydf->mf", inputs, serve_gate.reshape(by_part), preferred_element_type=jnp.float32
     )
     arrived_up, gate_act = lax.optimization_barrier((arrived_up, gate_act))
-    down_ring.hop()
-    arrived_up = down_ring.hold(arrived_up)
-    down_ring.hop()
     serve_up = assemble(arrived_up)
     up_act = jnp.einsum(
         "ymd,ydf->mf", inputs, serve_up.reshape(by_part), preferred_element_type=jnp.float32
     )
     hidden = (jax.nn.silu(gate_act) * up_act * row_weight.reshape(-1, 1)).astype(jnp.bfloat16)
 
-    down_ring.hop()
 
     plane_hidden = lax.all_gather(hidden, XC, axis=0, tiled=False).reshape(
         PLANE, PLANE, capacity, width
     )
-    down_rows = down_ring.pick(chosen).reshape(PLANE, part_count, block_rows, width)
-    serve_down = assemble(exchange(down_rows, XC))
+    down_rows = take_rows(down_all, chosen_slot)
+    half_parts = part_count // 2
+    arrived_down = [exchange(down_rows[:, :half_parts], XC), exchange(down_rows[:, half_parts:], XC)]
+    down_rows, arrived_down[0] = lax.optimization_barrier((down_rows, arrived_down[0]))
+    serve_down = assemble(jnp.concatenate(arrived_down, axis=1))
     partial_value = jnp.einsum(
         "slpf,syrf->slpyr", plane_hidden, down_rows, preferred_element_type=jnp.float32
     ).astype(jnp.bfloat16)

time: 377 us -> 387 us (1.027)
  blocking collectives: 43.1 us -> 98.8 us
  waiting for transfers between devices: 159 us -> 131 us
  starting transfers between devices: 67.9 us -> 52 us
  Pallas kernels: 7.03 us -> 2.67 us
  local copies, waits for them, and re-layouts: 49.3 us -> 53.4 us
    all_to_all x2 -> x4, blocking collectives: 43.1 us -> 98.8 us  [exchange(): return lax.all_to_all(value, axes, split_axis=0, concat_axis=0, tiled=True)]
    ppermute x16 -> x8, waiting for transfers between devices: 56.9 us -> 12.9 us  [shift(): return lax.ppermute(value, 'z', [(i, (i + step) % Z) for i in range(Z)])]
    ppermute x1, waiting for transfers between devices: 21.2 us -> 0.01 us  [body(): from_next = lax.ppermute(quarters, 'y', to_last)]
    all_gather x2 -> x3, waiting for transfers between devices: 0.35 us -> 17.6 us  [gather_planes(): rows = lax.all_gather(block.reshape(-1, width), 'z', axis=0, tiled=True)]
    ppermute x16 -> x8, starting transfers between devices: 23.8 us -> 12.9 us  [shift(): return lax.ppermute(value, 'z', [(i, (i + step) % Z) for i in range(Z)])]
    all_to_all x6 -> x5, waiting for transfers between devices: 36.6 us -> 47.1 us  [exchange(): return lax.all_to_all(value, axes, split_axis=0, concat_axis=0, tiled=True)]
    ppermute x1, waiting for transfers between devices: 3.23 us -> 10.4 us  [body(): from_last = lax.ppermute(quarters, 'y', to_next)]
    all_to_all x6 -> x5, starting transfers between devices: 38.3 us -> 31.8 us  [exchange(): return lax.all_to_all(value, axes, split_axis=0, concat_axis=0, tiled=True)]
  transfers between devices with their start and end apart: 30 -> 22, of which waited for: 19 -> 14; matrix products, arithmetic and copies ran while one was open for 14% -> 17% of each run, Pallas kernels for 2% -> 1%
where the time goes in v3:
time: 387 us; the launch traced here: 386 us
  waiting for transfers between devices  131 us (34%)
  blocking collectives  98.8 us (26%)
  local copies, waits for them, and re-layouts  53.4 us (14%)
  starting transfers between devices  52 us (13%)
  matrix products  21.1 us (5%)
  between operations  14.3 us (4%)
  other arithmetic  12.2 us (3%)
    all_to_all x4, blocking collectives, exchange(): return lax.all_to_all(value, axes, split_axis=0, concat_axis=0, tiled=True)  98.8 us
    all_to_all x5, waiting for transfers between devices, exchange(): return lax.all_to_all(value, axes, split_axis=0, concat_axis=0, tiled=True)  47.1 us
    all_to_all x5, starting transfers between devices, exchange(): return lax.all_to_all(value, axes, split_axis=0, concat_axis=0, tiled=True)  31.8 us
    reduce_scatter x1, waiting for transfers between devices, body(): lax.psum_scatter(plane_out.reshape(-1, block_rows), 'y', scatter_dimensio...  25.2 us
    gather x6, local copies, waits for them, and re-layouts, take_rows(): return value.at[index].get(mode='promise_in_bounds')  21.5 us
    all_gather x3, waiting for transfers between devices, gather_planes(): rows = lax.all_gather(block.reshape(-1, width), 'z', axis=0, tiled=True)  17.6 us
    ppermute x1, waiting for transfers between devices, body(): lax.ppermute(from_last[:half], 'y', to_next)  13.6 us
    ppermute x8, waiting for transfers between devices, shift(): return lax.ppermute(value, 'z', [(i, (i + step) % Z) for i in range(Z)])  12.9 us
  transfers between devices with their start and end apart: 22, of which 14 were waited for; matrix products, arithmetic and copies ran while one was open for 17% of the time, Pallas kernels for 1%

profile of v3, /device:TPU:1, one launch (start us, length us, event | category | flops | bytes accessed | tf_op | source)
XLA Modules:
  0.0 385.6 jit_solution(158656312479629117)
XLA Ops:
  7.2 6.8 %all-to-all-start = ((bf16[8,128,384]{2,1,0:T(8,128)(2,1)}), bf16[8,128,384]{2,1,0:T(8,128)(2,1)S(1)}, u32[]{:S(2)}, u32[]{:S(2)}) async-start(bf16[8,128,384]{2,1,0:T(8,128)(2,1)} %bitcast.138), calls=%async_computation | async-start | bytes 1572864 | tf_op jit(solution)/shard_map/all_to_all | solution.py:17
  14.0 0.7 copy.79
  14.8 0.7 copy.80
  16.1 10.2 %all-to-all-done = bf16[8,128,384]{2,1,0:T(8,128)(2,1)S(1)} async-done(((bf16[8,128,384]{2,1,0:T(8,128)(2,1)}), bf16[8,128,384]{2,1,0:T(8,128)(2,1)S(1)}, u32[]{:S(2)}, u32[]{:S(2)}) %all-to-all-start) | async-done | bytes 786464 | tf_op jit(solution)/shard_map/all_to_all | solution.py:17
  26.3 0.9 copy-done.9
  27.3 16.2 %all_to_all.45 = bf16[8,128,384]{2,1,0:T(8,128)(2,1)} all-to-all(bf16[8,128,384]{2,1,0:T(8,128)(2,1)S(1)} %bitcast.139), channel_id=1, replica_groups=mesh['z'=8,'x'=4,'c'=2,'y'=4] {'x','c'}, dimensions={0} | all-to-all | bytes 1572864 | tf_op jit(solution)/shard_map/all_to_all | solution.py:17
  43.9 0.8 collective-permute-start
  44.7 4.0 %collective-permute-start.4 = (bf16[2,16,1152]{2,1,0:T(8,128)(2,1)S(1)}, bf16[2,16,1152]{2,1,0:T(8,128)(2,1)S(1)}, u32[]{:S(2)}, u32[]{:S(2)}) collective-permute-start(bf16[2,16,1152]{2,1,0:T(8,128)(2,1)S(1)} %bitcast.143), channel_id=1, source_target_pairs={{0,224},{32,0},{64,32},{96,64},{128,96},{160,128},{192,160},{224,1... | collective-permute-start | bytes 221192 | tf_op jit(solution)/shard_map/ppermute | solution.py:21
  48.8 3.9 %collective-permute-done.refs_8_ = bf16[2,16,1152]{2,1,0:T(8,128)(2,1)S(1)} collective-permute-done((bf16[2,16,1152]{2,1,0:T(8,128)(2,1)S(1)}, bf16[2,16,1152]{2,1,0:T(8,128)(2,1)S(1)}, u32[]{:S(2)}, u32[]{:S(2)}) %collective-permute-start) | collective-permute-done | bytes 73760 | tf_op jit(solution)/shard_map/ppermute | solution.py:21
  52.7 2.7 collective-permute-start.5
  55.5 3.7 collective-permute-done.1.refs_7_
  59.3 2.7 collective-permute-start.6
  61.9 3.7 collective-permute-done.2.refs_6_
  65.6 2.7 collective-permute-start.7
  69.2 1.6 collective-permute-done.3.refs_4_
  72.0 2.7 pick_pieces.1
  74.7 0.9 slice_bitcast_fusion.4
  76.5 1.6 convolution_convert_fusion
  78.2 27.1 %all_to_all.46 = bf16[8,96,1024]{2,1,0:T(8,128)(2,1)S(1)} all-to-all(bf16[8,96,1024]{2,1,0:T(8,128)(2,1)S(1)} %pad_maximum_fusion.1), channel_id=1, replica_groups=mesh['z'=8,'x'=4,'c'=2,'y'=4] {'x','c'}, dimensions={0} | all-to-all | bytes 3145728 | tf_op jit(solution)/shard_map/all_to_all | solution.py:17
  105.3 1.1 copy-done.3
  106.6 1.4 collective-permute-start.8
  107.9 2.4 collective-permute-start.9
  110.4 16.6 %all_to_all.47 = bf16[8,128,384]{2,1,0:T(8,128)(2,1)} all-to-all(bf16[8,128,384]{2,1,0:T(8,128)(2,1)S(1)} %bitcast.140), channel_id=1, replica_groups=mesh['z'=8,'x'=4,'c'=2,'y'=4] {'x','c'}, dimensions={0} | all-to-all | bytes 1572864 | tf_op jit(solution)/shard_map/all_to_all | solution.py:17
  127.0 10.4 %collective-permute-done.8 = bf16[640,1024]{1,0:T(8,128)(2,1)S(1)} collective-permute-done((bf16[640,1024]{1,0:T(8,128)(2,1)S(1)}, bf16[640,1024]{1,0:T(8,128)(2,1)S(1)}, u32[]{:S(2)}, u32[]{:S(2)}) %collective-permute-start.8) | collective-permute-done | bytes 1310752 | tf_op jit(solution)/shard_map/ppermute | solution.py:220
  137.4 1.1 copy-done.10
  138.7 0.7 gather_fusion
  139.6 5.5 %gather_fusion.1 = bf16[32,128,384]{2,1,0:T(8,128)(2,1)} fusion(bf16[64,128,384]{2,1,0:T(8,128)(2,1)} %bitcast.136, s32[1024]{0:T(1024)S(1)} %pad_clamp_fusion.1), kind=kCustom, calls=%fused_computation.1 | custom fusion | bytes 6291584 | tf_op jit(solution)/shard_map/gather | solution.py:109
  145.1 5.3 %all-to-all-start.4 = ((bf16[8,4,128,384]{3,2,1,0:T(8,128)(2,1)}), bf16[8,4,128,384]{3,2,1,0:T(8,128)(2,1)S(1)}, u32[]{:S(2)}, u32[]{:S(2)}) async-start(bf16[8,4,128,384]{3,2,1,0:T(8,128)(2,1)} %bitcast.116), calls=%async_computation.4 | async-start | bytes 6291456 | tf_op jit(solution)/shard_map/all_to_all | solution.py:17
  150.4 1.3 slice.51
  152.3 1.1 slice.52
  153.5 2.4 collective-permute-start.11
  155.9 13.6 %collective-permute-done.10 = bf16[320,1024]{1,0:T(8,128)(2,1)S(1)} collective-permute-done((bf16[320,1024]{1,0:T(8,128)(2,1)S(1)}, bf16[320,1024]{1,0:T(8,128)(2,1)S(1)}, u32[]{:S(2)}, u32[]{:S(2)}) %collective-permute-start.10) | collective-permute-done | bytes 655392 | tf_op jit(solution)/shard_map/ppermute | solution.py:226
  169.7 4.0 %pad_maximum_fusion = bf16[4,640,1024]{2,1,0:T(8,128)(2,1)} fusion(bf16[1,640,1024]{2,1,0:T(8,128)(2,1)S(1)} %bitcast.131, bf16[1,640,1024]{2,1,0:T(8,128)(2,1)S(1)} %maximum_bitcast_fusion.1, bf16[1,640,1024]{2,1,0:T(8,128)(2,1)} %bitcast.21, bf16[1,640,1024]{2,1,0:T(8,128)(2,1)S(1)} %bitcast.122), kind=kLoop, calls=%fused_computation.5 | loop fusion | flops 7864320 | bytes 10485760 | tf_op jit(solution)/shard_map/stack | solution.py:231
  173.7 5.8 %gather_fusion.2 = bf16[4,640,1024]{2,1,0:T(8,128)(2,1)} fusion(bf16[4,640,1024]{2,1,0:T(8,128)(2,1)} %pad_maximum_fusion, s32[1024]{0:T(1024)S(1)} %pad_clamp_fusion), kind=kCustom, calls=%fused_computation.2 | custom fusion | bytes 10485776 | tf_op jit(solution)/shard_map/gather | solution.py:109
  179.5 3.2 all-gather.8.cloned.1.call-done
  182.7 5.4 %gather_fusion.3 = bf16[32,128,384]{2,1,0:T(8,128)(2,1)} fusion(bf16[64,128,384]{2,1,0:T(8,128)(2,1)} %bitcast.135, s32[1024]{0:T(1024)S(1)} %pad_clamp_fusion.1), kind=kCustom, calls=%fused_computation.3 | custom fusion | bytes 6291584 | tf_op jit(solution)/shard_map/gather | solution.py:109
  188.2 1.7 copy-done.2
  189.8 5.0 %all-to-all-start.5 = ((bf16[8,4,128,384]{3,2,1,0:T(8,128)(2,1)}), bf16[8,4,128,384]{3,2,1,0:T(8,128)(2,1)}, u32[]{:S(2)}, u32[]{:S(2)}) async-start(bf16[8,4,128,384]{3,2,1,0:T(8,128)(2,1)} %bitcast.115), calls=%async_computation.5 | async-start | bytes 6291456 | tf_op jit(solution)/shard_map/all_to_all | solution.py:17
  197.5 0.8 select_reduce_fusion
  198.3 0.8 add_select_fusion
  199.0 0.8 fusion.29
  199.8 1.3 fusion.2
  201.4 2.4 copy.86
  203.9 1.7 copy-done.7
  205.5 5.4 %convolution_bitcast_fusion.1 = f32[640,384]{1,0:T(8,128)S(1)} fusion(bf16[4,640,1024]{2,1,0:T(8,128)(2,1)} %gather_fusion.2, bf16[4,1024,384]{2,1,0:T(8,128)(2,1)S(1)} %bitcast.123), kind=kOutput, calls=%fused_computation.23 | convolution fusion | flops 2013265920 | bytes 9371648 | tf_op jit(solution)/shard_map/ymd,ydf->mf/dot_general | solution.py:251
  210.9 21.7 %all-to-all-done.5 = bf16[8,4,128,384]{3,2,1,0:T(8,128)(2,1)} async-done(((bf16[8,4,128,384]{3,2,1,0:T(8,128)(2,1)}), bf16[8,4,128,384]{3,2,1,0:T(8,128)(2,1)}, u32[]{:S(2)}, u32[]{:S(2)}) %all-to-all-start.5) | async-done | bytes 3145760 | tf_op jit(solution)/shard_map/all_to_all | solution.py:17
  232.6 2.4 copy.88
  235.0 1.7 copy-done.8
  236.7 6.2 %fusion.19 = bf16[640,384]{1,0:T(8,128)(2,1)} fusion(bf16[4,640,1024]{2,1,0:T(8,128)(2,1)} %gather_fusion.2, bf16[4,1024,384]{2,1,0:T(8,128)(2,1)S(1)} %bitcast.125, f32[640,384]{1,0:T(8,128)S(1)} %convolution_bitcast_fusion.1, f32[640]{0:T(1024)S(1)} %mul.45), kind=kOutput, calls=%fused_computation.25 | convolution fusion | flops 2014986240 | bytes 9865728 | tf_op jit(solution)/shard_map/ymd,ydf->mf/dot_general | solution.py:256
  243.2 14.4 %all-gather.10.cloned.1.call-done = bf16[8192,384]{1,0:T(8,128)(2,1)} async-done(((bf16[1024,384]{1,0:T(8,128)(2,1)}), bf16[8192,384]{1,0:T(8,128)(2,1)}) %all-gather.10.cloned.1.call-update) | async-done | bytes 6291472 | tf_op jit(solution)/shard_map/all_gather | solution.py:150
  257.6 4.0 %gather_fusion.4 = bf16[32,128,384]{2,1,0:T(8,128)(2,1)S(1)} fusion(bf16[64,128,384]{2,1,0:T(8,128)(2,1)} %bitcast.137, s32[1024]{0:T(1024)S(1)} %pad_clamp_fusion.1), kind=kCustom, calls=%fused_computation.4 | custom fusion | bytes 6291584 | tf_op jit(solution)/shard_map/gather | solution.py:109
  261.7 1.5 fusion.50
  263.2 39.0 %all_to_all.48 = bf16[8,2,128,384]{3,2,1,0:T(8,128)(2,1)} all-to-all(bf16[8,2,128,384]{3,2,1,0:T(8,128)(2,1)S(1)} %get-tuple-element.46), channel_id=1, replica_groups=mesh['z'=8,'x'=4,'c'=2,'y'=4] {'x','c'}, dimensions={0} | all-to-all | bytes 3145728 | tf_op jit(solution)/shard_map/all_to_all | solution.py:17
  302.1 4.2 %all-gather.12.cloned.1.call-done = bf16[5120,384]{1,0:T(8,128)(2,1)} async-done(((bf16[640,384]{1,0:T(8,128)(2,1)}), bf16[5120,384]{1,0:T(8,128)(2,1)}) %all-gather.12.cloned.1.call-update) | async-done | bytes 3932176 | tf_op jit(solution)/shard_map/all_gather | solution.py:262
  306.4 7.5 %fusion.12 = bf16[4,8,256,128]{2,3,0,1:T(8,128)(2,1)} fusion(s32[8,8,256]{2,1,0:T(8,128)S(1)} %add_select_fusion, pred[8,8,256]{2,1,0:T(8,128)(4,1)S(1)} %fusion.29, bf16[8,8,80,384,1]{3,2,1,0,4:T(8,128)(2,1)} %bitcast.146, bf16[8,4,128,384]{3,2,1,0:T(8,128)(2,1)S(1)} %bitcast.118), kind=kOutput, calls=%fused_computation.17 | convolution fusion | flops 3361734656 | bytes 9256960 | tf_op jit(solution)/shard_map/lspt,slpyr->yltr/dot_general | solution.py:273
  313.8 4.0 %copy.94 = bf16[4,8,256,128]{3,2,1,0:T(8,128)(2,1)} copy(bf16[4,8,256,128]{2,3,0,1:T(8,128)(2,1)} %fusion.12) | data formatting | bytes 4194304 | tf_op jit(solution)/shard_map/convert_element_type | solution.py:275
  317.8 3.9 %all-to-all-start.7 = ((bf16[8,2,128,384]{3,2,1,0:T(8,128)(2,1)}), bf16[8,2,128,384]{3,2,1,0:T(8,128)(2,1)S(1)}, u32[]{:S(2)}, u32[]{:S(2)}) async-start(bf16[8,2,128,384]{3,2,1,0:T(8,128)(2,1)} %get-tuple-element.47), calls=%async_computation.7 | async-start | bytes 3145728 | tf_op jit(solution)/shard_map/all_to_all | solution.py:17
  321.7 25.2 %reduce-scatter.2.cloned.1.call-done = bf16[2048,128]{1,0:T(8,128)(2,1)} async-done(((bf16[8192,128]{1,0:T(8,128)(2,1)}), bf16[2048,128]{1,0:T(8,128)(2,1)}) %reduce-scatter.2.cloned.1.call-update) | async-done | bytes 524304 | tf_op jit(solution)/shard_map/reduce_scatter | solution.py:276
  347.0 1.9 copy.95
  348.9 10.8 %all-to-all-start.8 = ((bf16[64,32,128]{2,1,0:T(8,128)(2,1)}), bf16[64,32,128]{2,1,0:T(8,128)(2,1)}, u32[]{:S(2)}, u32[]{:S(2)}) async-start(bf16[64,32,128]{2,1,0:T(8,128)(2,1)} %bitcast.134), calls=%async_computation.9 | async-start | bytes 1048576 | tf_op jit(solution)/shard_map/all_to_all | solution.py:17
  360.0 2.1 copy.89
  362.1 15.2 %all-to-all-done.8 = bf16[64,32,128]{2,1,0:T(8,128)(2,1)} async-done(((bf16[64,32,128]{2,1,0:T(8,128)(2,1)}), bf16[64,32,128]{2,1,0:T(8,128)(2,1)}, u32[]{:S(2)}, u32[]{:S(2)}) %all-to-all-start.8) | async-done | bytes 524320 | tf_op jit(solution)/shard_map/all_to_all | solution.py:17
  377.3 1.1 reduce_sum.112
  378.5 0.7 reshape.435
  (125 shorter events, 9.3 us)
Async XLA Ops:
  7.2 8.9 %copy-start = (bf16[2,16,4096]{2,1,0:T(8,128)(2,1)S(1)}, bf16[2,16,4096]{2,1,0:T(8,128)(2,1)}, u32[]{:S(2)}) copy-start(bf16[2,16,4096]{2,1,0:T(8,128)(2,1)} %param.8) | copy-start | bytes 786436
  7.2 20.1 %copy-start.12 = (bf16[1,1024,384]{2,1,0:T(8,128)(2,1)S(1)}, bf16[1,1024,384]{2,1,0:T(8,128)(2,1)}, u32[]{:S(2)}) copy-start(bf16[1,1024,384]{2,1,0:T(8,128)(2,1)} %param.14) | copy-start | bytes 2359300
  7.2 36.4 %copy-start.23 = (s32[64]{0:T(128)S(1)}, s32[64]{0:T(128)}, u32[]{:S(2)}) copy-start(s32[64]{0:T(128)} %param.12) | copy-start | bytes 772
  7.2 19.1 %all-to-all-start = ((bf16[8,128,384]{2,1,0:T(8,128)(2,1)}), bf16[8,128,384]{2,1,0:T(8,128)(2,1)S(1)}, u32[]{:S(2)}, u32[]{:S(2)}) async-start(bf16[8,128,384]{2,1,0:T(8,128)(2,1)} %bitcast.138), calls=%async_computation | async-start | bytes 1572864 | tf_op jit(solution)/shard_map/all_to_all | solution.py:17
  14.0 124.4 %all-gather.6.cloned.1.call-start = ((), (), s32[]{:S(2)}) async-start(), calls=%async_computation.10 | async-start | bytes 7077888 | tf_op jit(solution)/shard_map/all_gather | solution.py:150
  26.3 0.9 copy-start.9
  27.2 155.5 %all-gather.8.cloned.1.call-start = ((), (), s32[]{:S(2)}) async-start(), calls=%async_computation.11 | async-start | bytes 7077888 | tf_op jit(solution)/shard_map/all_gather | solution.py:150
  43.5 214.1 %all-gather.10.cloned.1.call-start = ((), (), s32[]{:S(2)}) async-start(), calls=%async_computation.12 | async-start | bytes 7077888 | tf_op jit(solution)/shard_map/all_gather | solution.py:150
  43.9 26.9 %copy-start.14 = (bf16[32,1152]{1,0:T(8,128)(2,1)}, bf16[32,1152]{1,0:T(8,128)(2,1)S(1)}, u32[]{:S(2)}) copy-start(bf16[32,1152]{1,0:T(8,128)(2,1)S(1)} %pad.4) | copy-start | bytes 221188
  43.9 8.8 %collective-permute-start = (bf16[2,16,1152]{2,1,0:T(8,128)(2,1)S(1)}, bf16[2,16,1152]{2,1,0:T(8,128)(2,1)S(1)}, u32[]{:S(2)}, u32[]{:S(2)}) collective-permute-start(bf16[2,16,1152]{2,1,0:T(8,128)(2,1)S(1)} %bitcast.142), channel_id=1, source_target_pairs={{0,32},{32,64},{64,96},{96,128},{128,160},{160,192},{192,224},{224... | collective-permute-start | bytes 221192 | tf_op jit(solution)/shard_map/ppermute | solution.py:21
  44.7 8.0 %collective-permute-start.4 = (bf16[2,16,1152]{2,1,0:T(8,128)(2,1)S(1)}, bf16[2,16,1152]{2,1,0:T(8,128)(2,1)S(1)}, u32[]{:S(2)}, u32[]{:S(2)}) collective-permute-start(bf16[2,16,1152]{2,1,0:T(8,128)(2,1)S(1)} %bitcast.143), channel_id=1, source_target_pairs={{0,224},{32,0},{64,32},{96,64},{128,96},{160,128},{192,160},{224,1... | collective-permute-start | bytes 221192 | tf_op jit(solution)/shard_map/ppermute | solution.py:21
  52.7 18.1 %copy-start.17 = (bf16[2,16,1152]{2,1,0:T(8,128)(2,1)}, bf16[2,16,1152]{2,1,0:T(8,128)(2,1)S(1)}, u32[]{:S(2)}) copy-start(bf16[2,16,1152]{2,1,0:T(8,128)(2,1)S(1)} %collective-permute-done.refs_8_) | copy-start | bytes 221188
  52.7 6.5 %collective-permute-start.1 = (bf16[2,16,1152]{2,1,0:T(8,128)(2,1)S(1)}, bf16[2,16,1152]{2,1,0:T(8,128)(2,1)S(1)}, u32[]{:S(2)}, u32[]{:S(2)}) collective-permute-start(bf16[2,16,1152]{2,1,0:T(8,128)(2,1)S(1)} %collective-permute-done.refs_8_), channel_id=1, source_target_pairs={{0,32},{32,64},{64,96},{96,128},{128,160},{160,192},{192,224},{224... | collective-permute-start | bytes 221192 | tf_op jit(solution)/shard_map/ppermute | solution.py:21
  52.7 18.1 %copy-start.18 = (bf16[2,16,1152]{2,1,0:T(8,128)(2,1)}, bf16[2,16,1152]{2,1,0:T(8,128)(2,1)S(1)}, u32[]{:S(2)}) copy-start(bf16[2,16,1152]{2,1,0:T(8,128)(2,1)S(1)} %collective-permute-done.4.refs_1_) | copy-start | bytes 221188
  52.7 6.5 %collective-permute-start.5 = (bf16[2,16,1152]{2,1,0:T(8,128)(2,1)S(1)}, bf16[2,16,1152]{2,1,0:T(8,128)(2,1)S(1)}, u32[]{:S(2)}, u32[]{:S(2)}) collective-permute-start(bf16[2,16,1152]{2,1,0:T(8,128)(2,1)S(1)} %collective-permute-done.4.refs_1_), channel_id=1, source_target_pairs={{0,224},{32,0},{64,32},{96,64},{128,96},{160,128},{192,160},{224,1... | collective-permute-start | bytes 221192 | tf_op jit(solution)/shard_map/ppermute | solution.py:21
  59.2 11.6 %copy-start.19 = (bf16[2,16,1152]{2,1,0:T(8,128)(2,1)}, bf16[2,16,1152]{2,1,0:T(8,128)(2,1)S(1)}, u32[]{:S(2)}) copy-start(bf16[2,16,1152]{2,1,0:T(8,128)(2,1)S(1)} %collective-permute-done.1.refs_7_) | copy-start | bytes 221188
  59.2 6.4 %collective-permute-start.2 = (bf16[2,16,1152]{2,1,0:T(8,128)(2,1)S(1)}, bf16[2,16,1152]{2,1,0:T(8,128)(2,1)S(1)}, u32[]{:S(2)}, u32[]{:S(2)}) collective-permute-start(bf16[2,16,1152]{2,1,0:T(8,128)(2,1)S(1)} %collective-permute-done.1.refs_7_), channel_id=1, source_target_pairs={{0,32},{32,64},{64,96},{96,128},{128,160},{160,192},{192,224},{224... | collective-permute-start | bytes 221192 | tf_op jit(solution)/shard_map/ppermute | solution.py:21
  59.2 11.6 %copy-start.20 = (bf16[2,16,1152]{2,1,0:T(8,128)(2,1)}, bf16[2,16,1152]{2,1,0:T(8,128)(2,1)S(1)}, u32[]{:S(2)}) copy-start(bf16[2,16,1152]{2,1,0:T(8,128)(2,1)S(1)} %collective-permute-done.5.refs_2_) | copy-start | bytes 221188
  59.3 6.4 %collective-permute-start.6 = (bf16[2,16,1152]{2,1,0:T(8,128)(2,1)S(1)}, bf16[2,16,1152]{2,1,0:T(8,128)(2,1)S(1)}, u32[]{:S(2)}, u32[]{:S(2)}) collective-permute-start(bf16[2,16,1152]{2,1,0:T(8,128)(2,1)S(1)} %collective-permute-done.5.refs_2_), channel_id=1, source_target_pairs={{0,224},{32,0},{64,32},{96,64},{128,96},{160,128},{192,160},{224,1... | collective-permute-start | bytes 221192 | tf_op jit(solution)/shard_map/ppermute | solution.py:21
  65.6 5.2 %copy-start.15 = (bf16[2,16,1152]{2,1,0:T(8,128)(2,1)}, bf16[2,16,1152]{2,1,0:T(8,128)(2,1)S(1)}, u32[]{:S(2)}) copy-start(bf16[2,16,1152]{2,1,0:T(8,128)(2,1)S(1)} %collective-permute-done.2.refs_6_) | copy-start | bytes 221188
  65.6 5.2 %collective-permute-start.3 = (bf16[1,16,1152]{2,1,0:T(8,128)(2,1)S(1)}, bf16[1,16,1152]{2,1,0:T(8,128)(2,1)S(1)}, u32[]{:S(2)}, u32[]{:S(2)}) collective-permute-start(bf16[1,16,1152]{2,1,0:T(8,128)(2,1)S(1)} %slice.70), channel_id=1, source_target_pairs={{0,32},{32,64},{64,96},{96,128},{128,160},{160,192},{192,224},{224... | collective-permute-start | bytes 110600 | tf_op jit(solution)/shard_map/ppermute | solution.py:21
  65.6 5.2 %copy-start.16 = (bf16[2,16,1152]{2,1,0:T(8,128)(2,1)}, bf16[2,16,1152]{2,1,0:T(8,128)(2,1)S(1)}, u32[]{:S(2)}) copy-start(bf16[2,16,1152]{2,1,0:T(8,128)(2,1)S(1)} %collective-permute-done.6.refs_3_) | copy-start | bytes 221188
  65.6 5.1 %collective-permute-start.7 = (bf16[1,16,1152]{2,1,0:T(8,128)(2,1)S(1)}, bf16[1,16,1152]{2,1,0:T(8,128)(2,1)S(1)}, u32[]{:S(2)}, u32[]{:S(2)}) collective-permute-start(bf16[1,16,1152]{2,1,0:T(8,128)(2,1)S(1)} %slice.71), channel_id=1, source_target_pairs={{0,224},{32,0},{64,32},{96,64},{128,96},{160,128},{192,160},{224,1... | collective-permute-start | bytes 110600 | tf_op jit(solution)/shard_map/ppermute | solution.py:21
  70.8 0.6 copy-start.21
  71.4 0.6 copy-start.22
  78.2 32.2 %copy-start.13 = (bf16[1,1024,384]{2,1,0:T(8,128)(2,1)S(1)}, bf16[1,1024,384]{2,1,0:T(8,128)(2,1)}, u32[]{:S(2)}) copy-start(bf16[1,1024,384]{2,1,0:T(8,128)(2,1)} %param.15) | copy-start | bytes 2359300
  105.3 1.1 copy-start.3
  106.5 32.2 %copy-start.24 = (s32[64]{0:T(128)S(1)}, s32[64]{0:T(128)}, u32[]{:S(2)}) copy-start(s32[64]{0:T(128)} %param.11) | copy-start | bytes 772
  106.6 1.4 copy-start.5
  106.6 30.8 %collective-permute-start.8 = (bf16[640,1024]{1,0:T(8,128)(2,1)S(1)}, bf16[640,1024]{1,0:T(8,128)(2,1)S(1)}, u32[]{:S(2)}, u32[]{:S(2)}) collective-permute-start(bf16[640,1024]{1,0:T(8,128)(2,1)S(1)} %bitcast.120), channel_id=1, source_target_pairs={{0,1},{1,2},{2,3},{3,0},{4,5},{5,6},{6,7},{7,4},{8,9},{9,10},{10,1... | collective-permute-start | bytes 3932168 | tf_op jit(solution)/shard_map/ppermute | solution.py:220
  107.9 30.5 %collective-permute-start.9 = (bf16[640,1024]{1,0:T(8,128)(2,1)S(1)}, bf16[640,1024]{1,0:T(8,128)(2,1)}, u32[]{:S(2)}, u32[]{:S(2)}) collective-permute-start(bf16[640,1024]{1,0:T(8,128)(2,1)S(1)} %bitcast.121), channel_id=1, source_target_pairs={{0,3},{1,0},{2,1},{3,2},{4,7},{5,4},{6,5},{7,6},{8,11},{9,8},{10,9... | collective-permute-start | bytes 3932168 | tf_op jit(solution)/shard_map/ppermute | solution.py:221
  137.4 1.1 copy-start.10
  145.1 43.0 %all-to-all-start.4 = ((bf16[8,4,128,384]{3,2,1,0:T(8,128)(2,1)}), bf16[8,4,128,384]{3,2,1,0:T(8,128)(2,1)S(1)}, u32[]{:S(2)}, u32[]{:S(2)}) async-start(bf16[8,4,128,384]{3,2,1,0:T(8,128)(2,1)} %bitcast.116), calls=%async_computation.4 | async-start | bytes 6291456 | tf_op jit(solution)/shard_map/all_to_all | solution.py:17
  150.4 19.3 %copy-start.6 = (bf16[8,80,1024]{2,1,0:T(8,128)(2,1)S(1)}, bf16[8,80,1024]{2,1,0:T(8,128)(2,1)}, u32[]{:S(2)}) copy-start(bf16[8,80,1024]{2,1,0:T(8,128)(2,1)} %copy-done.5) | copy-start | bytes 3932164
  150.4 19.3 %copy-start.11 = (bf16[640,1024]{1,0:T(8,128)(2,1)S(1)}, bf16[640,1024]{1,0:T(8,128)(2,1)}, u32[]{:S(2)}) copy-start(bf16[640,1024]{1,0:T(8,128)(2,1)} %copy-done.10) | copy-start | bytes 3932164
  151.7 17.9 %collective-permute-start.10 = (bf16[320,1024]{1,0:T(8,128)(2,1)S(1)}, bf16[320,1024]{1,0:T(8,128)(2,1)S(1)}, u32[]{:S(2)}, u32[]{:S(2)}) collective-permute-start(bf16[320,1024]{1,0:T(8,128)(2,1)S(1)} %slice.51), channel_id=1, source_target_pairs={{0,1},{1,2},{2,3},{3,0},{4,5},{5,6},{6,7},{7,4},{8,9},{9,10},{10,1... | collective-permute-start | bytes 1966088 | tf_op jit(solution)/shard_map/ppermute | solution.py:226
  153.5 16.1 %collective-permute-start.11 = (bf16[320,1024]{1,0:T(8,128)(2,1)S(1)}, bf16[320,1024]{1,0:T(8,128)(2,1)S(1)}, u32[]{:S(2)}, u32[]{:S(2)}) collective-permute-start(bf16[320,1024]{1,0:T(8,128)(2,1)S(1)} %slice.52), channel_id=1, source_target_pairs={{0,3},{1,0},{2,1},{3,2},{4,7},{5,4},{6,5},{7,6},{8,11},{9,8},{10,9... | collective-permute-start | bytes 1966088 | tf_op jit(solution)/shard_map/ppermute | solution.py:227
  188.2 1.7 copy-start.2
  188.2 8.0 %slice-start = ((bf16[8,96,1024]{2,1,0:T(8,128)(2,1)}), bf16[8,16,1024]{2,1,0:T(8,128)(2,1)S(1)}, s32[]{:S(2)}) async-start(bf16[8,96,1024]{2,1,0:T(8,128)(2,1)} %copy-done.3), calls=%async_computation.15 | async-start | bytes 524288 | tf_op jit(solution)/shard_map/slice | solution.py:235
  189.8 42.7 %all-to-all-start.5 = ((bf16[8,4,128,384]{3,2,1,0:T(8,128)(2,1)}), bf16[8,4,128,384]{3,2,1,0:T(8,128)(2,1)}, u32[]{:S(2)}, u32[]{:S(2)}) async-start(bf16[8,4,128,384]{3,2,1,0:T(8,128)(2,1)} %bitcast.115), calls=%async_computation.5 | async-start | bytes 6291456 | tf_op jit(solution)/shard_map/all_to_all | solution.py:17
  194.9 111.5 %all-gather.12.cloned.1.call-start = ((), (), s32[]{:S(2)}) async-start(), calls=%async_computation.14 | async-start | bytes 4423680 | tf_op jit(solution)/shard_map/all_gather | solution.py:262
  203.8 1.7 copy-start.7
  235.0 1.7 copy-start.8
  242.9 104.0 %reduce-scatter.2.cloned.1.call-start = ((), (), s32[]{:S(2)}) async-start(), calls=%async_computation.13 | async-start | bytes 2621440 | tf_op jit(solution)/shard_map/reduce_scatter | solution.py:276
  317.8 41.9 %copy-start.4 = (bf16[8,2,128,384]{3,2,1,0:T(8,128)(2,1)S(1)}, bf16[8,2,128,384]{3,2,1,0:T(8,128)(2,1)}, u32[]{:S(2)}) copy-start(bf16[8,2,128,384]{3,2,1,0:T(8,128)(2,1)} %all_to_all.48) | copy-start | bytes 4718596
  317.8 31.0 %all-to-all-start.7 = ((bf16[8,2,128,384]{3,2,1,0:T(8,128)(2,1)}), bf16[8,2,128,384]{3,2,1,0:T(8,128)(2,1)S(1)}, u32[]{:S(2)}, u32[]{:S(2)}) async-start(bf16[8,2,128,384]{3,2,1,0:T(8,128)(2,1)} %get-tuple-element.47), calls=%async_computation.7 | async-start | bytes 3145728 | tf_op jit(solution)/shard_map/all_to_all | solution.py:17
  348.9 28.4 %all-to-all-start.8 = ((bf16[64,32,128]{2,1,0:T(8,128)(2,1)}), bf16[64,32,128]{2,1,0:T(8,128)(2,1)}, u32[]{:S(2)}, u32[]{:S(2)}) async-start(bf16[64,32,128]{2,1,0:T(8,128)(2,1)} %bitcast.134), calls=%async_computation.9 | async-start | bytes 1048576 | tf_op jit(solution)/shard_map/all_to_all | solution.py:17
  359.7 19.4 %copy-start.1 = (bf16[2,16,4096]{2,1,0:T(8,128)(2,1)S(1)}, bf16[2,16,4096]{2,1,0:T(8,128)(2,1)}, u32[]{:S(2)}) copy-start(bf16[2,16,4096]{2,1,0:T(8,128)(2,1)} %param.8) | copy-start | bytes 786436
Sparse Core Ops, SparseCore 0:
  27.4 80.4 all-gather.5
  109.6 73.0 all-gather.7
  184.5 73.0 all-gather.9
  259.9 46.4 all-gather.11
  317.9 28.9 reduce-scatter.1

commit v4 on v2

--- a/solution.py
+++ b/solution.py
@@ -267,13 +267,16 @@
         PLANE, PLANE, capacity, width
     )
     down_rows = down_ring.pick(chosen).reshape(PLANE, part_count, block_rows, width)
-    serve_down = assemble(exchange(down_rows, XC))
+    early_rows, plane_hidden = lax.optimization_barrier((down_rows[:, :1], plane_hidden))
+    arrived_down = [exchange(early_rows, XC), exchange(down_rows[:, 1:], XC)]
     partial_value = jnp.einsum(
         "slpf,syrf->slpyr", plane_hidden, down_rows, preferred_element_type=jnp.float32
     ).astype(jnp.bfloat16)
     plane_out = jnp.einsum(
         "lspt,slpyr->yltr", placing, partial_value, preferred_element_type=jnp.float32
     ).astype(jnp.bfloat16)
+    plane_out, arrived_down[0] = lax.optimization_barrier((plane_out, arrived_down[0]))
+    serve_down = assemble(jnp.concatenate(arrived_down, axis=1))
     line_out = lax.psum_scatter(
         plane_out.reshape(-1, block_rows), "y", scatter_dimension=0, tiled=True
     )

time: 377 us -> 383 us (1.016)
  local copies, waits for them, and re-layouts: 49.3 us -> 54.8 us
  waiting for transfers between devices: 159 us -> 154 us
  starting transfers between devices: 67.9 us -> 72.5 us
    all_to_all x6 -> x7, starting transfers between devices: 38.3 us -> 42.9 us  [exchange(): return lax.all_to_all(value, axes, split_axis=0, concat_axis=0, tiled=True)]
    slice x0 -> x2, local copies, waits for them, and re-layouts: none -> 3.97 us  [the longest x1 2.29 us: body(): down_rows[:, :1]]
    optimization_barrier x0 -> x1, local copies, waits for them, and re-layouts: none -> 3.94 us  [body(): lax.optimization_barrier((plane_out, arrived_down[0]))]
    all_to_all x6 -> x7, waiting for transfers between devices: 36.6 us -> 33.8 us  [exchange(): return lax.all_to_all(value, axes, split_axis=0, concat_axis=0, tiled=True)]
    unnamed x67 -> x69, local copies, waits for them, and re-layouts: 11.5 us -> 11.5 us
  transfers between devices with their start and end apart: 30 -> 31, of which waited for: 19 -> 20; matrix products, arithmetic and copies ran while one was open for 14% -> 17% of each run, Pallas kernels for 2% -> 2%
where the time goes in v4:
time: 383 us; the launch traced here: 381 us
  waiting for transfers between devices  154 us (40%)
  starting transfers between devices  72.5 us (19%)
  local copies, waits for them, and re-layouts  54.8 us (14%)
  blocking collectives  43.1 us (11%)
  matrix products  22.2 us (6%)
  between operations  14.3 us (4%)
  other arithmetic  12.9 us (3%)
  Pallas kernels  7.04 us (2%)
    ppermute x16, waiting for transfers between devices, shift(): return lax.ppermute(value, 'z', [(i, (i + step) % Z) for i in range(Z)])  56.9 us
    all_to_all x2, blocking collectives, exchange(): return lax.all_to_all(value, axes, split_axis=0, concat_axis=0, tiled=True)  43.1 us
    all_to_all x7, starting transfers between devices, exchange(): return lax.all_to_all(value, axes, split_axis=0, concat_axis=0, tiled=True)  42.9 us
    all_to_all x7, waiting for transfers between devices, exchange(): return lax.all_to_all(value, axes, split_axis=0, concat_axis=0, tiled=True)  33.8 us
    reduce_scatter x1, waiting for transfers between devices, body(): lax.psum_scatter(plane_out.reshape(-1, block_rows), 'y', scatter_dimensio...  23.8 us
    ppermute x16, starting transfers between devices, shift(): return lax.ppermute(value, 'z', [(i, (i + step) % Z) for i in range(Z)])  23.8 us
    ppermute x1, waiting for transfers between devices, body(): from_next = lax.ppermute(quarters, 'y', to_last)  21.2 us
    gather x6, local copies, waits for them, and re-layouts, take_rows(): return value.at[index].get(mode='promise_in_bounds')  18.6 us
  transfers between devices with their start and end apart: 31, of which 20 were waited for; matrix products, arithmetic and copies ran while one was open for 17% of the time, Pallas kernels for 2%

profile of v4, /device:TPU:1, one launch (start us, length us, event | category | flops | bytes accessed | tf_op | source)
XLA Modules:
  0.0 381.3 jit_solution(4414584975351846778)
XLA Ops:
  7.2 6.8 %all-to-all-start = ((bf16[8,128,384]{2,1,0:T(8,128)(2,1)}), bf16[8,128,384]{2,1,0:T(8,128)(2,1)S(1)}, u32[]{:S(2)}, u32[]{:S(2)}) async-start(bf16[8,128,384]{2,1,0:T(8,128)(2,1)} %bitcast.137), calls=%async_computation | async-start | bytes 1572864 | tf_op jit(solution)/shard_map/all_to_all | solution.py:17
  16.1 10.2 %all-to-all-done = bf16[8,128,384]{2,1,0:T(8,128)(2,1)S(1)} async-done(((bf16[8,128,384]{2,1,0:T(8,128)(2,1)}), bf16[8,128,384]{2,1,0:T(8,128)(2,1)S(1)}, u32[]{:S(2)}, u32[]{:S(2)}) %all-to-all-start) | async-done | bytes 786464 | tf_op jit(solution)/shard_map/all_to_all | solution.py:17
  27.3 16.2 %all_to_all.45 = bf16[8,128,384]{2,1,0:T(8,128)(2,1)} all-to-all(bf16[8,128,384]{2,1,0:T(8,128)(2,1)S(1)} %bitcast.138), channel_id=1, replica_groups=mesh['z'=8,'x'=4,'c'=2,'y'=4] {'x','c'}, dimensions={0} | all-to-all | bytes 1572864 | tf_op jit(solution)/shard_map/all_to_all | solution.py:17
  44.6 4.0 %collective-permute-start = (bf16[2,16,1152]{2,1,0:T(8,128)(2,1)S(1)}, bf16[2,16,1152]{2,1,0:T(8,128)(2,1)S(1)}, u32[]{:S(2)}, u32[]{:S(2)}) collective-permute-start(bf16[2,16,1152]{2,1,0:T(8,128)(2,1)S(1)} %bitcast.141), channel_id=1, source_target_pairs={{0,224},{32,0},{64,32},{96,64},{128,96},{160,128},{192,160},{224,1... | collective-permute-start | bytes 221192 | tf_op jit(solution)/shard_map/ppermute | solution.py:21
  48.7 3.9 %collective-permute-done.3.refs_8_ = bf16[2,16,1152]{2,1,0:T(8,128)(2,1)S(1)} collective-permute-done((bf16[2,16,1152]{2,1,0:T(8,128)(2,1)S(1)}, bf16[2,16,1152]{2,1,0:T(8,128)(2,1)S(1)}, u32[]{:S(2)}, u32[]{:S(2)}) %collective-permute-start.3) | collective-permute-done | bytes 73760 | tf_op jit(solution)/shard_map/ppermute | solution.py:21
  52.7 2.7 collective-permute-start.1
  55.4 3.7 collective-permute-done.4.refs_7_
  59.2 2.7 collective-permute-start.2
  61.9 3.7 collective-permute-done.5.refs_6_
  65.6 2.7 collective-permute-start.7
  69.2 1.6 collective-permute-done.6.refs_4_
  72.0 2.7 pick_pieces.2
  76.4 1.6 convolution_convert_fusion
  78.2 27.0 %all_to_all.46 = bf16[8,96,1024]{2,1,0:T(8,128)(2,1)S(1)} all-to-all(bf16[8,96,1024]{2,1,0:T(8,128)(2,1)S(1)} %pad_maximum_fusion.1), channel_id=1, replica_groups=mesh['z'=8,'x'=4,'c'=2,'y'=4] {'x','c'}, dimensions={0} | all-to-all | bytes 3145728 | tf_op jit(solution)/shard_map/all_to_all | solution.py:17
  105.1 1.1 copy-done.4
  106.4 2.8 collective-permute-start.9
  109.2 4.7 %all-to-all-start.4 = ((bf16[8,128,384]{2,1,0:T(8,128)(2,1)}), bf16[8,128,384]{2,1,0:T(8,128)(2,1)S(1)}, u32[]{:S(2)}, u32[]{:S(2)}) async-start(bf16[8,128,384]{2,1,0:T(8,128)(2,1)} %bitcast.21), calls=%async_computation.4 | async-start | bytes 1572864 | tf_op jit(solution)/shard_map/all_to_all | solution.py:17
  115.1 21.2 %collective-permute-done.9 = bf16[640,1024]{1,0:T(8,128)(2,1)} collective-permute-done((bf16[640,1024]{1,0:T(8,128)(2,1)S(1)}, bf16[640,1024]{1,0:T(8,128)(2,1)}, u32[]{:S(2)}, u32[]{:S(2)}) %collective-permute-start.9) | collective-permute-done | bytes 1310752 | tf_op jit(solution)/shard_map/ppermute | solution.py:221
  136.3 3.2 collective-permute-done.8
  139.6 5.5 %gather_fusion.1 = bf16[32,128,384]{2,1,0:T(8,128)(2,1)} fusion(bf16[64,128,384]{2,1,0:T(8,128)(2,1)} %bitcast.136, s32[1024]{0:T(1024)S(1)} %pad_clamp_fusion.1), kind=kCustom, calls=%fused_computation.1 | custom fusion | bytes 6291584 | tf_op jit(solution)/shard_map/gather | solution.py:109
  145.9 5.7 %all-to-all-start.3 = ((bf16[8,4,128,384]{3,2,1,0:T(8,128)(2,1)}), bf16[8,4,128,384]{3,2,1,0:T(8,128)(2,1)S(1)}, u32[]{:S(2)}, u32[]{:S(2)}) async-start(bf16[8,4,128,384]{3,2,1,0:T(8,128)(2,1)} %bitcast.117), calls=%async_computation.3 | async-start | bytes 6291456 | tf_op jit(solution)/shard_map/all_to_all | solution.py:17
  151.7 1.2 slice.58
  152.9 1.1 slice.57
  154.4 2.7 collective-permute-start.11
  157.1 14.9 %collective-permute-done.10 = bf16[320,1024]{1,0:T(8,128)(2,1)S(1)} collective-permute-done((bf16[320,1024]{1,0:T(8,128)(2,1)S(1)}, bf16[320,1024]{1,0:T(8,128)(2,1)S(1)}, u32[]{:S(2)}, u32[]{:S(2)}) %collective-permute-start.10) | collective-permute-done | bytes 655392 | tf_op jit(solution)/shard_map/ppermute | solution.py:224
  172.1 4.6 %pad_maximum_fusion = bf16[4,640,1024]{2,1,0:T(8,128)(2,1)} fusion(bf16[1,640,1024]{2,1,0:T(8,128)(2,1)} %bitcast.23, bf16[1,640,1024]{2,1,0:T(8,128)(2,1)S(1)} %maximum_bitcast_fusion.1, bf16[1,640,1024]{2,1,0:T(8,128)(2,1)} %bitcast.20, bf16[1,640,1024]{2,1,0:T(8,128)(2,1)S(1)} %bitcast.124), kind=kLoop, calls=%fused_computation.5 | loop fusion | flops 7864320 | bytes 10485760 | tf_op jit(solution)/shard_map/stack | solution.py:229
  176.7 5.7 %gather_fusion.2 = bf16[4,640,1024]{2,1,0:T(8,128)(2,1)} fusion(bf16[4,640,1024]{2,1,0:T(8,128)(2,1)} %pad_maximum_fusion, s32[1024]{0:T(1024)S(1)} %pad_clamp_fusion), kind=kCustom, calls=%fused_computation.2 | custom fusion | bytes 10485776 | tf_op jit(solution)/shard_map/gather | solution.py:109
  182.7 5.4 %gather_fusion.3 = bf16[32,128,384]{2,1,0:T(8,128)(2,1)} fusion(bf16[64,128,384]{2,1,0:T(8,128)(2,1)} %bitcast.135, s32[1024]{0:T(1024)S(1)} %pad_clamp_fusion.1), kind=kCustom, calls=%fused_computation.3 | custom fusion | bytes 6291584 | tf_op jit(solution)/shard_map/gather | solution.py:109
  188.2 1.1 all-to-all-done.3
  189.3 1.7 copy-done.2
  190.9 5.2 %all-to-all-start.5 = ((bf16[8,4,128,384]{3,2,1,0:T(8,128)(2,1)}), bf16[8,4,128,384]{3,2,1,0:T(8,128)(2,1)}, u32[]{:S(2)}, u32[]{:S(2)}) async-start(bf16[8,4,128,384]{3,2,1,0:T(8,128)(2,1)} %bitcast.116), calls=%async_computation.5 | async-start | bytes 6291456 | tf_op jit(solution)/shard_map/all_to_all | solution.py:17
  199.7 2.5 collective-permute-start.13
  204.6 1.3 fusion.2
  205.9 13.1 %collective-permute-done.13.refs_1_ = bf16[8,128,384]{2,1,0:T(8,128)(2,1)S(1)} collective-permute-done((bf16[8,128,384]{2,1,0:T(8,128)(2,1)S(1)}, bf16[8,128,384]{2,1,0:T(8,128)(2,1)S(1)}, u32[]{:S(2)}, u32[]{:S(2)}) %collective-permute-start.13) | collective-permute-done | bytes 786464 | tf_op jit(solution)/shard_map/ppermute | solution.py:21
  219.0 3.2 collective-permute-done.12.refs_8_
  222.2 2.7 collective-permute-start.15
  225.2 2.4 copy.88
  227.6 1.7 copy-done.9
  229.3 6.3 %convolution_bitcast_fusion.1 = f32[640,384]{1,0:T(8,128)} fusion(bf16[4,640,1024]{2,1,0:T(8,128)(2,1)} %gather_fusion.2, bf16[4,1024,384]{2,1,0:T(8,128)(2,1)S(1)} %bitcast.125), kind=kOutput, calls=%fused_computation.23 | convolution fusion | flops 2013265920 | bytes 9371648 | tf_op jit(solution)/shard_map/ymd,ydf->mf/dot_general | solution.py:251
  235.6 5.7 %collective-permute-done.14.refs_7_ = bf16[8,128,384]{2,1,0:T(8,128)(2,1)S(1)} collective-permute-done((bf16[8,128,384]{2,1,0:T(8,128)(2,1)S(1)}, bf16[8,128,384]{2,1,0:T(8,128)(2,1)S(1)}, u32[]{:S(2)}, u32[]{:S(2)}) %collective-permute-start.14) | collective-permute-done | bytes 786464 | tf_op jit(solution)/shard_map/ppermute | solution.py:21
  241.2 2.7 copy.90
  244.0 1.7 copy-done.10
  245.6 6.3 %fusion.19 = bf16[640,384]{1,0:T(8,128)(2,1)} fusion(bf16[4,640,1024]{2,1,0:T(8,128)(2,1)} %gather_fusion.2, bf16[4,1024,384]{2,1,0:T(8,128)(2,1)S(1)} %bitcast.127, f32[640,384]{1,0:T(8,128)S(1)} %copy-done.32, f32[640]{0:T(1024)S(1)} %mul.54), kind=kOutput, calls=%fused_computation.25 | convolution fusion | flops 2014986240 | bytes 9865728 | tf_op jit(solution)/shard_map/ymd,ydf->mf/dot_general | solution.py:259
  252.0 2.3 collective-permute-start.16
  254.3 14.9 %collective-permute-done.16.refs_3_ = bf16[8,128,384]{2,1,0:T(8,128)(2,1)S(1)} collective-permute-done((bf16[8,128,384]{2,1,0:T(8,128)(2,1)}, bf16[8,128,384]{2,1,0:T(8,128)(2,1)S(1)}, u32[]{:S(2)}, u32[]{:S(2)}) %collective-permute-start.16) | collective-permute-done | bytes 786464 | tf_op jit(solution)/shard_map/ppermute | solution.py:21
  269.3 3.3 collective-permute-start.19
  272.8 1.2 gather_fusion.4
  274.0 3.8 collective-permute-done.19.refs_5_
  277.8 3.4 collective-permute-done.18.refs_4_
  281.9 4.4 %pick_pieces.3 = bf16[32,128,384]{2,1,0:T(8,128)(2,1)} custom-call(s32[32]{0:T(128)} %gather_fusion.4, bf16[8,128,384]{2,1,0:T(8,128)(2,1)} %copy-done.7, bf16[8,128,384]{2,1,0:T(8,128)(2,1)} %copy-done.14, bf16[8,128,384]{2,1,0:T(8,128)(2,1)} %collective-permute-done.15.refs_2_, bf16[8,128,384]{2,1,0:T(8,128)(2,1)} %copy-done.12, ...), custom_call_target="tpu_custom_call" | custom-call | tf_op jit(solution)/shard_map/pick_pieces/pallas_call | solution.py:93
  286.3 2.3 slice.86
  288.6 8.3 %all-to-all-start.6 = ((bf16[8,1,128,384]{3,2,1,0:T(8,128)(2,1)}), bf16[8,1,128,384]{3,2,1,0:T(8,128)(2,1)}, u32[]{:S(2)}, u32[]{:S(2)}) async-start(bf16[8,1,128,384]{3,2,1,0:T(8,128)(2,1)} %slice.86), calls=%async_computation.6 | async-start | bytes 1572864 | tf_op jit(solution)/shard_map/all_to_all | solution.py:17
  296.9 7.5 %fusion.12 = bf16[4,8,256,128]{2,3,0,1:T(8,128)(2,1)} fusion(s32[8,8,256]{2,1,0:T(8,128)S(1)} %add_select_fusion, pred[8,8,256]{2,1,0:T(8,128)(4,1)S(1)} %fusion.29, bf16[8,4,128,384]{3,2,1,0:T(8,128)(2,1)S(1)} %bitcast.119, bf16[8,8,80,384]{3,2,1,0:T(8,128)(2,1)} %bitcast.144), kind=kOutput, calls=%fused_computation.17 | convolution fusion | flops 3361734656 | bytes 9256960 | tf_op jit(solution)/shard_map/lspt,slpyr->yltr/dot_general | solution.py:275
  304.4 4.9 %all-to-all-done.6 = bf16[8,1,128,384]{3,2,1,0:T(8,128)(2,1)} async-done(((bf16[8,1,128,384]{3,2,1,0:T(8,128)(2,1)}), bf16[8,1,128,384]{3,2,1,0:T(8,128)(2,1)}, u32[]{:S(2)}, u32[]{:S(2)}) %all-to-all-start.6) | async-done | bytes 786464 | tf_op jit(solution)/shard_map/all_to_all | solution.py:17
  309.3 3.9 %copy.96 = bf16[4,8,256,128]{3,2,1,0:T(8,128)(2,1)} copy(bf16[4,8,256,128]{2,3,0,1:T(8,128)(2,1)} %fusion.12) | data formatting | bytes 4194304 | tf_op jit(solution)/shard_map/optimization_barrier | solution.py:278
  313.3 1.7 slice.92
  314.9 4.4 %all-to-all-start.7 = ((bf16[8,3,128,384]{3,2,1,0:T(8,128)(2,1)}), bf16[8,3,128,384]{3,2,1,0:T(8,128)(2,1)S(1)}, u32[]{:S(2)}, u32[]{:S(2)}) async-start(bf16[8,3,128,384]{3,2,1,0:T(8,128)(2,1)} %slice.92), calls=%async_computation.7 | async-start | bytes 4718592 | tf_op jit(solution)/shard_map/all_to_all | solution.py:17
  319.3 23.8 %reduce-scatter.2.cloned.1.call-done = bf16[2048,128]{1,0:T(8,128)(2,1)} async-done(((bf16[8192,128]{1,0:T(8,128)(2,1)}), bf16[2048,128]{1,0:T(8,128)(2,1)}) %reduce-scatter.2.cloned.1.call-update) | async-done | bytes 524304 | tf_op jit(solution)/shard_map/reduce_scatter | solution.py:280
  343.2 1.9 copy.97
  345.1 3.4 all-to-all-done.7
  348.5 7.7 %all-to-all-start.8 = ((bf16[64,32,128]{2,1,0:T(8,128)(2,1)}), bf16[64,32,128]{2,1,0:T(8,128)(2,1)S(1)}, u32[]{:S(2)}, u32[]{:S(2)}) async-start(bf16[64,32,128]{2,1,0:T(8,128)(2,1)} %bitcast.50), calls=%async_computation.9 | async-start | bytes 1048576 | tf_op jit(solution)/shard_map/all_to_all | solution.py:17
  356.2 1.5 maximum_bitcast_fusion
  357.8 2.0 copy.95
  359.8 14.2 %all-to-all-done.8 = bf16[64,32,128]{2,1,0:T(8,128)(2,1)S(1)} async-done(((bf16[64,32,128]{2,1,0:T(8,128)(2,1)}), bf16[64,32,128]{2,1,0:T(8,128)(2,1)S(1)}, u32[]{:S(2)}, u32[]{:S(2)}) %all-to-all-start.8) | async-done | bytes 524320 | tf_op jit(solution)/shard_map/all_to_all | solution.py:17
  (160 shorter events, 19.1 us)
Async XLA Ops:
  7.2 8.9 %copy-start = (bf16[2,16,4096]{2,1,0:T(8,128)(2,1)S(1)}, bf16[2,16,4096]{2,1,0:T(8,128)(2,1)}, u32[]{:S(2)}) copy-start(bf16[2,16,4096]{2,1,0:T(8,128)(2,1)} %param.8) | copy-start | bytes 786436
  7.2 20.1 %copy-start.18 = (bf16[1,1024,384]{2,1,0:T(8,128)(2,1)S(1)}, bf16[1,1024,384]{2,1,0:T(8,128)(2,1)}, u32[]{:S(2)}) copy-start(bf16[1,1024,384]{2,1,0:T(8,128)(2,1)} %param.14) | copy-start | bytes 2359300
  7.2 36.3 %copy-start.30 = (s32[64]{0:T(128)S(1)}, s32[64]{0:T(128)}, u32[]{:S(2)}) copy-start(s32[64]{0:T(128)} %param.12) | copy-start | bytes 772
  7.2 19.1 %all-to-all-start = ((bf16[8,128,384]{2,1,0:T(8,128)(2,1)}), bf16[8,128,384]{2,1,0:T(8,128)(2,1)S(1)}, u32[]{:S(2)}, u32[]{:S(2)}) async-start(bf16[8,128,384]{2,1,0:T(8,128)(2,1)} %bitcast.137), calls=%async_computation | async-start | bytes 1572864 | tf_op jit(solution)/shard_map/all_to_all | solution.py:17
  14.0 125.5 %all-gather.5.cloned.1.call-start = ((), (), s32[]{:S(2)}) async-start(), calls=%async_computation.10 | async-start | bytes 7077888 | tf_op jit(solution)/shard_map/all_gather | solution.py:150
  26.3 0.9 copy-start.11
  27.2 155.5 %all-gather.7.cloned.1.call-start = ((), (), s32[]{:S(2)}) async-start(), calls=%async_computation.11 | async-start | bytes 7077888 | tf_op jit(solution)/shard_map/all_gather | solution.py:150
  43.8 26.9 %copy-start.21 = (bf16[32,1152]{1,0:T(8,128)(2,1)}, bf16[32,1152]{1,0:T(8,128)(2,1)S(1)}, u32[]{:S(2)}) copy-start(bf16[32,1152]{1,0:T(8,128)(2,1)S(1)} %pad.4) | copy-start | bytes 221188
  43.8 8.8 %collective-permute-start.3 = (bf16[2,16,1152]{2,1,0:T(8,128)(2,1)S(1)}, bf16[2,16,1152]{2,1,0:T(8,128)(2,1)S(1)}, u32[]{:S(2)}, u32[]{:S(2)}) collective-permute-start(bf16[2,16,1152]{2,1,0:T(8,128)(2,1)S(1)} %bitcast.140), channel_id=1, source_target_pairs={{0,32},{32,64},{64,96},{96,128},{128,160},{160,192},{192,224},{224... | collective-permute-start | bytes 221192 | tf_op jit(solution)/shard_map/ppermute | solution.py:21
  44.6 8.0 %collective-permute-start = (bf16[2,16,1152]{2,1,0:T(8,128)(2,1)S(1)}, bf16[2,16,1152]{2,1,0:T(8,128)(2,1)S(1)}, u32[]{:S(2)}, u32[]{:S(2)}) collective-permute-start(bf16[2,16,1152]{2,1,0:T(8,128)(2,1)S(1)} %bitcast.141), channel_id=1, source_target_pairs={{0,224},{32,0},{64,32},{96,64},{128,96},{160,128},{192,160},{224,1... | collective-permute-start | bytes 221192 | tf_op jit(solution)/shard_map/ppermute | solution.py:21
  52.7 18.1 %copy-start.24 = (bf16[2,16,1152]{2,1,0:T(8,128)(2,1)}, bf16[2,16,1152]{2,1,0:T(8,128)(2,1)S(1)}, u32[]{:S(2)}) copy-start(bf16[2,16,1152]{2,1,0:T(8,128)(2,1)S(1)} %collective-permute-done.3.refs_8_) | copy-start | bytes 221188
  52.7 6.5 %collective-permute-start.4 = (bf16[2,16,1152]{2,1,0:T(8,128)(2,1)S(1)}, bf16[2,16,1152]{2,1,0:T(8,128)(2,1)S(1)}, u32[]{:S(2)}, u32[]{:S(2)}) collective-permute-start(bf16[2,16,1152]{2,1,0:T(8,128)(2,1)S(1)} %collective-permute-done.3.refs_8_), channel_id=1, source_target_pairs={{0,32},{32,64},{64,96},{96,128},{128,160},{160,192},{192,224},{224... | collective-permute-start | bytes 221192 | tf_op jit(solution)/shard_map/ppermute | solution.py:21
  52.7 18.1 %copy-start.25 = (bf16[2,16,1152]{2,1,0:T(8,128)(2,1)}, bf16[2,16,1152]{2,1,0:T(8,128)(2,1)S(1)}, u32[]{:S(2)}) copy-start(bf16[2,16,1152]{2,1,0:T(8,128)(2,1)S(1)} %collective-permute-done.refs_1_) | copy-start | bytes 221188
  52.7 6.5 %collective-permute-start.1 = (bf16[2,16,1152]{2,1,0:T(8,128)(2,1)S(1)}, bf16[2,16,1152]{2,1,0:T(8,128)(2,1)S(1)}, u32[]{:S(2)}, u32[]{:S(2)}) collective-permute-start(bf16[2,16,1152]{2,1,0:T(8,128)(2,1)S(1)} %collective-permute-done.refs_1_), channel_id=1, source_target_pairs={{0,224},{32,0},{64,32},{96,64},{128,96},{160,128},{192,160},{224,1... | collective-permute-start | bytes 221192 | tf_op jit(solution)/shard_map/ppermute | solution.py:21
  59.2 11.6 %copy-start.26 = (bf16[2,16,1152]{2,1,0:T(8,128)(2,1)}, bf16[2,16,1152]{2,1,0:T(8,128)(2,1)S(1)}, u32[]{:S(2)}) copy-start(bf16[2,16,1152]{2,1,0:T(8,128)(2,1)S(1)} %collective-permute-done.4.refs_7_) | copy-start | bytes 221188
  59.2 6.4 %collective-permute-start.5 = (bf16[2,16,1152]{2,1,0:T(8,128)(2,1)S(1)}, bf16[2,16,1152]{2,1,0:T(8,128)(2,1)S(1)}, u32[]{:S(2)}, u32[]{:S(2)}) collective-permute-start(bf16[2,16,1152]{2,1,0:T(8,128)(2,1)S(1)} %collective-permute-done.4.refs_7_), channel_id=1, source_target_pairs={{0,32},{32,64},{64,96},{96,128},{128,160},{160,192},{192,224},{224... | collective-permute-start | bytes 221192 | tf_op jit(solution)/shard_map/ppermute | solution.py:21
  59.2 11.6 %copy-start.27 = (bf16[2,16,1152]{2,1,0:T(8,128)(2,1)}, bf16[2,16,1152]{2,1,0:T(8,128)(2,1)S(1)}, u32[]{:S(2)}) copy-start(bf16[2,16,1152]{2,1,0:T(8,128)(2,1)S(1)} %collective-permute-done.1.refs_2_) | copy-start | bytes 221188
  59.2 6.4 %collective-permute-start.2 = (bf16[2,16,1152]{2,1,0:T(8,128)(2,1)S(1)}, bf16[2,16,1152]{2,1,0:T(8,128)(2,1)S(1)}, u32[]{:S(2)}, u32[]{:S(2)}) collective-permute-start(bf16[2,16,1152]{2,1,0:T(8,128)(2,1)S(1)} %collective-permute-done.1.refs_2_), channel_id=1, source_target_pairs={{0,224},{32,0},{64,32},{96,64},{128,96},{160,128},{192,160},{224,1... | collective-permute-start | bytes 221192 | tf_op jit(solution)/shard_map/ppermute | solution.py:21
  65.5 5.2 %copy-start.22 = (bf16[2,16,1152]{2,1,0:T(8,128)(2,1)}, bf16[2,16,1152]{2,1,0:T(8,128)(2,1)S(1)}, u32[]{:S(2)}) copy-start(bf16[2,16,1152]{2,1,0:T(8,128)(2,1)S(1)} %collective-permute-done.5.refs_6_) | copy-start | bytes 221188
  65.5 5.2 %collective-permute-start.6 = (bf16[1,16,1152]{2,1,0:T(8,128)(2,1)S(1)}, bf16[1,16,1152]{2,1,0:T(8,128)(2,1)S(1)}, u32[]{:S(2)}, u32[]{:S(2)}) collective-permute-start(bf16[1,16,1152]{2,1,0:T(8,128)(2,1)S(1)} %slice.78), channel_id=1, source_target_pairs={{0,32},{32,64},{64,96},{96,128},{128,160},{160,192},{192,224},{224... | collective-permute-start | bytes 110600 | tf_op jit(solution)/shard_map/ppermute | solution.py:21
  65.6 5.2 %copy-start.23 = (bf16[2,16,1152]{2,1,0:T(8,128)(2,1)}, bf16[2,16,1152]{2,1,0:T(8,128)(2,1)S(1)}, u32[]{:S(2)}) copy-start(bf16[2,16,1152]{2,1,0:T(8,128)(2,1)S(1)} %collective-permute-done.2.refs_3_) | copy-start | bytes 221188
  65.6 5.1 %collective-permute-start.7 = (bf16[1,16,1152]{2,1,0:T(8,128)(2,1)S(1)}, bf16[1,16,1152]{2,1,0:T(8,128)(2,1)S(1)}, u32[]{:S(2)}, u32[]{:S(2)}) collective-permute-start(bf16[1,16,1152]{2,1,0:T(8,128)(2,1)S(1)} %slice.79), channel_id=1, source_target_pairs={{0,224},{32,0},{64,32},{96,64},{128,96},{160,128},{192,160},{224,1... | collective-permute-start | bytes 110600 | tf_op jit(solution)/shard_map/ppermute | solution.py:21
  70.7 0.6 copy-start.28
  71.3 0.6 copy-start.29
  78.2 36.0 %copy-start.31 = (s32[64]{0:T(128)S(1)}, s32[64]{0:T(128)}, u32[]{:S(2)}) copy-start(s32[64]{0:T(128)} %param.11) | copy-start | bytes 772
  105.1 1.1 copy-start.4
  106.4 38.6 %copy-start.5 = (bf16[8,80,1024]{2,1,0:T(8,128)(2,1)}, bf16[8,80,1024]{2,1,0:T(8,128)(2,1)S(1)}, u32[]{:S(2)}) copy-start(bf16[8,80,1024]{2,1,0:T(8,128)(2,1)S(1)} %slice.83) | copy-start | bytes 3932164
  106.4 29.9 %collective-permute-start.9 = (bf16[640,1024]{1,0:T(8,128)(2,1)S(1)}, bf16[640,1024]{1,0:T(8,128)(2,1)}, u32[]{:S(2)}, u32[]{:S(2)}) collective-permute-start(bf16[640,1024]{1,0:T(8,128)(2,1)S(1)} %bitcast.122), channel_id=1, source_target_pairs={{0,3},{1,0},{2,1},{3,2},{4,7},{5,4},{6,5},{7,6},{8,11},{9,8},{10,9... | collective-permute-start | bytes 3932168 | tf_op jit(solution)/shard_map/ppermute | solution.py:221
  109.2 30.3 %collective-permute-start.8 = (bf16[640,1024]{1,0:T(8,128)(2,1)S(1)}, bf16[640,1024]{1,0:T(8,128)(2,1)}, u32[]{:S(2)}, u32[]{:S(2)}) collective-permute-start(bf16[640,1024]{1,0:T(8,128)(2,1)S(1)} %bitcast.123), channel_id=1, source_target_pairs={{0,1},{1,2},{2,3},{3,0},{4,5},{5,6},{6,7},{7,4},{8,9},{9,10},{10,1... | collective-permute-start | bytes 3932168 | tf_op jit(solution)/shard_map/ppermute | solution.py:220
  109.2 35.8 %all-to-all-start.4 = ((bf16[8,128,384]{2,1,0:T(8,128)(2,1)}), bf16[8,128,384]{2,1,0:T(8,128)(2,1)S(1)}, u32[]{:S(2)}, u32[]{:S(2)}) async-start(bf16[8,128,384]{2,1,0:T(8,128)(2,1)} %bitcast.21), calls=%async_computation.4 | async-start | bytes 1572864 | tf_op jit(solution)/shard_map/all_to_all | solution.py:17
  145.1 0.9 copy-start.7
  145.9 43.3 %all-to-all-start.3 = ((bf16[8,4,128,384]{3,2,1,0:T(8,128)(2,1)}), bf16[8,4,128,384]{3,2,1,0:T(8,128)(2,1)S(1)}, u32[]{:S(2)}, u32[]{:S(2)}) async-start(bf16[8,4,128,384]{3,2,1,0:T(8,128)(2,1)} %bitcast.117), calls=%async_computation.3 | async-start | bytes 6291456 | tf_op jit(solution)/shard_map/all_to_all | solution.py:17
  151.7 20.4 %copy-start.6 = (bf16[8,80,1024]{2,1,0:T(8,128)(2,1)S(1)}, bf16[8,80,1024]{2,1,0:T(8,128)(2,1)}, u32[]{:S(2)}) copy-start(bf16[8,80,1024]{2,1,0:T(8,128)(2,1)} %copy-done.5) | copy-start | bytes 3932164
  154.1 17.9 %collective-permute-start.10 = (bf16[320,1024]{1,0:T(8,128)(2,1)S(1)}, bf16[320,1024]{1,0:T(8,128)(2,1)S(1)}, u32[]{:S(2)}, u32[]{:S(2)}) collective-permute-start(bf16[320,1024]{1,0:T(8,128)(2,1)S(1)} %slice.57), channel_id=1, source_target_pairs={{0,1},{1,2},{2,3},{3,0},{4,5},{5,6},{6,7},{7,4},{8,9},{9,10},{10,1... | collective-permute-start | bytes 1966088 | tf_op jit(solution)/shard_map/ppermute | solution.py:224
  154.4 17.6 %collective-permute-start.11 = (bf16[320,1024]{1,0:T(8,128)(2,1)S(1)}, bf16[320,1024]{1,0:T(8,128)(2,1)S(1)}, u32[]{:S(2)}, u32[]{:S(2)}) collective-permute-start(bf16[320,1024]{1,0:T(8,128)(2,1)S(1)} %slice.58), channel_id=1, source_target_pairs={{0,3},{1,0},{2,1},{3,2},{4,7},{5,4},{6,5},{7,6},{8,11},{9,8},{10,9... | collective-permute-start | bytes 1966088 | tf_op jit(solution)/shard_map/ppermute | solution.py:225
  189.3 1.7 copy-start.2
  190.9 44.6 %all-to-all-start.5 = ((bf16[8,4,128,384]{3,2,1,0:T(8,128)(2,1)}), bf16[8,4,128,384]{3,2,1,0:T(8,128)(2,1)}, u32[]{:S(2)}, u32[]{:S(2)}) async-start(bf16[8,4,128,384]{3,2,1,0:T(8,128)(2,1)} %bitcast.116), calls=%async_computation.5 | async-start | bytes 6291456 | tf_op jit(solution)/shard_map/all_to_all | solution.py:17
  196.1 3.6 copy-start.8
  196.1 92.4 %all-gather.9.cloned.1.call-start = ((), (), s32[]{:S(2)}) async-start(), calls=%async_computation.13 | async-start | bytes 4423680 | tf_op jit(solution)/shard_map/all_gather | solution.py:266
  199.7 19.3 %collective-permute-start.13 = (bf16[8,128,384]{2,1,0:T(8,128)(2,1)S(1)}, bf16[8,128,384]{2,1,0:T(8,128)(2,1)S(1)}, u32[]{:S(2)}, u32[]{:S(2)}) collective-permute-start(bf16[8,128,384]{2,1,0:T(8,128)(2,1)S(1)} %copy-done.8), channel_id=1, source_target_pairs={{0,224},{32,0},{64,32},{96,64},{128,96},{160,128},{192,160},{224,1... | collective-permute-start | bytes 2359304 | tf_op jit(solution)/shard_map/ppermute | solution.py:21
  202.3 19.9 %collective-permute-start.12 = (bf16[8,128,384]{2,1,0:T(8,128)(2,1)S(1)}, bf16[8,128,384]{2,1,0:T(8,128)(2,1)S(1)}, u32[]{:S(2)}, u32[]{:S(2)}) collective-permute-start(bf16[8,128,384]{2,1,0:T(8,128)(2,1)S(1)} %copy-done.8), channel_id=1, source_target_pairs={{0,32},{32,64},{64,96},{96,128},{128,160},{160,192},{192,224},{224... | collective-permute-start | bytes 2359304 | tf_op jit(solution)/shard_map/ppermute | solution.py:21
  219.0 8.6 %copy-start.14 = (bf16[8,128,384]{2,1,0:T(8,128)(2,1)}, bf16[8,128,384]{2,1,0:T(8,128)(2,1)S(1)}, u32[]{:S(2)}) copy-start(bf16[8,128,384]{2,1,0:T(8,128)(2,1)S(1)} %collective-permute-done.13.refs_1_) | copy-start | bytes 2359300
  222.2 5.4 %copy-start.15 = (bf16[8,128,384]{2,1,0:T(8,128)(2,1)}, bf16[8,128,384]{2,1,0:T(8,128)(2,1)S(1)}, u32[]{:S(2)}) copy-start(bf16[8,128,384]{2,1,0:T(8,128)(2,1)S(1)} %collective-permute-done.12.refs_8_) | copy-start | bytes 2359300
  222.2 19.0 %collective-permute-start.14 = (bf16[8,128,384]{2,1,0:T(8,128)(2,1)S(1)}, bf16[8,128,384]{2,1,0:T(8,128)(2,1)S(1)}, u32[]{:S(2)}, u32[]{:S(2)}) collective-permute-start(bf16[8,128,384]{2,1,0:T(8,128)(2,1)S(1)} %collective-permute-done.12.refs_8_), channel_id=1, source_target_pairs={{0,32},{32,64},{64,96},{96,128},{128,160},{160,192},{192,224},{224... | collective-permute-start | bytes 2359304 | tf_op jit(solution)/shard_map/ppermute | solution.py:21
  222.2 19.0 %collective-permute-start.15 = (bf16[8,128,384]{2,1,0:T(8,128)(2,1)S(1)}, bf16[8,128,384]{2,1,0:T(8,128)(2,1)}, u32[]{:S(2)}, u32[]{:S(2)}) collective-permute-start(bf16[8,128,384]{2,1,0:T(8,128)(2,1)S(1)} %collective-permute-done.13.refs_1_), channel_id=1, source_target_pairs={{0,224},{32,0},{64,32},{96,64},{128,96},{160,128},{192,160},{224,1... | collective-permute-start | bytes 2359304 | tf_op jit(solution)/shard_map/ppermute | solution.py:21
  227.6 1.7 copy-start.9
  241.2 2.7 copy-start.16
  241.2 4.4 %copy-start.32 = (f32[640,384]{1,0:T(8,128)S(1)}, f32[640,384]{1,0:T(8,128)}, u32[]{:S(2)}) copy-start(f32[640,384]{1,0:T(8,128)} %convolution_bitcast_fusion.1) | copy-start | bytes 2949124
  244.0 1.7 copy-start.10
  245.6 8.7 %copy-start.17 = (bf16[8,128,384]{2,1,0:T(8,128)(2,1)S(1)}, bf16[8,128,384]{2,1,0:T(8,128)(2,1)}, u32[]{:S(2)}) copy-start(bf16[8,128,384]{2,1,0:T(8,128)(2,1)} %copy-done.16) | copy-start | bytes 2359300
  252.0 17.3 %collective-permute-start.16 = (bf16[8,128,384]{2,1,0:T(8,128)(2,1)}, bf16[8,128,384]{2,1,0:T(8,128)(2,1)S(1)}, u32[]{:S(2)}, u32[]{:S(2)}) collective-permute-start(bf16[8,128,384]{2,1,0:T(8,128)(2,1)} %collective-permute-done.15.refs_2_), channel_id=1, source_target_pairs={{0,224},{32,0},{64,32},{96,64},{128,96},{160,128},{192,160},{224,1... | collective-permute-start | bytes 2359304 | tf_op jit(solution)/shard_map/ppermute | solution.py:21
  254.3 18.3 %collective-permute-start.17 = (bf16[8,128,384]{2,1,0:T(8,128)(2,1)S(1)}, bf16[8,128,384]{2,1,0:T(8,128)(2,1)S(1)}, u32[]{:S(2)}, u32[]{:S(2)}) collective-permute-start(bf16[8,128,384]{2,1,0:T(8,128)(2,1)S(1)} %copy-done.17), channel_id=1, source_target_pairs={{0,32},{32,64},{64,96},{96,128},{128,160},{160,192},{192,224},{224... | collective-permute-start | bytes 2359304 | tf_op jit(solution)/shard_map/ppermute | solution.py:21
  269.3 11.9 %copy-start.12 = (bf16[8,128,384]{2,1,0:T(8,128)(2,1)}, bf16[8,128,384]{2,1,0:T(8,128)(2,1)S(1)}, u32[]{:S(2)}) copy-start(bf16[8,128,384]{2,1,0:T(8,128)(2,1)S(1)} %collective-permute-done.16.refs_3_) | copy-start | bytes 2359300
  269.3 8.4 %collective-permute-start.19 = (bf16[4,128,384]{2,1,0:T(8,128)(2,1)S(1)}, bf16[4,128,384]{2,1,0:T(8,128)(2,1)S(1)}, u32[]{:S(2)}, u32[]{:S(2)}) collective-permute-start(bf16[4,128,384]{2,1,0:T(8,128)(2,1)S(1)} %slice.85), channel_id=1, source_target_pairs={{0,224},{32,0},{64,32},{96,64},{128,96},{160,128},{192,160},{224,1... | collective-permute-start | bytes 1179656 | tf_op jit(solution)/shard_map/ppermute | solution.py:21
  272.6 8.5 %copy-start.13 = (bf16[8,128,384]{2,1,0:T(8,128)(2,1)}, bf16[8,128,384]{2,1,0:T(8,128)(2,1)S(1)}, u32[]{:S(2)}) copy-start(bf16[8,128,384]{2,1,0:T(8,128)(2,1)S(1)} %collective-permute-done.17.refs_6_) | copy-start | bytes 2359300
  272.7 8.5 %collective-permute-start.18 = (bf16[4,128,384]{2,1,0:T(8,128)(2,1)S(1)}, bf16[4,128,384]{2,1,0:T(8,128)(2,1)S(1)}, u32[]{:S(2)}, u32[]{:S(2)}) collective-permute-start(bf16[4,128,384]{2,1,0:T(8,128)(2,1)S(1)} %slice.84), channel_id=1, source_target_pairs={{0,32},{32,64},{64,96},{96,128},{128,160},{160,192},{192,224},{224... | collective-permute-start | bytes 1179656 | tf_op jit(solution)/shard_map/ppermute | solution.py:21
  277.8 3.4 copy-start.19
  281.1 0.8 copy-start.20
  286.3 10.6 %copy-start.3 = (bf16[32,128,384]{2,1,0:T(8,128)(2,1)S(1)}, bf16[32,128,384]{2,1,0:T(8,128)(2,1)}, u32[]{:S(2)}) copy-start(bf16[32,128,384]{2,1,0:T(8,128)(2,1)} %pick_pieces.3) | copy-start | bytes 9437188
  288.6 20.7 %all-to-all-start.6 = ((bf16[8,1,128,384]{3,2,1,0:T(8,128)(2,1)}), bf16[8,1,128,384]{3,2,1,0:T(8,128)(2,1)}, u32[]{:S(2)}, u32[]{:S(2)}) async-start(bf16[8,1,128,384]{3,2,1,0:T(8,128)(2,1)} %slice.86), calls=%async_computation.6 | async-start | bytes 1572864 | tf_op jit(solution)/shard_map/all_to_all | solution.py:17
  296.9 46.3 %reduce-scatter.2.cloned.1.call-start = ((), (), s32[]{:S(2)}) async-start(), calls=%async_computation.12 | async-start | bytes 2621440 | tf_op jit(solution)/shard_map/reduce_scatter | solution.py:280
  314.9 33.6 %all-to-all-start.7 = ((bf16[8,3,128,384]{3,2,1,0:T(8,128)(2,1)}), bf16[8,3,128,384]{3,2,1,0:T(8,128)(2,1)S(1)}, u32[]{:S(2)}, u32[]{:S(2)}) async-start(bf16[8,3,128,384]{3,2,1,0:T(8,128)(2,1)} %slice.92), calls=%async_computation.7 | async-start | bytes 4718592 | tf_op jit(solution)/shard_map/all_to_all | solution.py:17
  348.5 25.4 %all-to-all-start.8 = ((bf16[64,32,128]{2,1,0:T(8,128)(2,1)}), bf16[64,32,128]{2,1,0:T(8,128)(2,1)S(1)}, u32[]{:S(2)}, u32[]{:S(2)}) async-start(bf16[64,32,128]{2,1,0:T(8,128)(2,1)} %bitcast.50), calls=%async_computation.9 | async-start | bytes 1048576 | tf_op jit(solution)/shard_map/all_to_all | solution.py:17
  356.2 18.5 %copy-start.1 = (bf16[2,16,4096]{2,1,0:T(8,128)(2,1)S(1)}, bf16[2,16,4096]{2,1,0:T(8,128)(2,1)}, u32[]{:S(2)}) copy-start(bf16[2,16,4096]{2,1,0:T(8,128)(2,1)} %param.8) | copy-start | bytes 786436
Sparse Core Ops, SparseCore 0:
  27.4 80.4 all-gather.4
  109.6 73.0 all-gather.6
  252.1 33.9 all-gather.8
  313.4 29.7 reduce-scatter.1

commit v5 on v2

--- a/solution.py
+++ b/solution.py
@@ -253,13 +253,13 @@
     )
     arrived_up, gate_act = lax.optimization_barrier((arrived_up, gate_act))
     down_ring.hop()
-    arrived_up = down_ring.hold(arrived_up)
-    down_ring.hop()
     serve_up = assemble(arrived_up)
     up_act = jnp.einsum(
         "ymd,ydf->mf", inputs, serve_up.reshape(by_part), preferred_element_type=jnp.float32
     )
     hidden = (jax.nn.silu(gate_act) * up_act * row_weight.reshape(-1, 1)).astype(jnp.bfloat16)
+    hidden = down_ring.hold(hidden)
+    down_ring.hop()
 
     down_ring.hop()
 

time: 377 us -> 372 us (0.987)
    unnamed x67 -> x65, local copies, waits for them, and re-layouts: 11.5 us -> 12.3 us
  transfers between devices with their start and end apart: 30 -> 30, of which waited for: 19 -> 18; matrix products, arithmetic and copies ran while one was open for 14% -> 17% of each run, Pallas kernels for 2% -> 2%
where the time goes in v5:
time: 372 us; the launch traced here: 370 us
  waiting for transfers between devices  156 us (42%)
  starting transfers between devices  65.1 us (17%)
  local copies, waits for them, and re-layouts  49.9 us (13%)
  blocking collectives  43.1 us (12%)
  matrix products  22 us (6%)
  between operations  14.3 us (4%)
  other arithmetic  12.5 us (3%)
  Pallas kernels  7.2 us (2%)
    ppermute x16, waiting for transfers between devices, shift(): return lax.ppermute(value, 'z', [(i, (i + step) % Z) for i in range(Z)])  53.7 us
    all_to_all x2, blocking collectives, exchange(): return lax.all_to_all(value, axes, split_axis=0, concat_axis=0, tiled=True)  43.1 us
    all_to_all x6, starting transfers between devices, exchange(): return lax.all_to_all(value, axes, split_axis=0, concat_axis=0, tiled=True)  37.5 us
    all_to_all x6, waiting for transfers between devices, exchange(): return lax.all_to_all(value, axes, split_axis=0, concat_axis=0, tiled=True)  36.8 us
    reduce_scatter x1, waiting for transfers between devices, body(): lax.psum_scatter(plane_out.reshape(-1, block_rows), 'y', scatter_dimensio...  25.8 us
    ppermute x16, starting transfers between devices, shift(): return lax.ppermute(value, 'z', [(i, (i + step) % Z) for i in range(Z)])  21.8 us
    ppermute x1, waiting for transfers between devices, body(): from_next = lax.ppermute(quarters, 'y', to_last)  21.2 us
    gather x6, local copies, waits for them, and re-layouts, take_rows(): return value.at[index].get(mode='promise_in_bounds')  18.6 us
  transfers between devices with their start and end apart: 30, of which 18 were waited for; matrix products, arithmetic and copies ran while one was open for 17% of the time, Pallas kernels for 2%

profile of v5, /device:TPU:1, one launch (start us, length us, event | category | flops | bytes accessed | tf_op | source)
XLA Modules:
  0.0 370.2 jit_solution(4732785835426378060)
XLA Ops:
  7.2 6.8 %all-to-all-start = ((bf16[8,128,384]{2,1,0:T(8,128)(2,1)}), bf16[8,128,384]{2,1,0:T(8,128)(2,1)S(1)}, u32[]{:S(2)}, u32[]{:S(2)}) async-start(bf16[8,128,384]{2,1,0:T(8,128)(2,1)} %bitcast.133), calls=%async_computation | async-start | bytes 1572864 | tf_op jit(solution)/shard_map/all_to_all | solution.py:17
  16.1 10.2 %all-to-all-done = bf16[8,128,384]{2,1,0:T(8,128)(2,1)S(1)} async-done(((bf16[8,128,384]{2,1,0:T(8,128)(2,1)}), bf16[8,128,384]{2,1,0:T(8,128)(2,1)S(1)}, u32[]{:S(2)}, u32[]{:S(2)}) %all-to-all-start) | async-done | bytes 786464 | tf_op jit(solution)/shard_map/all_to_all | solution.py:17
  26.3 0.9 copy-done.10
  27.3 16.2 %all_to_all.40 = bf16[8,128,384]{2,1,0:T(8,128)(2,1)} all-to-all(bf16[8,128,384]{2,1,0:T(8,128)(2,1)S(1)} %bitcast.134), channel_id=1, replica_groups=mesh['z'=8,'x'=4,'c'=2,'y'=4] {'x','c'}, dimensions={0} | all-to-all | bytes 1572864 | tf_op jit(solution)/shard_map/all_to_all | solution.py:17
  44.6 4.0 %collective-permute-start = (bf16[2,16,1152]{2,1,0:T(8,128)(2,1)S(1)}, bf16[2,16,1152]{2,1,0:T(8,128)(2,1)S(1)}, u32[]{:S(2)}, u32[]{:S(2)}) collective-permute-start(bf16[2,16,1152]{2,1,0:T(8,128)(2,1)S(1)} %bitcast.137), channel_id=1, source_target_pairs={{0,224},{32,0},{64,32},{96,64},{128,96},{160,128},{192,160},{224,1... | collective-permute-start | bytes 221192 | tf_op jit(solution)/shard_map/ppermute | solution.py:21
  48.7 3.9 %collective-permute-done.3.refs_8_ = bf16[2,16,1152]{2,1,0:T(8,128)(2,1)S(1)} collective-permute-done((bf16[2,16,1152]{2,1,0:T(8,128)(2,1)S(1)}, bf16[2,16,1152]{2,1,0:T(8,128)(2,1)S(1)}, u32[]{:S(2)}, u32[]{:S(2)}) %collective-permute-start.3) | collective-permute-done | bytes 73760 | tf_op jit(solution)/shard_map/ppermute | solution.py:21
  52.7 2.7 collective-permute-start.1
  55.4 3.7 %collective-permute-done.4.refs_7_ = bf16[2,16,1152]{2,1,0:T(8,128)(2,1)S(1)} collective-permute-done((bf16[2,16,1152]{2,1,0:T(8,128)(2,1)S(1)}, bf16[2,16,1152]{2,1,0:T(8,128)(2,1)S(1)}, u32[]{:S(2)}, u32[]{:S(2)}) %collective-permute-start.4) | collective-permute-done | bytes 73760 | tf_op jit(solution)/shard_map/ppermute | solution.py:21
  59.2 2.7 collective-permute-start.2
  61.9 3.7 collective-permute-done.5.refs_6_
  65.6 2.7 collective-permute-start.7
  69.2 1.6 collective-permute-done.6.refs_4_
  71.9 2.7 pick_pieces.2
  74.6 0.9 slice_bitcast_fusion.4
  76.4 1.6 convolution_convert_fusion
  78.1 27.0 %all_to_all.41 = bf16[8,96,1024]{2,1,0:T(8,128)(2,1)S(1)} all-to-all(bf16[8,96,1024]{2,1,0:T(8,128)(2,1)S(1)} %pad_maximum_fusion.1), channel_id=1, replica_groups=mesh['z'=8,'x'=4,'c'=2,'y'=4] {'x','c'}, dimensions={0} | all-to-all | bytes 3145728 | tf_op jit(solution)/shard_map/all_to_all | solution.py:17
  105.1 1.1 copy-done.3
  106.4 2.8 collective-permute-start.9
  109.2 4.7 %all-to-all-start.4 = ((bf16[8,128,384]{2,1,0:T(8,128)(2,1)}), bf16[8,128,384]{2,1,0:T(8,128)(2,1)S(1)}, u32[]{:S(2)}, u32[]{:S(2)}) async-start(bf16[8,128,384]{2,1,0:T(8,128)(2,1)} %bitcast.21), calls=%async_computation.4 | async-start | bytes 1572864 | tf_op jit(solution)/shard_map/all_to_all | solution.py:17
  115.1 21.2 %collective-permute-done.9 = bf16[640,1024]{1,0:T(8,128)(2,1)} collective-permute-done((bf16[640,1024]{1,0:T(8,128)(2,1)S(1)}, bf16[640,1024]{1,0:T(8,128)(2,1)}, u32[]{:S(2)}, u32[]{:S(2)}) %collective-permute-start.9) | collective-permute-done | bytes 1310752 | tf_op jit(solution)/shard_map/ppermute | solution.py:221
  136.3 3.2 collective-permute-done.8
  139.5 5.5 %gather_fusion.1 = bf16[32,128,384]{2,1,0:T(8,128)(2,1)} fusion(bf16[64,128,384]{2,1,0:T(8,128)(2,1)} %bitcast.132, s32[1024]{0:T(1024)S(1)} %pad_clamp_fusion.1), kind=kCustom, calls=%fused_computation.1 | custom fusion | bytes 6291584 | tf_op jit(solution)/shard_map/gather | solution.py:109
  145.0 0.9 copy-done.6
  145.9 5.7 %all-to-all-start.3 = ((bf16[8,4,128,384]{3,2,1,0:T(8,128)(2,1)}), bf16[8,4,128,384]{3,2,1,0:T(8,128)(2,1)S(1)}, u32[]{:S(2)}, u32[]{:S(2)}) async-start(bf16[8,4,128,384]{3,2,1,0:T(8,128)(2,1)} %bitcast.114), calls=%async_computation.3 | async-start | bytes 6291456 | tf_op jit(solution)/shard_map/all_to_all | solution.py:17
  151.7 1.2 slice.52
  152.9 1.1 slice.51
  154.3 2.7 collective-permute-start.11
  157.1 14.9 %collective-permute-done.10 = bf16[320,1024]{1,0:T(8,128)(2,1)S(1)} collective-permute-done((bf16[320,1024]{1,0:T(8,128)(2,1)S(1)}, bf16[320,1024]{1,0:T(8,128)(2,1)S(1)}, u32[]{:S(2)}, u32[]{:S(2)}) %collective-permute-start.10) | collective-permute-done | bytes 655392 | tf_op jit(solution)/shard_map/ppermute | solution.py:224
  172.1 4.7 %pad_maximum_fusion = bf16[4,640,1024]{2,1,0:T(8,128)(2,1)} fusion(bf16[1,640,1024]{2,1,0:T(8,128)(2,1)} %bitcast.23, bf16[1,640,1024]{2,1,0:T(8,128)(2,1)S(1)} %maximum_bitcast_fusion, bf16[1,640,1024]{2,1,0:T(8,128)(2,1)} %bitcast.20, bf16[1,640,1024]{2,1,0:T(8,128)(2,1)S(1)} %bitcast.120), kind=kLoop, calls=%fused_computation.5 | loop fusion | flops 7864320 | bytes 10485760 | tf_op jit(solution)/shard_map/stack | solution.py:229
  176.7 5.7 %gather_fusion.2 = bf16[4,640,1024]{2,1,0:T(8,128)(2,1)} fusion(bf16[4,640,1024]{2,1,0:T(8,128)(2,1)} %pad_maximum_fusion, s32[1024]{0:T(1024)S(1)} %pad_clamp_fusion), kind=kCustom, calls=%fused_computation.2 | custom fusion | bytes 10485776 | tf_op jit(solution)/shard_map/gather | solution.py:109
  182.7 5.4 %gather_fusion.3 = bf16[32,128,384]{2,1,0:T(8,128)(2,1)} fusion(bf16[64,128,384]{2,1,0:T(8,128)(2,1)} %bitcast.131, s32[1024]{0:T(1024)S(1)} %pad_clamp_fusion.1), kind=kCustom, calls=%fused_computation.3 | custom fusion | bytes 6291584 | tf_op jit(solution)/shard_map/gather | solution.py:109
  188.2 1.1 all-to-all-done.3
  189.3 1.7 copy-done.2
  190.9 5.2 %all-to-all-start.5 = ((bf16[8,4,128,384]{3,2,1,0:T(8,128)(2,1)}), bf16[8,4,128,384]{3,2,1,0:T(8,128)(2,1)}, u32[]{:S(2)}, u32[]{:S(2)}) async-start(bf16[8,4,128,384]{3,2,1,0:T(8,128)(2,1)} %bitcast.113), calls=%async_computation.5 | async-start | bytes 6291456 | tf_op jit(solution)/shard_map/all_to_all | solution.py:17
  197.4 1.0 slice.76
  200.5 2.5 collective-permute-start.13
  204.6 1.3 fusion.2
  206.2 13.5 %collective-permute-done.13.refs_1_ = bf16[8,128,384]{2,1,0:T(8,128)(2,1)S(1)} collective-permute-done((bf16[8,128,384]{2,1,0:T(8,128)(2,1)S(1)}, bf16[8,128,384]{2,1,0:T(8,128)(2,1)S(1)}, u32[]{:S(2)}, u32[]{:S(2)}) %collective-permute-start.13) | collective-permute-done | bytes 786464 | tf_op jit(solution)/shard_map/ppermute | solution.py:21
  219.8 3.2 collective-permute-done.12.refs_8_
  223.3 1.1 collective-permute-start.14
  224.4 2.4 copy.88
  226.9 1.7 copy-done.8
  228.5 6.3 %convolution_bitcast_fusion.1 = f32[640,384]{1,0:T(8,128)} fusion(bf16[4,640,1024]{2,1,0:T(8,128)(2,1)} %gather_fusion.2, bf16[4,1024,384]{2,1,0:T(8,128)(2,1)S(1)} %bitcast.121), kind=kOutput, calls=%fused_computation.22 | convolution fusion | flops 2013265920 | bytes 9371648 | tf_op jit(solution)/shard_map/ymd,ydf->mf/dot_general | solution.py:251
  234.8 2.5 copy.90
  237.3 1.7 copy-done.9
  239.0 6.2 %fusion.19 = bf16[640,384]{1,0:T(8,128)(2,1)} fusion(bf16[4,640,1024]{2,1,0:T(8,128)(2,1)} %gather_fusion.2, bf16[4,1024,384]{2,1,0:T(8,128)(2,1)S(1)} %bitcast.123, f32[640,384]{1,0:T(8,128)S(1)} %copy-done.30, f32[640]{0:T(1024)S(1)} %mul.54), kind=kOutput, calls=%fused_computation.24 | convolution fusion | flops 2014986240 | bytes 9865728 | tf_op jit(solution)/shard_map/ymd,ydf->mf/dot_general | solution.py:257
  245.2 0.8 copy-done.15
  246.1 1.6 collective-permute-start.16
  247.7 16.0 %collective-permute-done.16.refs_3_ = bf16[8,128,384]{2,1,0:T(8,128)(2,1)S(1)} collective-permute-done((bf16[8,128,384]{2,1,0:T(8,128)(2,1)}, bf16[8,128,384]{2,1,0:T(8,128)(2,1)S(1)}, u32[]{:S(2)}, u32[]{:S(2)}) %collective-permute-start.16) | collective-permute-done | bytes 786464 | tf_op jit(solution)/shard_map/ppermute | solution.py:21
  263.7 3.2 collective-permute-start.19
  267.0 1.2 gather_fusion.4
  268.3 4.8 %collective-permute-done.19.refs_5_ = bf16[4,128,384]{2,1,0:T(8,128)(2,1)S(1)} collective-permute-done((bf16[4,128,384]{2,1,0:T(8,128)(2,1)S(1)}, bf16[4,128,384]{2,1,0:T(8,128)(2,1)S(1)}, u32[]{:S(2)}, u32[]{:S(2)}) %collective-permute-start.19) | collective-permute-done | bytes 393248 | tf_op jit(solution)/shard_map/ppermute | solution.py:21
  273.0 3.4 collective-permute-done.18.refs_4_
  277.2 4.5 %pick_pieces.3 = bf16[32,128,384]{2,1,0:T(8,128)(2,1)} custom-call(s32[32]{0:T(128)} %gather_fusion.4, bf16[8,128,384]{2,1,0:T(8,128)(2,1)} %copy-done.6, bf16[8,128,384]{2,1,0:T(8,128)(2,1)} %copy-done.13, bf16[8,128,384]{2,1,0:T(8,128)(2,1)} %collective-permute-done.15.refs_2_, bf16[8,128,384]{2,1,0:T(8,128)(2,1)} %copy-done.11, ...), custom_call_target="tpu_custom_call" | custom-call | tf_op jit(solution)/shard_map/pick_pieces/pallas_call | solution.py:93
  281.7 7.5 %fusion.12 = bf16[4,8,256,128]{2,3,0,1:T(8,128)(2,1)S(1)} fusion(s32[8,8,256]{2,1,0:T(8,128)S(1)} %add_select_fusion, pred[8,8,256]{2,1,0:T(8,128)(4,1)S(1)} %fusion.29, bf16[8,8,80,384,1]{3,2,1,0,4:T(8,128)(2,1)} %bitcast.140, bf16[8,4,128,384]{3,2,1,0:T(8,128)(2,1)} %bitcast.115), kind=kOutput, calls=%fused_computation.16 | convolution fusion | flops 3361734656 | bytes 9256960 | tf_op jit(solution)/shard_map/lspt,slpyr->yltr/dot_general | solution.py:274
  289.2 2.4 copy.96
  291.6 7.2 %all-to-all-start.6 = ((bf16[8,4,128,384]{3,2,1,0:T(8,128)(2,1)}), bf16[8,4,128,384]{3,2,1,0:T(8,128)(2,1)S(1)}, u32[]{:S(2)}, u32[]{:S(2)}) async-start(bf16[8,4,128,384]{3,2,1,0:T(8,128)(2,1)} %bitcast.116), calls=%async_computation.6 | async-start | bytes 6291456 | tf_op jit(solution)/shard_map/all_to_all | solution.py:17
  298.8 25.8 %reduce-scatter.2.cloned.1.call-done = bf16[2048,128]{1,0:T(8,128)(2,1)} async-done(((bf16[8192,128]{1,0:T(8,128)(2,1)}), bf16[2048,128]{1,0:T(8,128)(2,1)}) %reduce-scatter.2.cloned.1.call-update) | async-done | bytes 524304 | tf_op jit(solution)/shard_map/reduce_scatter | solution.py:277
  324.7 1.9 copy.97
  326.5 9.9 %all-to-all-done.6 = bf16[8,4,128,384]{3,2,1,0:T(8,128)(2,1)S(1)} async-done(((bf16[8,4,128,384]{3,2,1,0:T(8,128)(2,1)}), bf16[8,4,128,384]{3,2,1,0:T(8,128)(2,1)S(1)}, u32[]{:S(2)}, u32[]{:S(2)}) %all-to-all-start.6) | async-done | bytes 3145760 | tf_op jit(solution)/shard_map/all_to_all | solution.py:17
  336.4 7.8 %all-to-all-start.7 = ((bf16[64,32,128]{2,1,0:T(8,128)(2,1)}), bf16[64,32,128]{2,1,0:T(8,128)(2,1)}, u32[]{:S(2)}, u32[]{:S(2)}) async-start(bf16[64,32,128]{2,1,0:T(8,128)(2,1)} %bitcast.130), calls=%async_computation.8 | async-start | bytes 1048576 | tf_op jit(solution)/shard_map/all_to_all | solution.py:17
  344.2 2.0 copy.93
  346.2 15.6 %all-to-all-done.7 = bf16[64,32,128]{2,1,0:T(8,128)(2,1)} async-done(((bf16[64,32,128]{2,1,0:T(8,128)(2,1)}), bf16[64,32,128]{2,1,0:T(8,128)(2,1)}, u32[]{:S(2)}, u32[]{:S(2)}) %all-to-all-start.7) | async-done | bytes 524320 | tf_op jit(solution)/shard_map/all_to_all | solution.py:17
  361.9 1.1 reduce_sum.112
  (151 shorter events, 15.8 us)
Async XLA Ops:
  7.2 8.9 %copy-start = (bf16[2,16,4096]{2,1,0:T(8,128)(2,1)S(1)}, bf16[2,16,4096]{2,1,0:T(8,128)(2,1)}, u32[]{:S(2)}) copy-start(bf16[2,16,4096]{2,1,0:T(8,128)(2,1)} %param.8) | copy-start | bytes 786436
  7.2 20.1 %copy-start.16 = (bf16[1,1024,384]{2,1,0:T(8,128)(2,1)S(1)}, bf16[1,1024,384]{2,1,0:T(8,128)(2,1)}, u32[]{:S(2)}) copy-start(bf16[1,1024,384]{2,1,0:T(8,128)(2,1)} %param.14) | copy-start | bytes 2359300
  7.2 36.3 %copy-start.28 = (s32[64]{0:T(128)S(1)}, s32[64]{0:T(128)}, u32[]{:S(2)}) copy-start(s32[64]{0:T(128)} %param.12) | copy-start | bytes 772
  7.2 19.1 %all-to-all-start = ((bf16[8,128,384]{2,1,0:T(8,128)(2,1)}), bf16[8,128,384]{2,1,0:T(8,128)(2,1)S(1)}, u32[]{:S(2)}, u32[]{:S(2)}) async-start(bf16[8,128,384]{2,1,0:T(8,128)(2,1)} %bitcast.133), calls=%async_computation | async-start | bytes 1572864 | tf_op jit(solution)/shard_map/all_to_all | solution.py:17
  14.0 125.5 %all-gather.5.cloned.1.call-start = ((), (), s32[]{:S(2)}) async-start(), calls=%async_computation.9 | async-start | bytes 7077888 | tf_op jit(solution)/shard_map/all_gather | solution.py:150
  26.3 0.9 copy-start.10
  27.2 155.5 %all-gather.7.cloned.1.call-start = ((), (), s32[]{:S(2)}) async-start(), calls=%async_computation.10 | async-start | bytes 7077888 | tf_op jit(solution)/shard_map/all_gather | solution.py:150
  43.8 26.9 %copy-start.19 = (bf16[32,1152]{1,0:T(8,128)(2,1)}, bf16[32,1152]{1,0:T(8,128)(2,1)S(1)}, u32[]{:S(2)}) copy-start(bf16[32,1152]{1,0:T(8,128)(2,1)S(1)} %pad.4) | copy-start | bytes 221188
  43.8 8.8 %collective-permute-start.3 = (bf16[2,16,1152]{2,1,0:T(8,128)(2,1)S(1)}, bf16[2,16,1152]{2,1,0:T(8,128)(2,1)S(1)}, u32[]{:S(2)}, u32[]{:S(2)}) collective-permute-start(bf16[2,16,1152]{2,1,0:T(8,128)(2,1)S(1)} %bitcast.136), channel_id=1, source_target_pairs={{0,32},{32,64},{64,96},{96,128},{128,160},{160,192},{192,224},{224... | collective-permute-start | bytes 221192 | tf_op jit(solution)/shard_map/ppermute | solution.py:21
  44.6 8.0 %collective-permute-start = (bf16[2,16,1152]{2,1,0:T(8,128)(2,1)S(1)}, bf16[2,16,1152]{2,1,0:T(8,128)(2,1)S(1)}, u32[]{:S(2)}, u32[]{:S(2)}) collective-permute-start(bf16[2,16,1152]{2,1,0:T(8,128)(2,1)S(1)} %bitcast.137), channel_id=1, source_target_pairs={{0,224},{32,0},{64,32},{96,64},{128,96},{160,128},{192,160},{224,1... | collective-permute-start | bytes 221192 | tf_op jit(solution)/shard_map/ppermute | solution.py:21
  52.7 18.1 %copy-start.22 = (bf16[2,16,1152]{2,1,0:T(8,128)(2,1)}, bf16[2,16,1152]{2,1,0:T(8,128)(2,1)S(1)}, u32[]{:S(2)}) copy-start(bf16[2,16,1152]{2,1,0:T(8,128)(2,1)S(1)} %collective-permute-done.3.refs_8_) | copy-start | bytes 221188
  52.7 6.5 %collective-permute-start.4 = (bf16[2,16,1152]{2,1,0:T(8,128)(2,1)S(1)}, bf16[2,16,1152]{2,1,0:T(8,128)(2,1)S(1)}, u32[]{:S(2)}, u32[]{:S(2)}) collective-permute-start(bf16[2,16,1152]{2,1,0:T(8,128)(2,1)S(1)} %collective-permute-done.3.refs_8_), channel_id=1, source_target_pairs={{0,32},{32,64},{64,96},{96,128},{128,160},{160,192},{192,224},{224... | collective-permute-start | bytes 221192 | tf_op jit(solution)/shard_map/ppermute | solution.py:21
  52.7 18.1 %copy-start.23 = (bf16[2,16,1152]{2,1,0:T(8,128)(2,1)}, bf16[2,16,1152]{2,1,0:T(8,128)(2,1)S(1)}, u32[]{:S(2)}) copy-start(bf16[2,16,1152]{2,1,0:T(8,128)(2,1)S(1)} %collective-permute-done.refs_1_) | copy-start | bytes 221188
  52.7 6.5 %collective-permute-start.1 = (bf16[2,16,1152]{2,1,0:T(8,128)(2,1)S(1)}, bf16[2,16,1152]{2,1,0:T(8,128)(2,1)S(1)}, u32[]{:S(2)}, u32[]{:S(2)}) collective-permute-start(bf16[2,16,1152]{2,1,0:T(8,128)(2,1)S(1)} %collective-permute-done.refs_1_), channel_id=1, source_target_pairs={{0,224},{32,0},{64,32},{96,64},{128,96},{160,128},{192,160},{224,1... | collective-permute-start | bytes 221192 | tf_op jit(solution)/shard_map/ppermute | solution.py:21
  59.2 11.6 %copy-start.24 = (bf16[2,16,1152]{2,1,0:T(8,128)(2,1)}, bf16[2,16,1152]{2,1,0:T(8,128)(2,1)S(1)}, u32[]{:S(2)}) copy-start(bf16[2,16,1152]{2,1,0:T(8,128)(2,1)S(1)} %collective-permute-done.4.refs_7_) | copy-start | bytes 221188
  59.2 6.4 %collective-permute-start.5 = (bf16[2,16,1152]{2,1,0:T(8,128)(2,1)S(1)}, bf16[2,16,1152]{2,1,0:T(8,128)(2,1)S(1)}, u32[]{:S(2)}, u32[]{:S(2)}) collective-permute-start(bf16[2,16,1152]{2,1,0:T(8,128)(2,1)S(1)} %collective-permute-done.4.refs_7_), channel_id=1, source_target_pairs={{0,32},{32,64},{64,96},{96,128},{128,160},{160,192},{192,224},{224... | collective-permute-start | bytes 221192 | tf_op jit(solution)/shard_map/ppermute | solution.py:21
  59.2 11.6 %copy-start.25 = (bf16[2,16,1152]{2,1,0:T(8,128)(2,1)}, bf16[2,16,1152]{2,1,0:T(8,128)(2,1)S(1)}, u32[]{:S(2)}) copy-start(bf16[2,16,1152]{2,1,0:T(8,128)(2,1)S(1)} %collective-permute-done.1.refs_2_) | copy-start | bytes 221188
  59.2 6.4 %collective-permute-start.2 = (bf16[2,16,1152]{2,1,0:T(8,128)(2,1)S(1)}, bf16[2,16,1152]{2,1,0:T(8,128)(2,1)S(1)}, u32[]{:S(2)}, u32[]{:S(2)}) collective-permute-start(bf16[2,16,1152]{2,1,0:T(8,128)(2,1)S(1)} %collective-permute-done.1.refs_2_), channel_id=1, source_target_pairs={{0,224},{32,0},{64,32},{96,64},{128,96},{160,128},{192,160},{224,1... | collective-permute-start | bytes 221192 | tf_op jit(solution)/shard_map/ppermute | solution.py:21
  65.5 5.2 %copy-start.20 = (bf16[2,16,1152]{2,1,0:T(8,128)(2,1)}, bf16[2,16,1152]{2,1,0:T(8,128)(2,1)S(1)}, u32[]{:S(2)}) copy-start(bf16[2,16,1152]{2,1,0:T(8,128)(2,1)S(1)} %collective-permute-done.5.refs_6_) | copy-start | bytes 221188
  65.5 5.2 %collective-permute-start.6 = (bf16[1,16,1152]{2,1,0:T(8,128)(2,1)S(1)}, bf16[1,16,1152]{2,1,0:T(8,128)(2,1)S(1)}, u32[]{:S(2)}, u32[]{:S(2)}) collective-permute-start(bf16[1,16,1152]{2,1,0:T(8,128)(2,1)S(1)} %slice.70), channel_id=1, source_target_pairs={{0,32},{32,64},{64,96},{96,128},{128,160},{160,192},{192,224},{224... | collective-permute-start | bytes 110600 | tf_op jit(solution)/shard_map/ppermute | solution.py:21
  65.6 5.2 %copy-start.21 = (bf16[2,16,1152]{2,1,0:T(8,128)(2,1)}, bf16[2,16,1152]{2,1,0:T(8,128)(2,1)S(1)}, u32[]{:S(2)}) copy-start(bf16[2,16,1152]{2,1,0:T(8,128)(2,1)S(1)} %collective-permute-done.2.refs_3_) | copy-start | bytes 221188
  65.6 5.1 %collective-permute-start.7 = (bf16[1,16,1152]{2,1,0:T(8,128)(2,1)S(1)}, bf16[1,16,1152]{2,1,0:T(8,128)(2,1)S(1)}, u32[]{:S(2)}, u32[]{:S(2)}) collective-permute-start(bf16[1,16,1152]{2,1,0:T(8,128)(2,1)S(1)} %slice.71), channel_id=1, source_target_pairs={{0,224},{32,0},{64,32},{96,64},{128,96},{160,128},{192,160},{224,1... | collective-permute-start | bytes 110600 | tf_op jit(solution)/shard_map/ppermute | solution.py:21
  70.7 0.6 copy-start.26
  71.3 0.6 copy-start.27
  78.1 36.0 %copy-start.29 = (s32[64]{0:T(128)S(1)}, s32[64]{0:T(128)}, u32[]{:S(2)}) copy-start(s32[64]{0:T(128)} %param.11) | copy-start | bytes 772
  105.1 1.1 copy-start.3
  106.4 38.6 %copy-start.4 = (bf16[8,80,1024]{2,1,0:T(8,128)(2,1)}, bf16[8,80,1024]{2,1,0:T(8,128)(2,1)S(1)}, u32[]{:S(2)}) copy-start(bf16[8,80,1024]{2,1,0:T(8,128)(2,1)S(1)} %slice.75) | copy-start | bytes 3932164
  106.4 29.9 %collective-permute-start.9 = (bf16[640,1024]{1,0:T(8,128)(2,1)S(1)}, bf16[640,1024]{1,0:T(8,128)(2,1)}, u32[]{:S(2)}, u32[]{:S(2)}) collective-permute-start(bf16[640,1024]{1,0:T(8,128)(2,1)S(1)} %bitcast.118), channel_id=1, source_target_pairs={{0,3},{1,0},{2,1},{3,2},{4,7},{5,4},{6,5},{7,6},{8,11},{9,8},{10,9... | collective-permute-start | bytes 3932168 | tf_op jit(solution)/shard_map/ppermute | solution.py:221
  109.2 30.3 %collective-permute-start.8 = (bf16[640,1024]{1,0:T(8,128)(2,1)S(1)}, bf16[640,1024]{1,0:T(8,128)(2,1)}, u32[]{:S(2)}, u32[]{:S(2)}) collective-permute-start(bf16[640,1024]{1,0:T(8,128)(2,1)S(1)} %bitcast.119), channel_id=1, source_target_pairs={{0,1},{1,2},{2,3},{3,0},{4,5},{5,6},{6,7},{7,4},{8,9},{9,10},{10,1... | collective-permute-start | bytes 3932168 | tf_op jit(solution)/shard_map/ppermute | solution.py:220
  109.2 35.8 %all-to-all-start.4 = ((bf16[8,128,384]{2,1,0:T(8,128)(2,1)}), bf16[8,128,384]{2,1,0:T(8,128)(2,1)S(1)}, u32[]{:S(2)}, u32[]{:S(2)}) async-start(bf16[8,128,384]{2,1,0:T(8,128)(2,1)} %bitcast.21), calls=%async_computation.4 | async-start | bytes 1572864 | tf_op jit(solution)/shard_map/all_to_all | solution.py:17
  145.0 0.9 copy-start.6
  145.9 43.3 %all-to-all-start.3 = ((bf16[8,4,128,384]{3,2,1,0:T(8,128)(2,1)}), bf16[8,4,128,384]{3,2,1,0:T(8,128)(2,1)S(1)}, u32[]{:S(2)}, u32[]{:S(2)}) async-start(bf16[8,4,128,384]{3,2,1,0:T(8,128)(2,1)} %bitcast.114), calls=%async_computation.3 | async-start | bytes 6291456 | tf_op jit(solution)/shard_map/all_to_all | solution.py:17
  151.7 20.4 %copy-start.5 = (bf16[8,80,1024]{2,1,0:T(8,128)(2,1)S(1)}, bf16[8,80,1024]{2,1,0:T(8,128)(2,1)}, u32[]{:S(2)}) copy-start(bf16[8,80,1024]{2,1,0:T(8,128)(2,1)} %copy-done.4) | copy-start | bytes 3932164
  154.1 17.9 %collective-permute-start.10 = (bf16[320,1024]{1,0:T(8,128)(2,1)S(1)}, bf16[320,1024]{1,0:T(8,128)(2,1)S(1)}, u32[]{:S(2)}, u32[]{:S(2)}) collective-permute-start(bf16[320,1024]{1,0:T(8,128)(2,1)S(1)} %slice.51), channel_id=1, source_target_pairs={{0,1},{1,2},{2,3},{3,0},{4,5},{5,6},{6,7},{7,4},{8,9},{9,10},{10,1... | collective-permute-start | bytes 1966088 | tf_op jit(solution)/shard_map/ppermute | solution.py:224
  154.3 17.6 %collective-permute-start.11 = (bf16[320,1024]{1,0:T(8,128)(2,1)S(1)}, bf16[320,1024]{1,0:T(8,128)(2,1)S(1)}, u32[]{:S(2)}, u32[]{:S(2)}) collective-permute-start(bf16[320,1024]{1,0:T(8,128)(2,1)S(1)} %slice.52), channel_id=1, source_target_pairs={{0,3},{1,0},{2,1},{3,2},{4,7},{5,4},{6,5},{7,6},{8,11},{9,8},{10,9... | collective-permute-start | bytes 1966088 | tf_op jit(solution)/shard_map/ppermute | solution.py:225
  189.3 1.7 copy-start.2
  190.9 43.9 %all-to-all-start.5 = ((bf16[8,4,128,384]{3,2,1,0:T(8,128)(2,1)}), bf16[8,4,128,384]{3,2,1,0:T(8,128)(2,1)}, u32[]{:S(2)}, u32[]{:S(2)}) async-start(bf16[8,4,128,384]{3,2,1,0:T(8,128)(2,1)} %bitcast.113), calls=%async_computation.5 | async-start | bytes 6291456 | tf_op jit(solution)/shard_map/all_to_all | solution.py:17
  196.1 4.3 %copy-start.7 = (bf16[8,128,384]{2,1,0:T(8,128)(2,1)S(1)}, bf16[8,128,384]{2,1,0:T(8,128)(2,1)}, u32[]{:S(2)}) copy-start(bf16[8,128,384]{2,1,0:T(8,128)(2,1)} %copy-done.6) | copy-start | bytes 2359300
  196.1 85.6 %all-gather.9.cloned.1.call-start = ((), (), s32[]{:S(2)}) async-start(), calls=%async_computation.12 | async-start | bytes 4423680 | tf_op jit(solution)/shard_map/all_gather | solution.py:266
  200.5 19.3 %collective-permute-start.13 = (bf16[8,128,384]{2,1,0:T(8,128)(2,1)S(1)}, bf16[8,128,384]{2,1,0:T(8,128)(2,1)S(1)}, u32[]{:S(2)}, u32[]{:S(2)}) collective-permute-start(bf16[8,128,384]{2,1,0:T(8,128)(2,1)S(1)} %copy-done.7), channel_id=1, source_target_pairs={{0,224},{32,0},{64,32},{96,64},{128,96},{160,128},{192,160},{224,1... | collective-permute-start | bytes 2359304 | tf_op jit(solution)/shard_map/ppermute | solution.py:21
  203.0 19.9 %collective-permute-start.12 = (bf16[8,128,384]{2,1,0:T(8,128)(2,1)S(1)}, bf16[8,128,384]{2,1,0:T(8,128)(2,1)S(1)}, u32[]{:S(2)}, u32[]{:S(2)}) collective-permute-start(bf16[8,128,384]{2,1,0:T(8,128)(2,1)S(1)} %copy-done.7), channel_id=1, source_target_pairs={{0,32},{32,64},{64,96},{96,128},{128,160},{160,192},{192,224},{224... | collective-permute-start | bytes 2359304 | tf_op jit(solution)/shard_map/ppermute | solution.py:21
  219.8 7.1 %copy-start.13 = (bf16[8,128,384]{2,1,0:T(8,128)(2,1)}, bf16[8,128,384]{2,1,0:T(8,128)(2,1)S(1)}, u32[]{:S(2)}) copy-start(bf16[8,128,384]{2,1,0:T(8,128)(2,1)S(1)} %collective-permute-done.13.refs_1_) | copy-start | bytes 2359300
  222.9 3.9 %copy-start.14 = (bf16[8,128,384]{2,1,0:T(8,128)(2,1)}, bf16[8,128,384]{2,1,0:T(8,128)(2,1)S(1)}, u32[]{:S(2)}) copy-start(bf16[8,128,384]{2,1,0:T(8,128)(2,1)S(1)} %collective-permute-done.12.refs_8_) | copy-start | bytes 2359300
  223.0 22.2 %collective-permute-start.15 = (bf16[8,128,384]{2,1,0:T(8,128)(2,1)S(1)}, bf16[8,128,384]{2,1,0:T(8,128)(2,1)}, u32[]{:S(2)}, u32[]{:S(2)}) collective-permute-start(bf16[8,128,384]{2,1,0:T(8,128)(2,1)S(1)} %collective-permute-done.13.refs_1_), channel_id=1, source_target_pairs={{0,224},{32,0},{64,32},{96,64},{128,96},{160,128},{192,160},{224,1... | collective-permute-start | bytes 2359304 | tf_op jit(solution)/shard_map/ppermute | solution.py:21
  223.3 21.8 %collective-permute-start.14 = (bf16[8,128,384]{2,1,0:T(8,128)(2,1)S(1)}, bf16[8,128,384]{2,1,0:T(8,128)(2,1)S(1)}, u32[]{:S(2)}, u32[]{:S(2)}) collective-permute-start(bf16[8,128,384]{2,1,0:T(8,128)(2,1)S(1)} %collective-permute-done.12.refs_8_), channel_id=1, source_target_pairs={{0,32},{32,64},{64,96},{96,128},{128,160},{160,192},{192,224},{224... | collective-permute-start | bytes 2359304 | tf_op jit(solution)/shard_map/ppermute | solution.py:21
  226.8 1.7 copy-start.8
  234.8 4.2 %copy-start.30 = (f32[640,384]{1,0:T(8,128)S(1)}, f32[640,384]{1,0:T(8,128)}, u32[]{:S(2)}) copy-start(f32[640,384]{1,0:T(8,128)} %convolution_bitcast_fusion.1) | copy-start | bytes 2949124
  237.3 1.7 copy-start.9
  245.2 0.9 copy-start.15
  246.1 78.6 %reduce-scatter.2.cloned.1.call-start = ((), (), s32[]{:S(2)}) async-start(), calls=%async_computation.11 | async-start | bytes 2621440 | tf_op jit(solution)/shard_map/reduce_scatter | solution.py:277
  246.1 17.6 %collective-permute-start.16 = (bf16[8,128,384]{2,1,0:T(8,128)(2,1)}, bf16[8,128,384]{2,1,0:T(8,128)(2,1)S(1)}, u32[]{:S(2)}, u32[]{:S(2)}) collective-permute-start(bf16[8,128,384]{2,1,0:T(8,128)(2,1)} %collective-permute-done.15.refs_2_), channel_id=1, source_target_pairs={{0,224},{32,0},{64,32},{96,64},{128,96},{160,128},{192,160},{224,1... | collective-permute-start | bytes 2359304 | tf_op jit(solution)/shard_map/ppermute | solution.py:21
  247.7 19.2 %collective-permute-start.17 = (bf16[8,128,384]{2,1,0:T(8,128)(2,1)}, bf16[8,128,384]{2,1,0:T(8,128)(2,1)S(1)}, u32[]{:S(2)}, u32[]{:S(2)}) collective-permute-start(bf16[8,128,384]{2,1,0:T(8,128)(2,1)} %copy-done.15), channel_id=1, source_target_pairs={{0,32},{32,64},{64,96},{96,128},{128,160},{160,192},{192,224},{224... | collective-permute-start | bytes 2359304 | tf_op jit(solution)/shard_map/ppermute | solution.py:21
  263.6 12.8 %copy-start.11 = (bf16[8,128,384]{2,1,0:T(8,128)(2,1)}, bf16[8,128,384]{2,1,0:T(8,128)(2,1)S(1)}, u32[]{:S(2)}) copy-start(bf16[8,128,384]{2,1,0:T(8,128)(2,1)S(1)} %collective-permute-done.16.refs_3_) | copy-start | bytes 2359300
  263.7 9.3 %collective-permute-start.19 = (bf16[4,128,384]{2,1,0:T(8,128)(2,1)S(1)}, bf16[4,128,384]{2,1,0:T(8,128)(2,1)S(1)}, u32[]{:S(2)}, u32[]{:S(2)}) collective-permute-start(bf16[4,128,384]{2,1,0:T(8,128)(2,1)S(1)} %slice.82), channel_id=1, source_target_pairs={{0,224},{32,0},{64,32},{96,64},{128,96},{160,128},{192,160},{224,1... | collective-permute-start | bytes 1179656 | tf_op jit(solution)/shard_map/ppermute | solution.py:21
  266.9 9.5 %copy-start.12 = (bf16[8,128,384]{2,1,0:T(8,128)(2,1)}, bf16[8,128,384]{2,1,0:T(8,128)(2,1)S(1)}, u32[]{:S(2)}) copy-start(bf16[8,128,384]{2,1,0:T(8,128)(2,1)S(1)} %collective-permute-done.17.refs_6_) | copy-start | bytes 2359300
  266.9 9.4 %collective-permute-start.18 = (bf16[4,128,384]{2,1,0:T(8,128)(2,1)S(1)}, bf16[4,128,384]{2,1,0:T(8,128)(2,1)S(1)}, u32[]{:S(2)}, u32[]{:S(2)}) collective-permute-start(bf16[4,128,384]{2,1,0:T(8,128)(2,1)S(1)} %slice.81), channel_id=1, source_target_pairs={{0,32},{32,64},{64,96},{96,128},{128,160},{160,192},{192,224},{224... | collective-permute-start | bytes 1179656 | tf_op jit(solution)/shard_map/ppermute | solution.py:21
  273.0 3.4 copy-start.17
  276.4 0.8 copy-start.18
  291.6 44.8 %all-to-all-start.6 = ((bf16[8,4,128,384]{3,2,1,0:T(8,128)(2,1)}), bf16[8,4,128,384]{3,2,1,0:T(8,128)(2,1)S(1)}, u32[]{:S(2)}, u32[]{:S(2)}) async-start(bf16[8,4,128,384]{3,2,1,0:T(8,128)(2,1)} %bitcast.116), calls=%async_computation.6 | async-start | bytes 6291456 | tf_op jit(solution)/shard_map/all_to_all | solution.py:17
  336.4 25.4 %all-to-all-start.7 = ((bf16[64,32,128]{2,1,0:T(8,128)(2,1)}), bf16[64,32,128]{2,1,0:T(8,128)(2,1)}, u32[]{:S(2)}, u32[]{:S(2)}) async-start(bf16[64,32,128]{2,1,0:T(8,128)(2,1)} %bitcast.130), calls=%async_computation.8 | async-start | bytes 1048576 | tf_op jit(solution)/shard_map/all_to_all | solution.py:17
  344.2 19.5 %copy-start.1 = (bf16[2,16,4096]{2,1,0:T(8,128)(2,1)S(1)}, bf16[2,16,4096]{2,1,0:T(8,128)(2,1)}, u32[]{:S(2)}) copy-start(bf16[2,16,4096]{2,1,0:T(8,128)(2,1)} %param.8) | copy-start | bytes 786436
Sparse Core Ops, SparseCore 0:
  27.4 80.4 all-gather.4
  109.6 73.0 all-gather.6
  245.3 33.7 all-gather.8
  291.8 32.8 reduce-scatter.1
